TPU v7x, 32 devices: a whole 2x2x4 slice. The times are simulated.
32 devices in a mesh: groups: 2 (over y), slices: 8 (over z, x), ering: 2 (over core).
Axes of the slice: x: 2, y: 2, z: 4, core: 2. Of those that a mesh axis runs over, the one named last changes fastest.
Arguments:
- positions: float32 [3, 128, 256], P(None, ('groups', 'slices'), 'ering'), parts along dimension 1, may hold values from -9 to 9
- hidden: bfloat16 [128, 256, 256], P(('groups', 'slices'), 'ering'), parts along dimension 0, may hold values from -6 to 6
- cotangent: bfloat16 [128, 256, 256], P(('groups', 'slices'), 'ering'), parts along dimension 0, may hold values from -6 to 6
- embed_weight: float32 [32, 4], replicated, may hold values from -3 to 3
- embed_bias: float32 [32], replicated, may hold values from -3 to 3
- pair_weight: bfloat16 [32, 32], replicated, may hold values from -1 to 1
- pair_bias: float32 [32], replicated, may hold values from -3 to 3
- one_weight: bfloat16 [256, 256], replicated, may hold values from -0.375 to 0.375
- pool_weight: bfloat16 [32, 256], replicated, may hold values from -1 to 1
- mean_weight: bfloat16 [256, 256], replicated, may hold values from -0.375 to 0.375
- one_bias: float32 [256], replicated, may hold values from -3 to 3
- drift_weight: bfloat16 [3, 256], replicated, may hold values from -0.375 to 0.375
Outputs:
- updated: bfloat16 [128, 256, 256], P(('groups', 'slices'), 'ering'), parts along dimension 0
- hidden_grad: bfloat16 [128, 256, 256], P(('groups', 'slices'), 'ering'), parts along dimension 0
- link_terms: float32 [128, 256], P(('groups', 'slices'), 'ering'), parts along dimension 0
- pair_grad: float32 [64, 32], P('groups'), parts along dimension 0
- bias_grad: float32 [64], P('groups'), parts along dimension 0
- one_grad: float32 [512, 256], P('groups'), parts along dimension 0
- pool_grad: float32 [64, 256], P('groups'), parts along dimension 0
- mean_grad: float32 [512, 256], P('groups'), parts along dimension 0
There are 2 independent parts, one for each index of `groups`. A program takes and returns all parts, laid end to end along the dimension named above; an argument that names none is the same for every part. Nothing has to cross between parts.
All inputs are finite; a program needn't handle non-finite values.
Results may differ from a plain program's by a relative error of at most 0.0054.
Values may be sent and summed in bfloat16 or wider, within the bound.
No kernel may reach another device: no remote copies, remote signals or barrier semaphores. Data moves between devices by JAX's collectives and lax.ppermute only.
A program may use at most 64 MiB of HBM per device.

v0:
```python
import math

import jax
import jax.numpy as jnp
from jax import lax
from jax.sharding import PartitionSpec as P

HIGH = lax.Precision.HIGHEST
step_tau = 0.5


def from_behind(array, axis, by):
    size = lax.axis_size(axis)
    pairs = [(i, i + by) for i in range(size) if 0 <= i + by < size]
    return lax.ppermute(array, axis, pairs)


def local(
    positions,
    hidden,
    cotangent,
    embed_weight,
    embed_bias,
    pair_weight,
    pair_bias,
    one_weight,
    pool_weight,
    mean_weight,
    one_bias,
    drift_weight,
):
    own_count = hidden.shape[1]
    total_count = own_count * lax.axis_size("ering")
    slab_count = hidden.shape[0]
    scale = 1.0 / math.sqrt(slab_count * lax.axis_size("slices") * total_count)
    every_pos = lax.all_gather(positions, "ering", axis=2, tiled=True)
    full_rows = lax.all_gather(hidden, "ering", axis=1, tiled=True)
    mean_rows = (jnp.sum(full_rows.astype(jnp.float32), axis=1) / total_count).astype(jnp.bfloat16)

    def one_slice(carry, inputs):
        own_pos, all_pos, hid_s, cot_s, mean_s = inputs
        offsets = own_pos[:, :, None] - all_pos[:, None, :]
        radial = jnp.sqrt(jnp.sum(offsets * offsets, axis=0) + 1.0)
        features = jnp.concatenate([offsets, radial[None]], axis=0)
        pair_in = jnp.tanh(
            jnp.einsum("ck,kij->cij", embed_weight, features, precision=HIGH)
            + embed_bias[:, None, None]
        ).astype(jnp.bfloat16)
        pair_pre = (
            jnp.einsum("ck,kij->cij", pair_weight, pair_in, preferred_element_type=jnp.float32)
            + pair_bias[:, None, None]
        )
        pair_act = jnp.tanh(pair_pre)
        pooled = jnp.mean(pair_act + pair_in.astype(jnp.float32), axis=2).T.astype(jnp.bfloat16)
        one_pre = jnp.dot(hid_s, one_weight, preferred_element_type=jnp.float32)
        one_pre = one_pre + jnp.dot(pooled, pool_weight, preferred_element_type=jnp.float32)
        one_pre = (
            one_pre
            + jnp.dot(mean_s[None, :], mean_weight, preferred_element_type=jnp.float32)
            + one_bias
        )
        one_act = jnp.tanh(one_pre)
        updated = (one_act + hid_s.astype(jnp.float32)).astype(jnp.bfloat16)
        pre_grad = (cot_s.astype(jnp.float32) * (1.0 - one_act * one_act)).astype(jnp.bfloat16)
        column_part = jnp.sum(pre_grad.astype(jnp.float32), axis=0)
        pooled_grad = jnp.dot(pre_grad, pool_weight.T, preferred_element_type=jnp.float32)
        partial_grad = cot_s.astype(jnp.float32) + jnp.dot(
            pre_grad, one_weight.T, preferred_element_type=jnp.float32
        )
        act_grad = pooled_grad.T[:, :, None] / total_count * (1.0 - pair_act * pair_act)
        act_low = act_grad.astype(jnp.bfloat16)
        weight_term = jnp.einsum(
            "cij,kij->ck", act_low, pair_in, preferred_element_type=jnp.float32
        )
        bias_term = jnp.sum(act_grad, axis=(1, 2))
        carry = (
            carry[0] + weight_term,
            carry[1] + bias_term,
            carry[2] + jnp.einsum("id,ie->de", hid_s, pre_grad, preferred_element_type=jnp.float32),
            carry[3]
            + jnp.einsum("ic,ie->ce", pooled, pre_grad, preferred_element_type=jnp.float32),
        )
        return (carry, (updated, partial_grad, column_part))

    d_one = hidden.shape[2]
    p_width = pair_weight.shape[0]
    start = (
        jnp.zeros((p_width, p_width), jnp.float32),
        jnp.zeros((p_width,), jnp.float32),
        jnp.zeros((d_one, d_one), jnp.float32),
        jnp.zeros((p_width, d_one), jnp.float32),
    )
    inputs = (
        jnp.moveaxis(positions, 1, 0),
        jnp.moveaxis(every_pos, 1, 0),
        hidden,
        cotangent,
        mean_rows,
    )
    totals, (updated, partial_grad, column_parts) = lax.scan(one_slice, start, inputs)
    column_total = lax.psum(column_parts, "ering")
    mean_back = jnp.dot(column_total, mean_weight.astype(jnp.float32).T, precision=HIGH)
    hidden_grad = (partial_grad + mean_back[:, None, :] / total_count).astype(jnp.bfloat16)
    mean_term = jnp.dot(mean_rows.astype(jnp.float32).T, column_parts, precision=HIGH)
    grads = (totals[0], totals[1], totals[2], totals[3], mean_term)
    grads = lax.psum((grads[0], grads[1], grads[2], grads[3], grads[4]), ("slices", "ering"))
    drift = jnp.einsum(
        "cd,sid->csi", drift_weight.astype(jnp.float32), updated.astype(jnp.float32), precision=HIGH
    )
    first_next = from_behind(positions[:, :1, :], "slices", -1)
    following = jnp.concatenate([positions[:, 1:], first_next], axis=1)
    jump = following - positions - step_tau * drift
    link_terms = jnp.sum(jump * jump, axis=0) / (12.0 * step_tau)
    is_last = lax.axis_index("slices") == lax.axis_size("slices") - 1
    last_row = jnp.logical_and(is_last, jnp.arange(slab_count) == slab_count - 1)
    link_terms = jnp.where(last_row[:, None], jnp.float32(0.0), link_terms)
    return (
        updated,
        hidden_grad,
        link_terms,
        scale * grads[0],
        scale * grads[1],
        scale * grads[2],
        scale * grads[3],
        scale * grads[4],
    )


def solution(mesh):
    in_specs = (
        P(None, ("groups", "slices"), "ering"),
        P(("groups", "slices"), "ering", None),
        P(("groups", "slices"), "ering", None),
        P(),
        P(),
        P(),
        P(),
        P(),
        P(),
        P(),
        P(),
        P(),
    )
    out_specs = (
        P(("groups", "slices"), "ering", None),
        P(("groups", "slices"), "ering", None),
        P(("groups", "slices"), "ering"),
        P("groups", None),
        P("groups"),
        P("groups", None),
        P("groups", None),
        P("groups", None),
    )
    return jax.shard_map(local, mesh=mesh, in_specs=in_specs, out_specs=out_specs, check_vma=False)
```

profile of v0, /device:TPU:0, one launch (start us, length us, event | category | flops | bytes accessed | tf_op | source)
XLA Modules:
  0.0 349.6 jit_solution(2469969843966175401)
XLA Ops:
  11.0 1.9 all_gather.6
  12.9 8.4 %all-gather.2.cloned.1.call-done = bf16[8,256,256]{2,1,0:T(8,128)(2,1)} async-done(((bf16[8,128,256]{2,1,0:T(8,128)(2,1)}), bf16[8,256,256]{2,1,0:T(8,128)(2,1)}) %all-gather.2.cloned.1.call-update) | async-done | bytes 1048592 | tf_op jit(solution)/shard_map/all_gather | solution.py:37
  22.7 160.3 %while.23 = (s32[]{:T(128)}, f32[32,32]{1,0:T(8,128)S(1)}, f32[32]{0:T(128)S(1)}, f32[256,256]{1,0:T(8,128)S(1)}, f32[32,256]{1,0:T(8,128)S(1)}, /*index=5*/bf16...) while((s32[]{:T(128)}, f32[32,32]{1,0:T(8,128)S(1)}, ...), condition=%wide.region_6.7_spmd.clone, body=%wide.region_1.6_spmd.clone.sunk | while | flops 259163936 | bytes 40384416 | solution.py:100
  24.5 4.5 %tanh_convert_fusion.2 = bf16[128,256,32]{1,2,0:T(8,128)(2,1)S(1)} fusion(f32[32]{0:T(128)} %get-tuple-element.451, f32[1,128,256]{2,0,1:T(1,128)S(1)} %copy.37, f32[3,128,256]{2,0,1:T(4,128)S(1)} %get-tuple-element.385, f32[32,4]{0,1:T(4,128)} %get-tuple-element.450), kind=kOutput, calls=%fused_computation.6.clone.1 | convolution fusion | flops 52559872 | bytes 2622080 | tf_op jit(solution)/shard_map/while/body/eval_jaxpr/ck,kij->cij/dot_general | solution.py:46
  29.1 2.7 fusion.111
  33.5 3.5 fusion.115
  44.5 4.5 %tanh_convert_fusion.2 = bf16[128,256,32]{1,2,0:T(8,128)(2,1)S(1)} fusion(f32[32]{0:T(128)} %get-tuple-element.451, f32[1,128,256]{2,0,1:T(1,128)S(1)} %copy.37, f32[3,128,256]{2,0,1:T(4,128)S(1)} %get-tuple-element.385, f32[32,4]{0,1:T(4,128)} %get-tuple-element.450), kind=kOutput, calls=%fused_computation.6.clone.1 | convolution fusion | flops 52559872 | bytes 2622080 | tf_op jit(solution)/shard_map/while/body/eval_jaxpr/ck,kij->cij/dot_general | solution.py:46
  49.1 2.7 fusion.111
  53.5 3.5 fusion.115
  64.6 4.5 %tanh_convert_fusion.2 = bf16[128,256,32]{1,2,0:T(8,128)(2,1)S(1)} fusion(f32[32]{0:T(128)} %get-tuple-element.451, f32[1,128,256]{2,0,1:T(1,128)S(1)} %copy.37, f32[3,128,256]{2,0,1:T(4,128)S(1)} %get-tuple-element.385, f32[32,4]{0,1:T(4,128)} %get-tuple-element.450), kind=kOutput, calls=%fused_computation.6.clone.1 | convolution fusion | flops 52559872 | bytes 2622080 | tf_op jit(solution)/shard_map/while/body/eval_jaxpr/ck,kij->cij/dot_general | solution.py:46
  69.1 2.7 fusion.111
  73.6 3.5 fusion.115
  84.6 4.5 %tanh_convert_fusion.2 = bf16[128,256,32]{1,2,0:T(8,128)(2,1)S(1)} fusion(f32[32]{0:T(128)} %get-tuple-element.451, f32[1,128,256]{2,0,1:T(1,128)S(1)} %copy.37, f32[3,128,256]{2,0,1:T(4,128)S(1)} %get-tuple-element.385, f32[32,4]{0,1:T(4,128)} %get-tuple-element.450), kind=kOutput, calls=%fused_computation.6.clone.1 | convolution fusion | flops 52559872 | bytes 2622080 | tf_op jit(solution)/shard_map/while/body/eval_jaxpr/ck,kij->cij/dot_general | solution.py:46
  89.2 2.7 fusion.111
  93.6 3.5 fusion.115
  104.6 4.5 %tanh_convert_fusion.2 = bf16[128,256,32]{1,2,0:T(8,128)(2,1)S(1)} fusion(f32[32]{0:T(128)} %get-tuple-element.451, f32[1,128,256]{2,0,1:T(1,128)S(1)} %copy.37, f32[3,128,256]{2,0,1:T(4,128)S(1)} %get-tuple-element.385, f32[32,4]{0,1:T(4,128)} %get-tuple-element.450), kind=kOutput, calls=%fused_computation.6.clone.1 | convolution fusion | flops 52559872 | bytes 2622080 | tf_op jit(solution)/shard_map/while/body/eval_jaxpr/ck,kij->cij/dot_general | solution.py:46
  109.2 2.7 fusion.111
  113.7 3.5 fusion.115
  124.7 4.5 %tanh_convert_fusion.2 = bf16[128,256,32]{1,2,0:T(8,128)(2,1)S(1)} fusion(f32[32]{0:T(128)} %get-tuple-element.451, f32[1,128,256]{2,0,1:T(1,128)S(1)} %copy.37, f32[3,128,256]{2,0,1:T(4,128)S(1)} %get-tuple-element.385, f32[32,4]{0,1:T(4,128)} %get-tuple-element.450), kind=kOutput, calls=%fused_computation.6.clone.1 | convolution fusion | flops 52559872 | bytes 2622080 | tf_op jit(solution)/shard_map/while/body/eval_jaxpr/ck,kij->cij/dot_general | solution.py:46
  129.2 2.7 fusion.111
  133.7 3.5 fusion.115
  144.7 4.5 %tanh_convert_fusion.2 = bf16[128,256,32]{1,2,0:T(8,128)(2,1)S(1)} fusion(f32[32]{0:T(128)} %get-tuple-element.451, f32[1,128,256]{2,0,1:T(1,128)S(1)} %copy.37, f32[3,128,256]{2,0,1:T(4,128)S(1)} %get-tuple-element.385, f32[32,4]{0,1:T(4,128)} %get-tuple-element.450), kind=kOutput, calls=%fused_computation.6.clone.1 | convolution fusion | flops 52559872 | bytes 2622080 | tf_op jit(solution)/shard_map/while/body/eval_jaxpr/ck,kij->cij/dot_general | solution.py:46
  149.3 2.7 fusion.111
  153.7 3.5 fusion.115
  164.8 4.5 %tanh_convert_fusion.2 = bf16[128,256,32]{1,2,0:T(8,128)(2,1)S(1)} fusion(f32[32]{0:T(128)} %get-tuple-element.451, f32[1,128,256]{2,0,1:T(1,128)S(1)} %copy.37, f32[3,128,256]{2,0,1:T(4,128)S(1)} %get-tuple-element.385, f32[32,4]{0,1:T(4,128)} %get-tuple-element.450), kind=kOutput, calls=%fused_computation.6.clone.1 | convolution fusion | flops 52559872 | bytes 2622080 | tf_op jit(solution)/shard_map/while/body/eval_jaxpr/ck,kij->cij/dot_general | solution.py:46
  169.3 2.7 fusion.111
  173.8 3.5 fusion.115
  183.1 2.5 psum.42
  186.6 62.0 %all-reduce = (f32[32,32]{1,0:T(8,128)S(1)}, f32[32]{0:T(128)S(1)}, f32[32,256]{1,0:T(8,128)S(1)}) all-reduce(f32[32,32]{1,0:T(8,128)S(1)} %get-tuple-element.124, f32[32]{0:T(128)S(1)} %get-tuple-element.125, f32[32,256]{1,0:T(8,128)S(1)} %get-tuple-element.127), channel_id=1, replica_groups=mesh['groups'=2,'slices'=8,'ering'=2] {'slices','ering'}, use_global_device_ids=true, to_apply=%region_9.10 | all-reduce | flops 9248 | bytes 73984 | tf_op jit(solution)/shard_map/psum | solution.py:106
  253.5 2.1 add_convert_fusion.1
  255.6 85.3 %all-reduce.4.cloned.1.call-done = (f32[256,256]{1,0:T(8,128)}, f32[256,256]{1,0:T(8,128)}) async-done(((f32[256,256]{1,0:T(8,128)}, f32[256,256]{1,0:T(8,128)}), (f32[256,256]{1,0:T(8,128)}, f32[256,256]{1,0:T(8,128)})) %all-reduce.4.cloned.1.call-update) | async-done | bytes 524304 | tf_op jit(solution)/shard_map/psum | solution.py:106
  340.9 1.9 broadcast_multiply_fusion
  (265 shorter events, 84.0 us)
Async XLA Ops:
  7.2 244.3 %copy-start = (bf16[3,256]{1,0:T(4,128)(2,1)S(1)}, bf16[3,256]{1,0:T(4,128)(2,1)}, u32[]{:S(2)}) copy-start(bf16[3,256]{1,0:T(4,128)(2,1)} %param.25) | copy-start | bytes 4612
  7.2 14.1 %all-gather.2.cloned.1.call-start = ((), (), s32[]{:S(2)}) async-start(), calls=%async_computation | async-start | bytes 1572864 | tf_op jit(solution)/shard_map/all_gather | solution.py:37
  7.9 333.0 %all-reduce.4.cloned.1.call-start = ((), (), s32[]{:S(2)}) async-start(), calls=%async_computation.1 | async-start | bytes 1048576 | tf_op jit(solution)/shard_map/psum | solution.py:106
  8.7 242.8 %collective-permute-start = (f32[3,1,128]{2,0,1:T(4,128)S(1)}, f32[3,1,128]{2,0,1:T(4,128)S(1)}, u32[]{:S(2)}, u32[]{:S(2)}) collective-permute-start(f32[3,1,128]{2,0,1:T(4,128)S(1)} %slice.9), channel_id=1, source_target_pairs={{2,0},{4,2},{6,4},{8,6},{10,8},{12,10},{14,12},{3,1},{5,3},{7,5},{... | collective-permute-start | bytes 4616 | tf_op jit(solution)/shard_map/ppermute | solution.py:15
  22.7 228.8 %copy-start.6 = (f32[3,8,128]{2,1,0:T(8,128)S(1)}, f32[3,8,128]{2,1,0:T(8,128)}, u32[]{:S(2)}) copy-start(f32[3,8,128]{2,1,0:T(8,128)} %param.14) | copy-start | bytes 36868
  24.5 7.3 %copy-start.4 = (bf16[32,256]{1,0:T(8,128)(2,1)S(1)}, bf16[32,256]{1,0:T(8,128)(2,1)}, u32[]{:S(2)}) copy-start(bf16[32,256]{1,0:T(8,128)(2,1)} %get-tuple-element.454) | copy-start | bytes 49156 | tf_op jit(solution)/shard_map/while
  24.5 7.5 %copy-start.2 = (bf16[256,256]{1,0:T(8,128)(2,1)S(1)}, bf16[256,256]{1,0:T(8,128)(2,1)}, u32[]{:S(2)}) copy-start(bf16[256,256]{1,0:T(8,128)(2,1)} %get-tuple-element.447) | copy-start | bytes 393220 | tf_op jit(solution)/shard_map/while
  24.5 7.5 %copy-start.8 = (f32[256]{0:T(256)S(1)}, f32[256]{0:T(256)}, u32[]{:S(2)}) copy-start(f32[256]{0:T(256)} %get-tuple-element.457) | copy-start | bytes 3076 | tf_op jit(solution)/shard_map/while
  44.5 7.3 %copy-start.4 = (bf16[32,256]{1,0:T(8,128)(2,1)S(1)}, bf16[32,256]{1,0:T(8,128)(2,1)}, u32[]{:S(2)}) copy-start(bf16[32,256]{1,0:T(8,128)(2,1)} %get-tuple-element.454) | copy-start | bytes 49156 | tf_op jit(solution)/shard_map/while
  44.5 7.5 %copy-start.2 = (bf16[256,256]{1,0:T(8,128)(2,1)S(1)}, bf16[256,256]{1,0:T(8,128)(2,1)}, u32[]{:S(2)}) copy-start(bf16[256,256]{1,0:T(8,128)(2,1)} %get-tuple-element.447) | copy-start | bytes 393220 | tf_op jit(solution)/shard_map/while
  44.5 7.5 %copy-start.8 = (f32[256]{0:T(256)S(1)}, f32[256]{0:T(256)}, u32[]{:S(2)}) copy-start(f32[256]{0:T(256)} %get-tuple-element.457) | copy-start | bytes 3076 | tf_op jit(solution)/shard_map/while
  64.5 7.3 %copy-start.4 = (bf16[32,256]{1,0:T(8,128)(2,1)S(1)}, bf16[32,256]{1,0:T(8,128)(2,1)}, u32[]{:S(2)}) copy-start(bf16[32,256]{1,0:T(8,128)(2,1)} %get-tuple-element.454) | copy-start | bytes 49156 | tf_op jit(solution)/shard_map/while
  64.5 7.5 %copy-start.2 = (bf16[256,256]{1,0:T(8,128)(2,1)S(1)}, bf16[256,256]{1,0:T(8,128)(2,1)}, u32[]{:S(2)}) copy-start(bf16[256,256]{1,0:T(8,128)(2,1)} %get-tuple-element.447) | copy-start | bytes 393220 | tf_op jit(solution)/shard_map/while
  64.6 7.5 %copy-start.8 = (f32[256]{0:T(256)S(1)}, f32[256]{0:T(256)}, u32[]{:S(2)}) copy-start(f32[256]{0:T(256)} %get-tuple-element.457) | copy-start | bytes 3076 | tf_op jit(solution)/shard_map/while
  82.9 6.3 %copy-start.7 = (f32[32]{0:T(128)S(1)}, f32[32]{0:T(128)}, u32[]{:S(2)}) copy-start(f32[32]{0:T(128)} %get-tuple-element.453) | copy-start | bytes 388 | tf_op jit(solution)/shard_map/while
  84.6 7.3 %copy-start.4 = (bf16[32,256]{1,0:T(8,128)(2,1)S(1)}, bf16[32,256]{1,0:T(8,128)(2,1)}, u32[]{:S(2)}) copy-start(bf16[32,256]{1,0:T(8,128)(2,1)} %get-tuple-element.454) | copy-start | bytes 49156 | tf_op jit(solution)/shard_map/while
  84.6 7.5 %copy-start.2 = (bf16[256,256]{1,0:T(8,128)(2,1)S(1)}, bf16[256,256]{1,0:T(8,128)(2,1)}, u32[]{:S(2)}) copy-start(bf16[256,256]{1,0:T(8,128)(2,1)} %get-tuple-element.447) | copy-start | bytes 393220 | tf_op jit(solution)/shard_map/while
  84.6 7.5 %copy-start.8 = (f32[256]{0:T(256)S(1)}, f32[256]{0:T(256)}, u32[]{:S(2)}) copy-start(f32[256]{0:T(256)} %get-tuple-element.457) | copy-start | bytes 3076 | tf_op jit(solution)/shard_map/while
  102.9 6.3 %copy-start.7 = (f32[32]{0:T(128)S(1)}, f32[32]{0:T(128)}, u32[]{:S(2)}) copy-start(f32[32]{0:T(128)} %get-tuple-element.453) | copy-start | bytes 388 | tf_op jit(solution)/shard_map/while
  104.6 7.3 %copy-start.4 = (bf16[32,256]{1,0:T(8,128)(2,1)S(1)}, bf16[32,256]{1,0:T(8,128)(2,1)}, u32[]{:S(2)}) copy-start(bf16[32,256]{1,0:T(8,128)(2,1)} %get-tuple-element.454) | copy-start | bytes 49156 | tf_op jit(solution)/shard_map/while
  104.6 7.5 %copy-start.2 = (bf16[256,256]{1,0:T(8,128)(2,1)S(1)}, bf16[256,256]{1,0:T(8,128)(2,1)}, u32[]{:S(2)}) copy-start(bf16[256,256]{1,0:T(8,128)(2,1)} %get-tuple-element.447) | copy-start | bytes 393220 | tf_op jit(solution)/shard_map/while
  104.6 7.5 %copy-start.8 = (f32[256]{0:T(256)S(1)}, f32[256]{0:T(256)}, u32[]{:S(2)}) copy-start(f32[256]{0:T(256)} %get-tuple-element.457) | copy-start | bytes 3076 | tf_op jit(solution)/shard_map/while
  124.7 7.3 %copy-start.4 = (bf16[32,256]{1,0:T(8,128)(2,1)S(1)}, bf16[32,256]{1,0:T(8,128)(2,1)}, u32[]{:S(2)}) copy-start(bf16[32,256]{1,0:T(8,128)(2,1)} %get-tuple-element.454) | copy-start | bytes 49156 | tf_op jit(solution)/shard_map/while
  124.7 7.5 %copy-start.2 = (bf16[256,256]{1,0:T(8,128)(2,1)S(1)}, bf16[256,256]{1,0:T(8,128)(2,1)}, u32[]{:S(2)}) copy-start(bf16[256,256]{1,0:T(8,128)(2,1)} %get-tuple-element.447) | copy-start | bytes 393220 | tf_op jit(solution)/shard_map/while
  124.7 7.5 %copy-start.8 = (f32[256]{0:T(256)S(1)}, f32[256]{0:T(256)}, u32[]{:S(2)}) copy-start(f32[256]{0:T(256)} %get-tuple-element.457) | copy-start | bytes 3076 | tf_op jit(solution)/shard_map/while
  144.7 7.3 %copy-start.4 = (bf16[32,256]{1,0:T(8,128)(2,1)S(1)}, bf16[32,256]{1,0:T(8,128)(2,1)}, u32[]{:S(2)}) copy-start(bf16[32,256]{1,0:T(8,128)(2,1)} %get-tuple-element.454) | copy-start | bytes 49156 | tf_op jit(solution)/shard_map/while
  144.7 7.5 %copy-start.2 = (bf16[256,256]{1,0:T(8,128)(2,1)S(1)}, bf16[256,256]{1,0:T(8,128)(2,1)}, u32[]{:S(2)}) copy-start(bf16[256,256]{1,0:T(8,128)(2,1)} %get-tuple-element.447) | copy-start | bytes 393220 | tf_op jit(solution)/shard_map/while
  144.7 7.5 %copy-start.8 = (f32[256]{0:T(256)S(1)}, f32[256]{0:T(256)}, u32[]{:S(2)}) copy-start(f32[256]{0:T(256)} %get-tuple-element.457) | copy-start | bytes 3076 | tf_op jit(solution)/shard_map/while
  164.7 7.3 %copy-start.4 = (bf16[32,256]{1,0:T(8,128)(2,1)S(1)}, bf16[32,256]{1,0:T(8,128)(2,1)}, u32[]{:S(2)}) copy-start(bf16[32,256]{1,0:T(8,128)(2,1)} %get-tuple-element.454) | copy-start | bytes 49156 | tf_op jit(solution)/shard_map/while
  164.7 7.5 %copy-start.2 = (bf16[256,256]{1,0:T(8,128)(2,1)S(1)}, bf16[256,256]{1,0:T(8,128)(2,1)}, u32[]{:S(2)}) copy-start(bf16[256,256]{1,0:T(8,128)(2,1)} %get-tuple-element.447) | copy-start | bytes 393220 | tf_op jit(solution)/shard_map/while
  164.8 7.5 %copy-start.8 = (f32[256]{0:T(256)S(1)}, f32[256]{0:T(256)}, u32[]{:S(2)}) copy-start(f32[256]{0:T(256)} %get-tuple-element.457) | copy-start | bytes 3076 | tf_op jit(solution)/shard_map/while
  183.1 70.4 %copy-start.3 = (f32[256,256]{1,0:T(8,128)}, f32[256,256]{1,0:T(8,128)S(1)}, u32[]{:S(2)}) copy-start(f32[256,256]{1,0:T(8,128)S(1)} %get-tuple-element.126) | copy-start | bytes 786436
  (22 other events, 116.2 us)
Sparse Core Ops, SparseCore 0:
  9.6 11.7 all-gather.1
  253.6 87.2 all-reduce.3
where the time goes:
time: 352 us; the launch traced here: 350 us
  matrix products  132 us (38%)
  waiting for transfers between devices  94.4 us (27%)
  blocking collectives  66.4 us (19%)
  other arithmetic  35.4 us (10%)
  between operations  14.2 us (4%)
  local copies, waits for them, and re-layouts  4.24 us (1%)
    psum x1, waiting for transfers between devices, local(): lax.psum((grads[0], grads[1], grads[2], grads[3], grads[4]), ('slices', '...  85.3 us
    psum x1, blocking collectives, local(): lax.psum((grads[0], grads[1], grads[2], grads[3], grads[4]), ('slices', '...  62 us
    dot_general x8, matrix products, one_slice(): jnp.einsum('ck,kij->cij', embed_weight, features, precision=HIGH)  36.2 us
    dot_general x8, matrix products, one_slice(): jnp.einsum('cij,kij->ck', act_low, pair_in, preferred_element_type=jnp.fl...  27.9 us
    dot_general x8, matrix products, one_slice(): jnp.einsum('ck,kij->cij', pair_weight, pair_in, preferred_element_type=jn...  21.9 us
    dot_general x8, matrix products, one_slice(): jnp.dot(pre_grad, one_weight.T, preferred_element_type=jnp.float32)  13.5 us
    dynamic_update_slice x8, other arithmetic, local(): lax.scan(one_slice, start, inputs)  11.9 us
    reduce_sum x8, other arithmetic, one_slice(): bias_term = jnp.sum(act_grad, axis=(1, 2))  11.8 us
  transfers between devices with their start and end apart: 3, of which 2 were waited for; matrix products, arithmetic and copies ran while one was open for 48% of the time, Pallas kernels for 0%

commit v1 on v0

v1 whole, which is shorter than its diff:
```python
import math

import jax
import jax.numpy as jnp
from jax import lax
from jax.experimental import pallas as pl
from jax.experimental.pallas import tpu as pltpu
from jax.sharding import PartitionSpec as P

HIGH = lax.Precision.HIGHEST
f32 = jnp.float32
bf16 = jnp.bfloat16
step_tau = 0.5
VMEM_LIMIT = 56 << 20


def dot(a, b, ca, cb, precision=None):
    return lax.dot_general(
        a, b, (((ca,), (cb,)), ((), ())), preferred_element_type=f32, precision=precision
    )


def split3(x):
    first = x.astype(bf16).astype(f32)
    rest = x - first
    second = rest.astype(bf16).astype(f32)
    return first, second, rest - second


def iota(shape, dim):
    return lax.broadcasted_iota(jnp.int32, shape, dim)


def pair_kernel(
    own_ref, other_ref, ew_ref, eb_ref, pw_ref, pb_ref,
    pooled_ref, h_ref, g_ref,
    embed_mat, block_mat, a_rows, feat, bias_row,
):
    s = pl.program_id(0)

    @pl.when(s == 0)
    def _():
        wide = jnp.concatenate([ew_ref[...].T] * 8, axis=1)
        w1, w2, w3 = split3(wide)
        row = iota((256, 256), 0)
        lane = iota((256, 256), 1)
        for g in range(8):
            hit = (row % 64 == g * 8 + lane // 32) & (row < 192)
            out = jnp.where(hit, jnp.where(row < 128, w1[3:4, :], w2[3:4, :]), 0.0)
            pieces = (w1, w2, w3, w1, w2, w1)
            for c in range(3):
                for p in range(6):
                    out = jnp.where(row == 192 + 6 * c + p, -pieces[p][c : c + 1, :], out)
            embed_mat[:, g * 256 : (g + 1) * 256] = out.astype(bf16)
        tiled = jnp.concatenate([pw_ref[...].astype(f32).T] * 8, axis=1)
        tiled = jnp.concatenate([tiled] * 8, axis=0)
        block_mat[...] = jnp.where(row // 32 == lane // 32, tiled, 0.0).astype(bf16)
        bias_row[...] = jnp.broadcast_to(jnp.concatenate([pb_ref[...]] * 8, axis=1), (8, 256))
        wide_bias = jnp.concatenate([eb_ref[...]] * 8, axis=1)
        electron = iota((128, 256), 0)
        lane128 = iota((128, 256), 1)
        for g in range(16):
            pick = jnp.where(electron == g * 8 + lane128 // 32, 1.0, 0.0).astype(bf16)
            total = jnp.broadcast_to(wide_bias, (own_ref.shape[1], 256))
            for c in range(3):
                spread = sum(dot(q.astype(bf16), pick, 1, 0) for q in split3(own_ref[c]))
                total = total + spread * wide[c : c + 1, :]
            a_rows[:, g * 256 : (g + 1) * 256] = total

    lane = iota((256, 128), 1)
    square = jnp.ones((256, 128), f32)
    misc = jnp.zeros((256, 128), f32)
    rows = [own_ref[c, pl.ds(s, 1), :] for c in range(3)]
    others = [other_ref[c, pl.ds(s, 1), :] for c in range(3)]
    stacked = jnp.concatenate(
        [jnp.concatenate([rows[c], others[c]], axis=1) for c in range(3)]
        + [jnp.zeros((5, 256), f32)],
        axis=0,
    )
    columns = stacked.T
    for c in range(3):
        spread = jnp.broadcast_to(columns[:, c : c + 1], (256, 128))
        offset = spread - rows[c]
        square = square + offset * offset
        s1, s2, s3 = split3(spread)
        base = 64 + 6 * c
        misc = jnp.where((lane >= base) & (lane < base + 3), s1, misc)
        misc = jnp.where((lane >= base + 3) & (lane < base + 5), s2, misc)
        misc = jnp.where(lane == base + 5, s3, misc)
    radial = jnp.sqrt(square)
    high = radial.astype(bf16).astype(f32)
    low = radial - high
    high_turned = pltpu.roll(high, 64, 1)
    low_turned = pltpu.roll(low, 64, 1)
    left = lane < 64
    feat[0, :, :128] = jnp.where(left, high, low_turned).astype(bf16)
    feat[0, :, 128:] = jnp.where(left, high, misc).astype(bf16)
    feat[1, :, :128] = jnp.where(left, high_turned, low).astype(bf16)
    feat[1, :, 128:] = jnp.where(left, high_turned, misc).astype(bf16)
    diagonal = iota((8, 256), 0) == iota((8, 256), 1) // 32
    block = iota((32, 256), 1) // 32
    for g in range(16):
        half, inner = g // 8, g % 8
        pre = dot(feat[half], embed_mat[:, inner * 256 : (inner + 1) * 256], 1, 0)
        pre = pre + a_rows[pl.ds(s, 1), g * 256 : (g + 1) * 256]
        wide_in = jnp.tanh(pre)
        pair_in = wide_in.astype(bf16)
        act = jnp.tanh(dot(pair_in, block_mat[...], 1, 0) + bias_row[0:1, :])
        mean = jnp.sum(wide_in + act, axis=0, keepdims=True) * (1.0 / 256)
        slope = 1.0 - act * act
        h_ref[0, g : g + 1, :] = jnp.sum(slope, axis=0, keepdims=True)
        pooled_ref[0, g * 8 : (g + 1) * 8, :] = jnp.where(diagonal, mean, 0.0)
        outer = dot(pair_in, slope.astype(bf16), 0, 0)
        picked = outer[0:32]
        for q in range(1, 8):
            picked = jnp.where(block == q, outer[q * 32 : (q + 1) * 32], picked)
        g_ref[0, g * 32 : (g + 1) * 32, :] = picked


def pair_call(own, other, ew, eb, pw, pb):
    count = own.shape[1]
    args = (own, other, ew, eb.reshape(1, 32), pw, pb.reshape(1, 32))
    return pl.pallas_call(
        pair_kernel,
        grid=(count,),
        in_specs=[pl.BlockSpec(a.shape, lambda s, n=a.ndim: (0,) * n) for a in args],
        out_specs=[
            pl.BlockSpec((1, 128, 256), lambda s: (s, 0, 0)),
            pl.BlockSpec((1, 16, 256), lambda s: (s, 0, 0)),
            pl.BlockSpec((1, 512, 256), lambda s: (s, 0, 0)),
        ],
        out_shape=[
            jax.ShapeDtypeStruct((count, 128, 256), f32),
            jax.ShapeDtypeStruct((count, 16, 256), f32),
            jax.ShapeDtypeStruct((count, 512, 256), f32),
        ],
        scratch_shapes=[
            pltpu.VMEM((256, 2048), bf16),
            pltpu.VMEM((256, 256), bf16),
            pltpu.VMEM((count, 4096), f32),
            pltpu.VMEM((2, 256, 256), bf16),
            pltpu.VMEM((8, 256), f32),
        ],
        compiler_params=pltpu.CompilerParams(vmem_limit_bytes=VMEM_LIMIT),
        name="pair_stage",
    )(*args)


RED = 336
HALF = RED // 2


def one_kernel(
    core_ref, hid_ref, cot_ref, pooled_ref, h_ref, g_ref, sum_a_ref, sum_b_ref,
    ow_ref, qw_ref, mw_ref, ob_ref,
    updated_ref, pre_ref, keep_ref, send_ref, mean_ref,
    red,
):
    count = sum_a_ref.shape[0]
    mean_rows = ((sum_a_ref[...] + sum_b_ref[...]) * (1.0 / 256)).astype(bf16)
    mean_ref[...] = mean_rows.astype(f32)
    per_slice = dot(mean_rows, mw_ref[...], 1, 0) + ob_ref[...]
    pool_tiled = jnp.concatenate([qw_ref[...]] * 8, axis=0)
    one_total = jnp.zeros((256, 256), f32)
    pool_total = jnp.zeros((256, 256), f32)
    pair_total = jnp.zeros((32, 256), f32)
    bias_total = jnp.zeros((16, 256), f32)
    own_lanes = iota((128, 256), 0) % 8 == iota((128, 256), 1) // 32
    parts = []
    for s in range(count):
        at = slice(s * 128, (s + 1) * 128)
        hid = hid_ref[at, :]
        pooled = pooled_ref[at, :].astype(bf16)
        pre = dot(hid, ow_ref[...], 1, 0) + dot(pooled, pool_tiled, 1, 0) + per_slice[s : s + 1, :]
        act = jnp.tanh(pre)
        updated_ref[at, :] = (act + hid.astype(f32)).astype(bf16)
        grad = (cot_ref[at, :].astype(f32) * (1.0 - act * act)).astype(bf16)
        pre_ref[at, :] = grad
        parts.append(jnp.sum(grad.astype(f32), axis=0, keepdims=True))
        one_total = one_total + dot(hid, grad, 0, 0)
        pool_total = pool_total + dot(pooled, grad, 0, 0)
        back = jnp.where(own_lanes, dot(grad, pool_tiled, 1, 1), 0.0)
        back = jnp.sum(back.reshape(16, 8, 256), axis=1)
        bias_total = bias_total + back * h_ref[s * 16 : (s + 1) * 16, :]
        for g in range(16):
            base = s * 512 + g * 32
            pair_total = pair_total + g_ref[base : base + 32, :] * back[g : g + 1, :]
    fold = jnp.where(iota((256, 128), 0) % 32 == iota((256, 128), 1), 1.0, 0.0)
    pool = pool_total[0:32]
    for q in range(1, 8):
        pool = pool + pool_total[q * 32 : (q + 1) * 32]
    bias_one = jnp.broadcast_to(jnp.sum(bias_total, axis=0, keepdims=True), (16, 256))
    red[0:256, :] = one_total
    red[256:288, :] = pool
    red[288:336, :] = jnp.zeros((48, 256), f32)
    red[288:320, 0:128] = dot(pair_total, fold, 1, 0, HIGH)
    red[320:336, 0:128] = dot(bias_one, fold, 1, 0, HIGH)
    core = core_ref[0]
    keep_ref[...] = red[pl.ds(pl.multiple_of(core * HALF, 8), HALF), :]
    send_ref[0:HALF, :] = red[pl.ds(pl.multiple_of((1 - core) * HALF, 8), HALF), :]
    send_ref[HALF:, :] = jnp.concatenate(parts, axis=0)
    mean_ref[...] = mean_rows.astype(f32)


def one_call(core, hid, cot, pooled, h_sums, g_sums, sum_a, sum_b, ow, qw, mw, ob):
    rows = hid.shape[0]
    count = sum_a.shape[0]
    args = (core, hid, cot, pooled, h_sums, g_sums, sum_a, sum_b, ow, qw, mw, ob.reshape(1, 256))
    whole = pl.BlockSpec(memory_space=pltpu.VMEM)
    return pl.pallas_call(
        one_kernel,
        in_specs=[pl.BlockSpec(memory_space=pltpu.SMEM)] + [whole] * (len(args) - 1),
        out_specs=[whole] * 5,
        out_shape=[
            jax.ShapeDtypeStruct((rows, 256), bf16),
            jax.ShapeDtypeStruct((rows, 256), bf16),
            jax.ShapeDtypeStruct((HALF, 256), f32),
            jax.ShapeDtypeStruct((HALF + count, 256), f32),
            jax.ShapeDtypeStruct((count, 256), f32),
        ],
        scratch_shapes=[pltpu.VMEM((RED, 256), f32)],
        compiler_params=pltpu.CompilerParams(vmem_limit_bytes=VMEM_LIMIT),
        name="one_stage",
    )(*args)


def back_kernel(
    cot_ref, pre_ref, upd_ref, col_ref, pos_ref, ow_ref, mw_ref, dw_ref,
    grad_ref, link_ref, last_ref,
):
    count = col_ref.shape[0]
    back = dot(col_ref[...], mw_ref[...].astype(f32), 1, 1, HIGH) * (1.0 / 256)
    drifts = []
    for s in range(count):
        at = slice(s * 128, (s + 1) * 128)
        grad = cot_ref[at, :].astype(f32) + dot(pre_ref[at, :], ow_ref[...], 1, 1)
        grad_ref[at, :] = (grad + back[s : s + 1, :]).astype(bf16)
        drifts.append(dot(dw_ref[...], upd_ref[at, :], 1, 1))
    for s in range(count):
        here = [-pos_ref[c, s : s + 1, :] - step_tau * drifts[s][c : c + 1, :] for c in range(3)]
        if s < count - 1:
            jumps = [here[c] + pos_ref[c, s + 1 : s + 2, :] for c in range(3)]
            total = jumps[0] * jumps[0] + jumps[1] * jumps[1] + jumps[2] * jumps[2]
            link_ref[s : s + 1, :] = total * (1.0 / (12.0 * step_tau))
        else:
            link_ref[s : s + 1, :] = jnp.zeros((1, 128), f32)
            last_ref[...] = jnp.concatenate(here + [jnp.zeros((5, 128), f32)], axis=0)


def back_call(cot, pre, updated, col, pos, ow, mw, dw):
    whole = pl.BlockSpec(memory_space=pltpu.VMEM)
    args = (cot, pre, updated, col, pos, ow, mw, dw)
    return pl.pallas_call(
        back_kernel,
        in_specs=[whole] * len(args),
        out_specs=[whole] * 3,
        out_shape=[
            jax.ShapeDtypeStruct(cot.shape, bf16),
            jax.ShapeDtypeStruct((col.shape[0], 128), f32),
            jax.ShapeDtypeStruct((8, 128), f32),
        ],
        compiler_params=pltpu.CompilerParams(vmem_limit_bytes=VMEM_LIMIT),
        name="hidden_back",
    )(*args)


def end_kernel(
    info_ref, own_ref, other_ref, gath_ref, link_ref, last_ref,
    one_ref, pool_ref, pair_ref, bias_ref, mean_ref, out_link_ref,
    red, mean_all, col_all, *, scale, count, stride,
):
    core = info_ref[0]
    red[pl.ds(pl.multiple_of(core * HALF, 8), HALF), :] = own_ref[...]
    red[pl.ds(pl.multiple_of((1 - core) * HALF, 8), HALF), :] = other_ref[...]
    one_ref[...] = scale * red[0:256, :]
    pool_ref[...] = scale * red[256:288, :]
    pair_ref[...] = (scale / 256.0) * red[288:320, 0:128].T[0:32, :]
    bias_ref[...] = (scale / 256.0) * red[320:321, 0:32]
    devices = gath_ref.shape[0] // stride
    for d in range(devices):
        mean_all[d * count : (d + 1) * count, :] = gath_ref[d * stride : d * stride + count, :]
        base = d * stride + count
        col_all[d * count : (d + 1) * count, :] = gath_ref[base : base + count, :]
    mean_ref[...] = scale * dot(mean_all[...], col_all[...], 0, 0, HIGH)
    out_link_ref[...] = link_ref[...]
    at = pl.multiple_of(info_ref[1] * stride + 2 * count, 8)
    jump = gath_ref[pl.ds(at, 8), 0:128] + last_ref[...]
    total = jnp.sum(jump * jump, axis=0, keepdims=True) * (1.0 / (12.0 * step_tau))
    out_link_ref[count - 1 : count, :] = jnp.where(info_ref[2] == 1, 0.0, total)


def end_call(info, own, other, gath, link, last, scale, count, stride):
    whole = pl.BlockSpec(memory_space=pltpu.VMEM)
    args = (info, own, other, gath, link, last)
    devices = gath.shape[0] // stride

    def body(*refs):
        end_kernel(*refs, scale=scale, count=count, stride=stride)

    return pl.pallas_call(
        body,
        in_specs=[pl.BlockSpec(memory_space=pltpu.SMEM)] + [whole] * (len(args) - 1),
        out_specs=[whole] * 6,
        out_shape=[
            jax.ShapeDtypeStruct((256, 256), f32),
            jax.ShapeDtypeStruct((32, 256), f32),
            jax.ShapeDtypeStruct((32, 32), f32),
            jax.ShapeDtypeStruct((1, 32), f32),
            jax.ShapeDtypeStruct((256, 256), f32),
            jax.ShapeDtypeStruct((count, 128), f32),
        ],
        scratch_shapes=[
            pltpu.VMEM((RED, 256), f32),
            pltpu.VMEM((devices * count, 256), f32),
            pltpu.VMEM((devices * count, 256), f32),
        ],
        compiler_params=pltpu.CompilerParams(vmem_limit_bytes=VMEM_LIMIT),
        name="unpack",
    )(*args)


def local(
    positions, hidden, cotangent, embed_weight, embed_bias, pair_weight, pair_bias,
    one_weight, pool_weight, mean_weight, one_bias, drift_weight,
):
    count, own_count, width = hidden.shape
    slices = lax.axis_size("slices")
    bits = slices.bit_length() - 1
    scale = 1.0 / math.sqrt(count * slices * own_count * lax.axis_size("ering"))
    core = lax.axis_index("ering")
    place = lax.axis_index("slices")

    def swap(array):
        return lax.ppermute(array, "ering", [(0, 1), (1, 0)])

    other_pos = swap(positions)
    part_sum = jnp.sum(hidden.astype(f32), axis=1)
    other_sum = swap(part_sum)
    pooled, h_sums, g_sums = pair_call(
        positions, other_pos, embed_weight, embed_bias, pair_weight, pair_bias
    )
    flat = (count * own_count, width)
    hid = hidden.reshape(flat)
    cot = cotangent.reshape(flat)
    core_arr = core.reshape(1).astype(jnp.int32)
    updated, pre, keep, send, mean_rows = one_call(
        core_arr, hid, cot, pooled.reshape(flat), h_sums.reshape(-1, 256),
        g_sums.reshape(-1, 256), part_sum, other_sum, one_weight, pool_weight, mean_weight, one_bias,
    )
    came = swap(send)
    total = keep + came[:HALF]
    col_total = send[HALF:] + came[HALF:]
    border = jnp.pad(positions[:, 0, :], ((0, 5), (0, 128)))
    gath = jnp.concatenate([mean_rows, col_total, border], axis=0)
    stride = gath.shape[0]
    hidden_grad, link, last = back_call(
        cot, pre, updated, col_total, positions, one_weight, mean_weight, drift_weight
    )
    orders = [[(t + e) % max(bits, 1) for t in range(bits)] for e in range(2)]
    for t in range(bits):
        pairs = [
            (s * 2 + e, (s ^ (1 << orders[e][t])) * 2 + e) for s in range(slices) for e in range(2)
        ]
        came = lax.ppermute(
            jnp.concatenate([total, gath], axis=0), ("slices", "ering"), pairs
        )
        total = total + came[:HALF]
        gath = jnp.concatenate([gath, came[HALF:]], axis=0)
    other_total = swap(total)
    apart = place ^ jnp.minimum(place + 1, slices - 1)
    found = jnp.int32(0)
    for t in range(bits):
        bit = jnp.where(core == 0, apart >> orders[0][t], apart >> orders[1][t]) & 1
        found = found + (bit << t)
    info = jnp.stack([core, found, (place == slices - 1).astype(jnp.int32)]).astype(jnp.int32)
    one_grad, pool_grad, pair_grad, bias_grad, mean_grad, link_terms = end_call(
        info, total, other_total, gath, link, last, scale, count, stride
    )
    return (
        updated.reshape(hidden.shape),
        hidden_grad.reshape(hidden.shape),
        link_terms,
        pair_grad,
        bias_grad.reshape(-1),
        one_grad,
        pool_grad,
        mean_grad,
    )


def solution(mesh):
    in_specs = (
        P(None, ("groups", "slices"), "ering"),
        P(("groups", "slices"), "ering", None),
        P(("groups", "slices"), "ering", None),
    ) + (P(),) * 9
    out_specs = (
        P(("groups", "slices"), "ering", None),
        P(("groups", "slices"), "ering", None),
        P(("groups", "slices"), "ering"),
        P("groups", None),
        P("groups"),
        P("groups", None),
        P("groups", None),
        P("groups", None),
    )
    return jax.shard_map(local, mesh=mesh, in_specs=in_specs, out_specs=out_specs, check_vma=False)
```

time: 352 us -> 88.5 us (0.25)
  matrix products: 132 us -> 0 us
  waiting for transfers between devices: 94.4 us -> 14.3 us
  blocking collectives: 66.4 us -> 0 us
  Pallas kernels: 0 us -> 53.6 us
  other arithmetic: 35.4 us -> 4.22 us
  between operations: 14.2 us -> 0.73 us
  starting transfers between devices: 1.36 us -> 8.94 us
    dot_general x83 -> x0, matrix products: 132 us -> none  [the longest x8 36.2 us: one_slice(): jnp.einsum('ck,kij->cij', embed_weight, features, precision=HIGH)]
    psum x1 -> x0, waiting for transfers between devices: 85.3 us -> none  [local(): lax.psum((grads[0], grads[1], grads[2], grads[3], grads[4]), ('slices', '...]
    psum x2 -> x0, blocking collectives: 64.5 us -> none  [the longest x1 62 us: local(): lax.psum((grads[0], grads[1], grads[2], grads[3], grads[4]), ('slices', '...]
    pallas_call x0 -> x4, Pallas kernels: none -> 53.6 us  [the longest x1 41.8 us: pair_call(): pl.pallas_call(pair_kernel, grid=(count,), in_specs=[pl.BlockSpec(a.shape...]
    ppermute x1 -> x7, waiting for transfers between devices: 0.01 us -> 14.3 us  [the longest x3 13 us: local(): lax.ppermute(jnp.concatenate([total, gath], axis=0), ('slices', 'ering'),...]
    reduce_sum x9 -> x1, other arithmetic: 13.2 us -> 1.12 us  [local(): part_sum = jnp.sum(hidden.astype(f32), axis=1)]
    dynamic_update_slice x8 -> x0, other arithmetic: 11.9 us -> none  [local(): lax.scan(one_slice, start, inputs)]
    all_gather x1 -> x0, waiting for transfers between devices: 8.4 us -> none  [local(): full_rows = lax.all_gather(hidden, 'ering', axis=1, tiled=True)]
  transfers between devices with their start and end apart: 3 -> 7, of which waited for: 2 -> 4; matrix products, arithmetic and copies ran while one was open for 48% -> 5% of each run, Pallas kernels for 0% -> 51%
where the time goes in v1:
time: 88.5 us; the launch traced here: 87.9 us
  Pallas kernels  53.6 us (61%)
  waiting for transfers between devices  14.3 us (16%)
  starting transfers between devices  8.94 us (10%)
  local copies, waits for them, and re-layouts  6.07 us (7%)
  other arithmetic  4.22 us (5%)
    pallas_call x1, Pallas kernels, pair_call(): pl.pallas_call(pair_kernel, grid=(count,), in_specs=[pl.BlockSpec(a.shape...  41.8 us
    ppermute x3, waiting for transfers between devices, local(): lax.ppermute(jnp.concatenate([total, gath], axis=0), ('slices', 'ering'),...  13 us
    ppermute x3, starting transfers between devices, local(): lax.ppermute(jnp.concatenate([total, gath], axis=0), ('slices', 'ering'),...  7.78 us
    pallas_call x1, Pallas kernels, one_call(): pl.pallas_call(one_kernel, in_specs=[pl.BlockSpec(memory_space=pltpu.SMEM...  6.51 us
    unnamed x25, local copies, waits for them, and re-layouts  5.34 us
    pallas_call x1, Pallas kernels, back_call(): pl.pallas_call(back_kernel, in_specs=[whole] * len(args), out_specs=[whol...  3.05 us
    pallas_call x1, Pallas kernels, end_call(): pl.pallas_call(body, in_specs=[pl.BlockSpec(memory_space=pltpu.SMEM)] + [...  2.28 us
  transfers between devices with their start and end apart: 7, of which 4 were waited for; matrix products, arithmetic and copies ran while one was open for 5% of the time, Pallas kernels for 51%

profile of v1, /device:TPU:0, one launch (start us, length us, event | category | flops | bytes accessed | tf_op | source)
XLA Modules:
  0.0 87.9 jit_solution(14418412621060011182)
XLA Ops:
  0.6 0.5 collective-permute-start
  1.1 1.1 %convert_reduce_fusion.sum_a_ref = f32[8,256]{1,0:T(8,128)S(1)} fusion(bf16[8,128,256]{2,1,0:T(8,128)(2,1)} %param.13), kind=kLoop, calls=%fused_computation | loop fusion | flops 522240 | bytes 532480 | tf_op jit(solution)/shard_map/reduce_sum | solution.py:337
  2.3 0.1 collective-permute-start.1
  2.4 1.4 %copy.20.ew_ref = f32[32,4]{1,0:T(8,128)} copy(f32[32,4]{0,1:T(4,128)} %param.15) | data formatting | bytes 1024 | tf_op args[3]
  3.8 0.0 collective-permute-done.other_ref
  3.8 0.6 copy-done.5
  4.4 41.8 %pair_stage.1 = (f32[8,128,256]{2,1,0:T(8,128)}, f32[8,16,256]{2,1,0:T(8,128)}, f32[8,512,256]{2,1,0:T(8,128)}) custom-call(f32[3,8,128]{2,1,0:T(8,128)} %pos_ref.1, f32[3,8,128]{2,1,0:T(8,128)} %copy-done.5, f32[32,4]{1,0:T(8,128)} %copy.20.ew_ref, f32[1,32]{1,0:T(1,128)} %bitcast.28, bf16[32,32]{1,0:T(8,128)(2,1)} %pw_ref.1, f32[1,32]{1,0:T(1,128)} %bitcast.29), custom_call_target="tpu_custom_call" | custom-call | tf_op jit(solution)/shard_map/pair_stage/pallas_call | solution.py:123
  46.2 0.0 collective-permute-done.1.sum_b_ref
  46.2 0.6 copy-done.6
  46.8 6.5 %one_stage.1 = (bf16[1024,256]{1,0:T(8,128)(2,1)}, bf16[1024,256]{1,0:T(8,128)(2,1)}, f32[168,256]{1,0:T(8,128)}, f32[176,256]{1,0:T(8,128)}, f32[8,256]{1,0:T(8,128)}) custom-call(s32[1]{0:T(128)} %bitcast.core_ref, bf16[1024,256]{1,0:T(8,128)(2,1)} %bitcast.20, bf16[1024,256]{1,0:T(8,128)(2,1)} %bitcast.18, f32[1024,256]{1,0:T(8,128)} %bitcast.21, ...), custom_call_target="tpu_custom_call" | custom-call | tf_op jit(solution)/shard_map/one_stage/pallas_call | solution.py:210
  53.3 0.5 collective-permute-start.2
  53.7 0.7 slice.33
  54.4 0.7 constant_dynamic-update-slice_fusion.12
  55.1 0.0 collective-permute-done.2
  55.1 0.7 constant_dynamic-update-slice_fusion.11
  55.8 0.9 %slice_add_fusion.3 = f32[168,256]{1,0:T(8,128)S(1)} fusion(f32[168,256]{1,0:T(8,128)} %get-tuple-element.32, f32[176,256]{1,0:T(8,128)S(1)} %collective-permute-done.2), kind=kLoop, calls=%fused_computation.5 | loop fusion | flops 43008 | bytes 516096 | tf_op jit(solution)/shard_map/add | solution.py:351
  56.8 0.7 pad_maximum_fusion
  57.5 2.8 %collective-permute-start.3 = (f32[192,256]{1,0:T(8,128)S(1)}, f32[192,256]{1,0:T(8,128)S(1)}, u32[]{:S(2)}, u32[]{:S(2)}) collective-permute-start(f32[192,256]{1,0:T(8,128)S(1)} %pad_maximum_fusion), channel_id=1, source_target_pairs={{0,2},{1,5},{2,0},{3,7},{4,6},{5,1},{6,4},{7,3},{8,10},{9,13},{10,... | collective-permute-start | bytes 589832 | tf_op jit(solution)/shard_map/ppermute | solution.py:364
  60.3 3.6 %collective-permute-done.3 = f32[192,256]{1,0:T(8,128)S(1)} collective-permute-done((f32[192,256]{1,0:T(8,128)S(1)}, f32[192,256]{1,0:T(8,128)S(1)}, u32[]{:S(2)}, u32[]{:S(2)}) %collective-permute-start.3) | collective-permute-done | bytes 196640 | tf_op jit(solution)/shard_map/ppermute | solution.py:364
  63.9 0.7 constant_dynamic-update-slice_fusion.3
  64.7 2.2 %collective-permute-start.4 = (f32[216,256]{1,0:T(8,128)S(1)}, f32[216,256]{1,0:T(8,128)S(1)}, u32[]{:S(2)}, u32[]{:S(2)}) collective-permute-start(f32[216,256]{1,0:T(8,128)S(1)} %constant_dynamic-update-slice_fusion), channel_id=1, source_target_pairs={{0,4},{1,9},{2,6},{3,11},{4,0},{5,13},{6,2},{7,15},{8,12},{9,1},{1... | collective-permute-start | bytes 663560 | tf_op jit(solution)/shard_map/ppermute | solution.py:364
  66.8 5.5 %collective-permute-done.4 = f32[216,256]{1,0:T(8,128)S(1)} collective-permute-done((f32[216,256]{1,0:T(8,128)S(1)}, f32[216,256]{1,0:T(8,128)S(1)}, u32[]{:S(2)}, u32[]{:S(2)}) %collective-permute-start.4) | collective-permute-done | bytes 221216 | tf_op jit(solution)/shard_map/ppermute | solution.py:364
  72.4 0.7 constant_dynamic-update-slice_fusion.7
  73.1 2.9 %collective-permute-start.5 = (f32[264,256]{1,0:T(8,128)S(1)}, f32[264,256]{1,0:T(8,128)S(1)}, u32[]{:S(2)}, u32[]{:S(2)}) collective-permute-start(f32[264,256]{1,0:T(8,128)S(1)} %get-tuple-element.45), channel_id=1, source_target_pairs={{0,8},{1,3},{2,10},{3,1},{4,12},{5,7},{6,14},{7,5},{8,0},{9,11},{1... | collective-permute-start | bytes 811016 | tf_op jit(solution)/shard_map/ppermute | solution.py:364
  76.0 0.6 pad_add_fusion.refs_0_
  76.6 3.1 %hidden_back.1 = (bf16[1024,256]{1,0:T(8,128)(2,1)}, f32[8,128]{1,0:T(8,128)}, f32[8,128]{1,0:T(8,128)}) custom-call(bf16[1024,256]{1,0:T(8,128)(2,1)} %bitcast.19, bf16[1024,256]{1,0:T(8,128)(2,1)} %get-tuple-element.29.pre_ref, bf16[1024,256]{1,0:T(8,128)(2,1)} %get-tuple-element.28.upd_ref, f32[8,256]{1,0:T(8,128)} %copy-done.2, f32[3,8,128]{2,1,0:T(8,128)} %pos_ref.1, ...), custom_call_target="tpu_custom_call" | custom-call | tf_op jit(solution)/shard_map/hidden_back/pallas_call | solution.py:253
  79.6 3.8 %collective-permute-done.5 = f32[264,256]{1,0:T(8,128)S(1)} collective-permute-done((f32[264,256]{1,0:T(8,128)S(1)}, f32[264,256]{1,0:T(8,128)S(1)}, u32[]{:S(2)}, u32[]{:S(2)}) %collective-permute-start.5) | collective-permute-done | bytes 270368 | tf_op jit(solution)/shard_map/ppermute | solution.py:364
  83.4 0.1 slice_add_fusion.refs_1_
  83.5 0.1 collective-permute-start.6
  83.6 1.4 %collective-permute-done.6.refs_2_ = f32[168,256]{1,0:T(8,128)S(1)} collective-permute-done((f32[168,256]{1,0:T(8,128)S(1)}, f32[168,256]{1,0:T(8,128)S(1)}, u32[]{:S(2)}, u32[]{:S(2)}) %collective-permute-start.6) | collective-permute-done | bytes 172064 | tf_op jit(solution)/shard_map/ppermute | solution.py:334
  85.0 0.7 copy-done.3
  85.6 2.3 %unpack.1 = (f32[256,256]{1,0:T(8,128)}, f32[32,256]{1,0:T(8,128)}, f32[32,32]{1,0:T(8,128)}, f32[1,32]{1,0:T(1,128)}, f32[256,256]{1,0:T(8,128)}, /*index=5*/f32[8,128]{1,0:T(8,128)}) custom-call(s32[3]{0:T(128)} %pad_add_fusion.refs_0_, f32[168,256]{1,0:T(8,128)} %copy-done, f32[168,256]{1,0:T(8,128)} %copy-done.3, f32[192,256]{1,0:T(8,128)} %copy-done.1, ...), custom_call_target="tpu_custom_call" | custom-call | tf_op jit(solution)/shard_map/unpack/pallas_call | solution.py:300
  (23 shorter events, 0.1 us)
Async XLA Ops:
  0.6 3.1 %collective-permute-start = (f32[3,8,128]{2,1,0:T(8,128)}, f32[3,8,128]{2,1,0:T(8,128)S(1)}, u32[]{:S(2)}, u32[]{:S(2)}) collective-permute-start(f32[3,8,128]{2,1,0:T(8,128)} %pos_ref.1), channel_id=1, source_target_pairs={{0,1},{1,0},{2,3},{3,2},{4,5},{5,4},{6,7},{7,6},{8,9},{9,8},{10,11... | collective-permute-start | bytes 36872 | tf_op jit(solution)/shard_map/ppermute | solution.py:334
  2.3 43.9 %copy-start.4 = (f32[8,256]{1,0:T(8,128)}, f32[8,256]{1,0:T(8,128)S(1)}, u32[]{:S(2)}) copy-start(f32[8,256]{1,0:T(8,128)S(1)} %convert_reduce_fusion.sum_a_ref) | copy-start | bytes 24580
  2.3 43.9 %collective-permute-start.1 = (f32[8,256]{1,0:T(8,128)S(1)}, f32[8,256]{1,0:T(8,128)S(1)}, u32[]{:S(2)}, u32[]{:S(2)}) collective-permute-start(f32[8,256]{1,0:T(8,128)S(1)} %convert_reduce_fusion.sum_a_ref), channel_id=1, source_target_pairs={{0,1},{1,0},{2,3},{3,2},{4,5},{5,4},{6,7},{7,6},{8,9},{9,8},{10,11... | collective-permute-start | bytes 24584 | tf_op jit(solution)/shard_map/ppermute | solution.py:334
  3.8 0.6 copy-start.5
  46.2 0.6 copy-start.6
  53.3 1.9 %collective-permute-start.2 = (f32[176,256]{1,0:T(8,128)}, f32[176,256]{1,0:T(8,128)S(1)}, u32[]{:S(2)}, u32[]{:S(2)}) collective-permute-start(f32[176,256]{1,0:T(8,128)} %get-tuple-element.30), channel_id=1, source_target_pairs={{0,1},{1,0},{2,3},{3,2},{4,5},{5,4},{6,7},{7,6},{8,9},{9,8},{10,11... | collective-permute-start | bytes 540680 | tf_op jit(solution)/shard_map/ppermute | solution.py:334
  55.8 20.7 %copy-start.2 = (f32[8,256]{1,0:T(8,128)}, f32[8,256]{1,0:T(8,128)S(1)}, u32[]{:S(2)}) copy-start(f32[8,256]{1,0:T(8,128)S(1)} %get-tuple-element.43.col_ref) | copy-start | bytes 24580
  57.5 6.4 %collective-permute-start.3 = (f32[192,256]{1,0:T(8,128)S(1)}, f32[192,256]{1,0:T(8,128)S(1)}, u32[]{:S(2)}, u32[]{:S(2)}) collective-permute-start(f32[192,256]{1,0:T(8,128)S(1)} %pad_maximum_fusion), channel_id=1, source_target_pairs={{0,2},{1,5},{2,0},{3,7},{4,6},{5,1},{6,4},{7,3},{8,10},{9,13},{10,... | collective-permute-start | bytes 589832 | tf_op jit(solution)/shard_map/ppermute | solution.py:364
  64.7 7.7 %collective-permute-start.4 = (f32[216,256]{1,0:T(8,128)S(1)}, f32[216,256]{1,0:T(8,128)S(1)}, u32[]{:S(2)}, u32[]{:S(2)}) collective-permute-start(f32[216,256]{1,0:T(8,128)S(1)} %constant_dynamic-update-slice_fusion), channel_id=1, source_target_pairs={{0,4},{1,9},{2,6},{3,11},{4,0},{5,13},{6,2},{7,15},{8,12},{9,1},{1... | collective-permute-start | bytes 663560 | tf_op jit(solution)/shard_map/ppermute | solution.py:364
  73.1 10.3 %collective-permute-start.5 = (f32[264,256]{1,0:T(8,128)S(1)}, f32[264,256]{1,0:T(8,128)S(1)}, u32[]{:S(2)}, u32[]{:S(2)}) collective-permute-start(f32[264,256]{1,0:T(8,128)S(1)} %get-tuple-element.45), channel_id=1, source_target_pairs={{0,8},{1,3},{2,10},{3,1},{4,12},{5,7},{6,14},{7,5},{8,0},{9,11},{1... | collective-permute-start | bytes 811016 | tf_op jit(solution)/shard_map/ppermute | solution.py:364
  83.5 1.5 %copy-start = (f32[168,256]{1,0:T(8,128)}, f32[168,256]{1,0:T(8,128)S(1)}, u32[]{:S(2)}) copy-start(f32[168,256]{1,0:T(8,128)S(1)} %slice_add_fusion.refs_1_) | copy-start | bytes 516100
  83.5 1.5 %collective-permute-start.6 = (f32[168,256]{1,0:T(8,128)S(1)}, f32[168,256]{1,0:T(8,128)S(1)}, u32[]{:S(2)}, u32[]{:S(2)}) collective-permute-start(f32[168,256]{1,0:T(8,128)S(1)} %slice_add_fusion.refs_1_), channel_id=1, source_target_pairs={{0,1},{1,0},{2,3},{3,2},{4,5},{5,4},{6,7},{7,6},{8,9},{9,8},{10,11... | collective-permute-start | bytes 516104 | tf_op jit(solution)/shard_map/ppermute | solution.py:334
  83.6 1.4 %copy-start.1 = (f32[192,256]{1,0:T(8,128)}, f32[192,256]{1,0:T(8,128)S(1)}, u32[]{:S(2)}) copy-start(f32[192,256]{1,0:T(8,128)S(1)} %slice_dynamic-update-slice_fusion.refs_3_) | copy-start | bytes 589828
  85.0 0.7 copy-start.3

commit v2 on v1

v2 whole, which is shorter than its diff:
```python
import math

import jax
import jax.numpy as jnp
from jax import lax
from jax.experimental import pallas as pl
from jax.experimental.pallas import tpu as pltpu
from jax.sharding import PartitionSpec as P

HIGH = lax.Precision.HIGHEST
f32 = jnp.float32
bf16 = jnp.bfloat16
step_tau = 0.5
VMEM_LIMIT = 56 << 20
ONE, POOL, SMALL = 128, 16, 8
HALF = ONE + POOL + SMALL
SENT = HALF + SMALL
GATH = 24
PARAMS = pltpu.CompilerParams(vmem_limit_bytes=VMEM_LIMIT)
VMEM = pl.BlockSpec(memory_space=pltpu.VMEM)
SMEM = pl.BlockSpec(memory_space=pltpu.SMEM)


def dot(a, b, ca, cb, precision=None):
    return lax.dot_general(
        a, b, (((ca,), (cb,)), ((), ())), preferred_element_type=f32, precision=precision
    )


def split3(x):
    first = x.astype(bf16).astype(f32)
    rest = x - first
    second = rest.astype(bf16).astype(f32)
    return first, second, rest - second


def iota(shape, dim):
    return lax.broadcasted_iota(jnp.int32, shape, dim)


def main_kernel(
    core_ref, own_ref, other_ref, ew_ref, eb_ref, pw_ref, pb_ref, hid_ref, cot_ref,
    sum_a_ref, sum_b_ref, ow_ref, qw_ref, mw_ref, ob_ref,
    updated_ref, grad_ref, keep_ref, send_ref, mean_ref,
    embed_mat, block_mat, a_rows, feat, bias_row, pool_mat, columns,
    pre_a, pre_b, act_a, act_b, in_buf, slope_a, slope_b, sum_buf,
    pooled_all, h_all, g_all, hid_all, cot_all, one_pre, back_all,
):
    s = pl.program_id(0)
    count = own_ref.shape[1]

    def features(slot, at, first, size):
        lane = iota((size, 128), 1)
        square = jnp.ones((size, 128), f32)
        misc = jnp.zeros((size, 128), f32)
        for c in range(3):
            spread = jnp.broadcast_to(
                columns[at, first : first + size, c : c + 1], (size, 128)
            )
            offset = spread - own_ref[c, pl.ds(at, 1), :]
            square = square + offset * offset
            s1, s2, s3 = split3(spread)
            base = 64 + 6 * c
            misc = jnp.where((lane >= base) & (lane < base + 3), s1, misc)
            misc = jnp.where((lane >= base + 3) & (lane < base + 5), s2, misc)
            misc = jnp.where(lane == base + 5, s3, misc)
        radial = jnp.sqrt(square)
        high = radial.astype(bf16).astype(f32)
        low = radial - high
        high_turned = pltpu.roll(high, 64, 1)
        low_turned = pltpu.roll(low, 64, 1)
        left = lane < 64
        rows = slice(first, first + size)
        feat[slot, 0, rows, :128] = jnp.where(left, high, low_turned).astype(bf16)
        feat[slot, 0, rows, 128:] = jnp.where(left, high, misc).astype(bf16)
        feat[slot, 1, rows, :128] = jnp.where(left, high_turned, low).astype(bf16)
        feat[slot, 1, rows, 128:] = jnp.where(left, high_turned, misc).astype(bf16)

    @pl.when(s == 0)
    def _():
        wide = jnp.concatenate([ew_ref[...]] * 8, axis=1)
        w1, w2, w3 = split3(wide)
        row = iota((64, 256), 0)
        lane = iota((64, 256), 1)
        pieces = (w1, w2, w3, w1, w2, w1)
        misc = jnp.zeros((64, 256), f32)
        for c in range(3):
            for p in range(6):
                misc = jnp.where(row == 6 * c + p, -pieces[p][c : c + 1, :], misc)
        misc = misc.astype(bf16)
        for g in range(8):
            hit = row == g * 8 + lane // 32
            first = jnp.where(hit, w1[3:4, :], 0.0).astype(bf16)
            embed_mat[0:64, g * 256 : (g + 1) * 256] = first
            embed_mat[64:128, g * 256 : (g + 1) * 256] = first
            embed_mat[128:192, g * 256 : (g + 1) * 256] = jnp.where(hit, w2[3:4, :], 0.0).astype(bf16)
            embed_mat[192:256, g * 256 : (g + 1) * 256] = misc
        row = iota((256, 256), 0)
        lane = iota((256, 256), 1)
        tiled = jnp.concatenate([pw_ref[...].astype(f32).T] * 8, axis=1)
        tiled = jnp.concatenate([tiled] * 8, axis=0)
        block_mat[...] = jnp.where(row // 32 == lane // 32, tiled, 0.0).astype(bf16)
        pool_mat[...] = jnp.concatenate([qw_ref[...]] * 8, axis=0)
        bias_row[...] = jnp.broadcast_to(jnp.concatenate([pb_ref[...]] * 8, axis=1), (8, 256))
        wide_bias = jnp.concatenate([eb_ref[...]] * 8, axis=1)
        electron = iota((128, 256), 0)
        lane128 = iota((128, 256), 1)
        points = jnp.concatenate(
            [piece for c in range(3) for piece in split3(own_ref[c])], axis=0
        ).astype(bf16)
        for g in range(16):
            pick = jnp.where(electron == g * 8 + lane128 // 32, 1.0, 0.0).astype(bf16)
            spread = dot(points, pick, 1, 0)
            total = jnp.broadcast_to(wide_bias, (count, 256))
            for c in range(3):
                base = 3 * c * count
                point = (
                    spread[base : base + count]
                    + spread[base + count : base + 2 * count]
                    + spread[base + 2 * count : base + 3 * count]
                )
                total = total + point * wide[c : c + 1, :]
            a_rows[:, g * 256 : (g + 1) * 256] = total
        blank = jnp.zeros((5, 256), f32)
        for at in range(count):
            stacked = jnp.concatenate(
                [
                    jnp.concatenate(
                        [own_ref[c, at : at + 1, :], other_ref[c, at : at + 1, :]], axis=1
                    )
                    for c in range(3)
                ]
                + [blank],
                axis=0,
            )
            columns[at] = stacked.T
        features(0, 0, 0, 256)

    @pl.when(s < count)
    def _():
        diagonal = iota((8, 256), 0) == iota((8, 256), 1) // 32
        block = iota((32, 256), 1) // 32
        slot = lax.rem(s, 2)
        later = jnp.minimum(s + 1, count - 1)
        hid = hid_ref[0]
        pre = (pre_a, pre_b)
        acts = (act_a, act_b)
        slopes = (slope_a, slope_b)

        def embed(g):
            half, inner = g // 8, g % 8
            out = dot(feat[slot, half], embed_mat[:, inner * 256 : (inner + 1) * 256], 1, 0)
            pre[g % 2][...] = out + a_rows[pl.ds(s, 1), g * 256 : (g + 1) * 256]
            features(1 - slot, later, g * 16, 16)

        def first_tanh(g):
            out = jnp.tanh(pre[g % 2][...])
            in_buf[g % 4] = out.astype(bf16)
            sum_buf[g % 4] = jnp.sum(out.reshape(32, 8, 256), axis=0)

        def layer(g):
            acts[g % 2][...] = dot(in_buf[g % 4], block_mat[...], 1, 0) + bias_row[0:1, :]

        def second_tanh(g):
            act = jnp.tanh(acts[g % 2][...])
            total = sum_buf[g % 4] + jnp.sum(act.reshape(32, 8, 256), axis=0)
            mean = jnp.sum(total, axis=0, keepdims=True) * (1.0 / 256)
            slope = 1.0 - act * act
            h_all[s, g : g + 1, :] = jnp.sum(slope, axis=0, keepdims=True)
            pooled_all[s, g * 8 : (g + 1) * 8, :] = jnp.where(diagonal, mean, 0.0)
            slopes[g % 2][...] = slope.astype(bf16)

        def outer(g):
            product = dot(in_buf[g % 4], slopes[g % 2][...], 0, 0)
            picked = product[0:32]
            for q in range(1, 8):
                picked = jnp.where(block == q, product[q * 32 : (q + 1) * 32], picked)
            g_all[s, g * 32 : (g + 1) * 32, :] = picked

        for step in range(16 + 4):
            for lag, stage in enumerate((embed, first_tanh, layer, second_tanh, outer)):
                if 0 <= step - lag < 16:
                    stage(step - lag)
        hid_all[s] = hid
        cot_all[s] = cot_ref[0]
        one_pre[s] = dot(hid, ow_ref[...], 1, 0)

    @pl.when(s == count)
    def _():
        mean_rows = ((sum_a_ref[...] + sum_b_ref[...]) * (1.0 / 256)).astype(bf16)
        mean_ref[...] = mean_rows
        per_slice = dot(mean_rows, mw_ref[...], 1, 0) + ob_ref[...]
        own_lanes = iota((128, 256), 0) % 8 == iota((128, 256), 1) // 32
        one_total = jnp.zeros((256, 256), f32)
        pool_total = jnp.zeros((256, 256), f32)
        pair_total = jnp.zeros((32, 256), f32)
        bias_total = jnp.zeros((16, 256), f32)
        parts = []
        for step in range(count + 2):
            if step < count:
                at = step
                rows = slice(at * 128, (at + 1) * 128)
                pre = one_pre[at] + dot(pooled_all[at].astype(bf16), pool_mat[...], 1, 0)
                act = jnp.tanh(pre + per_slice[at : at + 1, :])
                updated_ref[rows, :] = (act + hid_all[at].astype(f32)).astype(bf16)
                grad = (cot_all[at].astype(f32) * (1.0 - act * act)).astype(bf16)
                grad_ref[rows, :] = grad
                parts.append(jnp.sum(grad.astype(f32), axis=0, keepdims=True))
            if 0 <= step - 1 < count:
                at = step - 1
                grad = grad_ref[at * 128 : (at + 1) * 128, :]
                back = jnp.where(own_lanes, dot(grad, pool_mat[...], 1, 1), 0.0)
                back_all[at] = jnp.sum(back.reshape(16, 8, 256), axis=1)
                one_total = one_total + dot(hid_all[at], grad, 0, 0)
                pool_total = pool_total + dot(pooled_all[at].astype(bf16), grad, 0, 0)
            if 0 <= step - 2 < count:
                at = step - 2
                bias_total = bias_total + back_all[at] * h_all[at]
                for g in range(16):
                    pair_total = pair_total + g_all[at, g * 32 : (g + 1) * 32, :] * back_all[at, g : g + 1, :]
        fold = jnp.where(iota((256, 256), 0) % 32 == iota((256, 256), 1) % 32, 1.0, 0.0)
        pool = pool_total[0:32]
        for q in range(1, 8):
            pool = pool + pool_total[q * 32 : (q + 1) * 32]
        bias_one = jnp.broadcast_to(jnp.sum(bias_total, axis=0, keepdims=True), (8, 256))
        folded = dot(jnp.concatenate([pair_total, bias_one], axis=0), fold, 1, 0, HIGH)
        picked = jnp.where(iota((32, 256), 0) % 8 == iota((32, 256), 1) // 32, folded[0:32], 0.0)
        packed = jnp.sum(picked.reshape(4, 8, 256), axis=1)
        small = jnp.concatenate([packed, folded[32:36]], axis=0)
        core = core_ref[0]

        @pl.when(core == 0)
        def _():
            keep_ref[0:ONE, :] = one_total[0:ONE]
            send_ref[0:ONE, :] = one_total[ONE:]
            keep_ref[ONE : ONE + POOL, :] = pool[0:POOL]
            send_ref[ONE : ONE + POOL, :] = pool[POOL:]

        @pl.when(core == 1)
        def _():
            send_ref[0:ONE, :] = one_total[0:ONE]
            keep_ref[0:ONE, :] = one_total[ONE:]
            send_ref[ONE : ONE + POOL, :] = pool[0:POOL]
            keep_ref[ONE : ONE + POOL, :] = pool[POOL:]

        keep_ref[ONE + POOL : HALF, :] = small
        send_ref[ONE + POOL : HALF, :] = small
        sums = jnp.concatenate(parts, axis=0)
        keep_ref[HALF:, :] = sums
        send_ref[HALF:, :] = sums


def main_call(core, own, other, ew, eb, pw, pb, hid, cot, sum_a, sum_b, ow, qw, mw, ob):
    count, rows, width = hid.shape
    args = (
        core, own, other, ew.T, eb.reshape(1, 32), pw, pb.reshape(1, 32), hid, cot,
        sum_a, sum_b, ow, qw, mw, ob.reshape(1, width),
    )
    whole = [pl.BlockSpec(a.shape, lambda s, n=a.ndim: (0,) * n) for a in args]
    by_slice = pl.BlockSpec((1, rows, width), lambda s: (jnp.minimum(s, count - 1), 0, 0))
    in_specs = [SMEM] + whole[1:7] + [by_slice, by_slice] + whole[9:]
    shapes = [
        jax.ShapeDtypeStruct((count * rows, width), bf16),
        jax.ShapeDtypeStruct((count * rows, width), bf16),
        jax.ShapeDtypeStruct((HALF + count, width), f32),
        jax.ShapeDtypeStruct((HALF + count, width), f32),
        jax.ShapeDtypeStruct((count, width), bf16),
    ]
    return pl.pallas_call(
        main_kernel,
        grid=(count + 1,),
        in_specs=in_specs,
        out_specs=[pl.BlockSpec(a.shape, lambda s: (0, 0)) for a in shapes],
        out_shape=shapes,
        scratch_shapes=[
            pltpu.VMEM((256, 2048), bf16),
            pltpu.VMEM((256, 256), bf16),
            pltpu.VMEM((count, 4096), f32),
            pltpu.VMEM((2, 2, 256, 256), bf16),
            pltpu.VMEM((8, 256), f32),
            pltpu.VMEM((256, 256), bf16),
            pltpu.VMEM((count, 256, 8), f32),
            pltpu.VMEM((256, 256), f32),
            pltpu.VMEM((256, 256), f32),
            pltpu.VMEM((256, 256), f32),
            pltpu.VMEM((256, 256), f32),
            pltpu.VMEM((4, 256, 256), bf16),
            pltpu.VMEM((256, 256), bf16),
            pltpu.VMEM((256, 256), bf16),
            pltpu.VMEM((4, 8, 256), f32),
            pltpu.VMEM((count, 128, 256), f32),
            pltpu.VMEM((count, 16, 256), f32),
            pltpu.VMEM((count, 512, 256), f32),
            pltpu.VMEM((count, 128, 256), bf16),
            pltpu.VMEM((count, 128, 256), bf16),
            pltpu.VMEM((count, 128, 256), f32),
            pltpu.VMEM((count, 16, 256), f32),
        ],
        compiler_params=PARAMS,
        name="pair_and_one",
    )(*args)


def pack(total, gath, out_ref):
    out_ref[0:HALF, :] = total.astype(bf16)
    small = total[ONE + POOL :]
    out_ref[HALF:SENT, :] = (small - small.astype(bf16).astype(f32)).astype(bf16)
    at = SENT
    for piece in gath:
        out_ref[at : at + piece.shape[0], :] = piece
        at += piece.shape[0]


def first_kernel(keep_ref, came_ref, mean_ref, pos_ref, out_ref, col_ref):
    both = keep_ref[...] + came_ref[...]
    col = both[HALF:]
    col_ref[...] = col
    p1, p2, p3 = split3(pos_ref[:, 0, :])
    blank = jnp.zeros((2, 256), f32)
    border = jnp.concatenate(
        [
            jnp.concatenate([p1, p2], axis=1),
            jnp.concatenate([p3, jnp.zeros_like(p3)], axis=1),
            blank,
        ],
        axis=0,
    )
    gath = jnp.concatenate([mean_ref[...].astype(f32), col, border], axis=0).astype(bf16)
    pack(both[0:HALF], [gath], out_ref)


def first_call(keep, came, mean_rows, pos):
    count = mean_rows.shape[0]
    return pl.pallas_call(
        first_kernel,
        in_specs=[VMEM] * 4,
        out_specs=[VMEM] * 2,
        out_shape=[
            jax.ShapeDtypeStruct((SENT + 2 * count + 8, 256), bf16),
            jax.ShapeDtypeStruct((count, 256), f32),
        ],
        compiler_params=PARAMS,
        name="first_mix",
    )(keep, came, mean_rows, pos)


def add_up(own_ref, came_ref):
    total = own_ref[0:HALF, :].astype(f32) + came_ref[0:HALF, :].astype(f32)
    rest = own_ref[HALF:SENT, :].astype(f32) + came_ref[HALF:SENT, :].astype(f32)
    return jnp.concatenate([total[0 : ONE + POOL], total[ONE + POOL :] + rest], axis=0)


def mix_kernel(own_ref, came_ref, out_ref):
    pack(add_up(own_ref, came_ref), [own_ref[SENT:, :], came_ref[SENT:, :]], out_ref)


def mix_call(own, came):
    rows = SENT + 2 * (own.shape[0] - SENT)
    return pl.pallas_call(
        mix_kernel,
        in_specs=[VMEM] * 2,
        out_specs=VMEM,
        out_shape=jax.ShapeDtypeStruct((rows, 256), bf16),
        compiler_params=PARAMS,
        name="mix",
    )(own, came)


def last_kernel(own_ref, came_ref, out_ref):
    out_ref[...] = add_up(own_ref, came_ref)


def last_call(own, came):
    return pl.pallas_call(
        last_kernel,
        in_specs=[VMEM] * 2,
        out_specs=VMEM,
        out_shape=jax.ShapeDtypeStruct((HALF, 256), f32),
        compiler_params=PARAMS,
        name="last_mix",
    )(own, came)


def back_kernel(
    cot_ref, pre_ref, upd_ref, col_ref, pos_ref, ow_ref, mw_ref, dw_ref,
    grad_ref, link_ref, last_ref,
):
    count = col_ref.shape[0]
    back = dot(col_ref[...], mw_ref[...].astype(f32), 1, 1, HIGH) * (1.0 / 256)
    drifts = []
    for s in range(count):
        at = slice(s * 128, (s + 1) * 128)
        grad = cot_ref[at, :].astype(f32) + dot(pre_ref[at, :], ow_ref[...], 1, 1)
        grad_ref[at, :] = (grad + back[s : s + 1, :]).astype(bf16)
        drifts.append(dot(dw_ref[...], upd_ref[at, :], 1, 1))
    for s in range(count):
        here = [-pos_ref[c, s : s + 1, :] - step_tau * drifts[s][c : c + 1, :] for c in range(3)]
        if s < count - 1:
            jumps = [here[c] + pos_ref[c, s + 1 : s + 2, :] for c in range(3)]
            total = jumps[0] * jumps[0] + jumps[1] * jumps[1] + jumps[2] * jumps[2]
            link_ref[s : s + 1, :] = total * (1.0 / (12.0 * step_tau))
        else:
            link_ref[s : s + 1, :] = jnp.zeros((1, 128), f32)
            last_ref[...] = jnp.concatenate(here + [jnp.zeros((5, 128), f32)], axis=0)


def back_call(cot, pre, updated, col, pos, ow, mw, dw):
    args = (cot, pre, updated, col, pos, ow, mw, dw)
    return pl.pallas_call(
        back_kernel,
        in_specs=[VMEM] * len(args),
        out_specs=[VMEM] * 3,
        out_shape=[
            jax.ShapeDtypeStruct(cot.shape, bf16),
            jax.ShapeDtypeStruct((col.shape[0], 128), f32),
            jax.ShapeDtypeStruct((8, 128), f32),
        ],
        compiler_params=PARAMS,
        name="hidden_back",
    )(*args)


def mean_kernel(
    info_ref, own_ref, came_ref, link_ref, last_ref,
    mean_ref, out_link_ref,
    mean_all, col_all, border, *, scale, count,
):
    stride = 2 * count + 8
    half = (own_ref.shape[0] - SENT) // stride
    for d in range(2 * half):
        ref = own_ref if d < half else came_ref
        base = SENT + (d % half) * stride
        block = ref[base : base + stride, :].astype(f32)
        at = pl.ds(pl.multiple_of(info_ref[2 + d] * count, 8), count)
        mean_all[at, :] = block[0:count]
        col_all[at, :] = block[count : 2 * count]
        border[pl.ds(pl.multiple_of(info_ref[2 + d] * 8, 8), 8), :] = block[2 * count :]
    mean_ref[...] = scale * dot(mean_all[...].astype(bf16), col_all[...].astype(bf16), 0, 0)
    out_link_ref[...] = link_ref[...]
    pieces = border[pl.ds(pl.multiple_of(info_ref[0] * 8, 8), 8), :]
    point = pieces[0:3, 0:128] + pieces[0:3, 128:] + pieces[3:6, 0:128]
    jump = point + last_ref[0:3, :]
    total = jnp.sum(jump * jump, axis=0, keepdims=True) * (1.0 / (12.0 * step_tau))
    out_link_ref[count - 1 : count, :] = jnp.where(info_ref[1] == 1, 0.0, total)


def mean_call(info, own, came, link, last, scale, count):
    args = (info, own, came, link, last)
    devices = info.shape[0] - 2

    def body(*refs):
        mean_kernel(*refs, scale=scale, count=count)

    return pl.pallas_call(
        body,
        in_specs=[SMEM] + [VMEM] * 4,
        out_specs=[VMEM] * 2,
        out_shape=[
            jax.ShapeDtypeStruct((256, 256), f32),
            jax.ShapeDtypeStruct((count, 128), f32),
        ],
        scratch_shapes=[
            pltpu.VMEM((devices * count, 256), f32),
            pltpu.VMEM((devices * count, 256), f32),
            pltpu.VMEM((devices * 8, 256), f32),
        ],
        compiler_params=PARAMS,
        name="mean_and_link",
    )(*args)


def end_kernel(core_ref, own_ref, came_ref, one_ref, pool_ref, pair_ref, bias_ref, *, scale):
    def write(low_ref, high_ref):
        one_ref[0:ONE, :] = scale * low_ref[0:ONE, :]
        one_ref[ONE:, :] = scale * high_ref[0:ONE, :]
        pool_ref[0:POOL, :] = scale * low_ref[ONE : ONE + POOL, :]
        pool_ref[POOL:, :] = scale * high_ref[ONE : ONE + POOL, :]

        small = low_ref[ONE + POOL : HALF, :]
        rows = jnp.concatenate(
            [jnp.broadcast_to(small[r : r + 1], (8, 256)) for r in range(4)], axis=0
        )
        rows = jnp.where(iota((32, 256), 0) % 8 == iota((32, 256), 1) // 32, rows, 0.0)
        total = rows[:, 0:128] + rows[:, 128:]
        total = total + pltpu.roll(total, 64, 1)
        total = total + pltpu.roll(total, 32, 1)
        pair_ref[...] = (scale / 256.0) * total[:, 0:32].T
        bias_ref[...] = (scale / 256.0) * small[4:5, 0:32]

    core = core_ref[0]
    pl.when(core == 0)(lambda: write(own_ref, came_ref))
    pl.when(core == 1)(lambda: write(came_ref, own_ref))


def end_call(core, own, came, scale):
    def body(*refs):
        end_kernel(*refs, scale=scale)

    return pl.pallas_call(
        body,
        in_specs=[SMEM, VMEM, VMEM],
        out_specs=[VMEM] * 4,
        out_shape=[
            jax.ShapeDtypeStruct((256, 256), f32),
            jax.ShapeDtypeStruct((32, 256), f32),
            jax.ShapeDtypeStruct((32, 32), f32),
            jax.ShapeDtypeStruct((1, 32), f32),
        ],
        compiler_params=PARAMS,
        name="unpack",
    )(core, own, came)


def local(
    positions, hidden, cotangent, embed_weight, embed_bias, pair_weight, pair_bias,
    one_weight, pool_weight, mean_weight, one_bias, drift_weight,
):
    count, own_count, width = hidden.shape
    slices = lax.axis_size("slices")
    bits = slices.bit_length() - 1
    scale = 1.0 / math.sqrt(count * slices * own_count * lax.axis_size("ering"))
    core = lax.axis_index("ering").astype(jnp.int32)
    place = lax.axis_index("slices").astype(jnp.int32)

    def swap(array):
        return lax.ppermute(array, "ering", [(0, 1), (1, 0)])

    orders = [[(t + e) % bits for t in range(bits)] for e in range(2)]
    masks = [
        [sum(((d >> t) & 1) << orders[e][t] for t in range(bits)) for d in range(slices)]
        for e in range(2)
    ]
    owners = place ^ jnp.where(core == 0, jnp.array(masks[0]), jnp.array(masks[1]))
    info = jnp.concatenate(
        [
            jnp.minimum(place + 1, slices - 1).reshape(1),
            (place == slices - 1).astype(jnp.int32).reshape(1),
            owners.astype(jnp.int32),
        ]
    )
    core = core.reshape(1)

    other_pos = swap(positions)
    part_sum = jnp.sum(hidden.astype(f32), axis=1)
    other_sum = swap(part_sum)
    updated, pre, keep, send, mean_rows = main_call(
        core, positions, other_pos, embed_weight, embed_bias, pair_weight, pair_bias, hidden,
        cotangent, part_sum, other_sum, one_weight, pool_weight, mean_weight, one_bias,
    )
    state, col_total = first_call(keep, swap(send), mean_rows, positions)
    hidden_grad, link, last = back_call(
        cotangent.reshape(pre.shape), pre, updated, col_total, positions, one_weight,
        mean_weight, drift_weight,
    )
    for t in range(bits):
        pairs = [
            (s * 2 + e, (s ^ (1 << orders[e][t])) * 2 + e) for s in range(slices) for e in range(2)
        ]
        came = lax.ppermute(state, ("slices", "ering"), pairs)
        if t < bits - 1:
            state = mix_call(state, came)
    total = last_call(state, came)
    other_total = swap(total)
    mean_grad, link_terms = mean_call(info, state, came, link, last, scale, count)
    one_grad, pool_grad, pair_grad, bias_grad = end_call(core, total, other_total, scale)
    return (
        updated.reshape(hidden.shape),
        hidden_grad.reshape(hidden.shape),
        link_terms,
        pair_grad,
        bias_grad.reshape(-1),
        one_grad,
        pool_grad,
        mean_grad,
    )


def solution(mesh):
    in_specs = (
        P(None, ("groups", "slices"), "ering"),
        P(("groups", "slices"), "ering", None),
        P(("groups", "slices"), "ering", None),
    ) + (P(),) * 9
    out_specs = (
        P(("groups", "slices"), "ering", None),
        P(("groups", "slices"), "ering", None),
        P(("groups", "slices"), "ering"),
        P("groups", None),
        P("groups"),
        P("groups", None),
        P("groups", None),
        P("groups", None),
    )
    return jax.shard_map(local, mesh=mesh, in_specs=in_specs, out_specs=out_specs, check_vma=False)
```

time: 88.5 us -> 68.4 us (0.77)
  Pallas kernels: 53.6 us -> 39.4 us
  other arithmetic: 4.22 us -> 1.74 us
  local copies, waits for them, and re-layouts: 6.07 us -> 3.88 us
  starting transfers between devices: 8.94 us -> 7.92 us
    pallas_call x4 -> x8, Pallas kernels: 53.6 us -> 39.4 us  [the longest x1 26 us: main_call(): pl.pallas_call(main_kernel, grid=(count + 1,), in_specs=in_specs, out_spe...]
    unnamed x25 -> x18, local copies, waits for them, and re-layouts: 5.34 us -> 3.88 us
    ppermute x4, waiting for transfers between devices: 1.37 us -> 2.55 us  [swap(): return lax.ppermute(array, 'ering', [(0, 1), (1, 0)])]
    ppermute x3, waiting for transfers between devices: 13 us -> 11.8 us  [local(): came = lax.ppermute(state, ('slices', 'ering'), pairs)]
    add x2 -> x0, other arithmetic: 1.01 us -> none  [the longest x1 0.94 us: local(): total = keep + came[:HALF]]
  transfers between devices with their start and end apart: 7 -> 7, of which waited for: 4 -> 5; matrix products, arithmetic and copies ran while one was open for 5% -> 3% of each run, Pallas kernels for 51% -> 7%
where the time goes in v2:
time: 68.4 us; the launch traced here: 68 us
  Pallas kernels  39.4 us (58%)
  waiting for transfers between devices  14.4 us (21%)
  starting transfers between devices  7.92 us (12%)
  local copies, waits for them, and re-layouts  3.88 us (6%)
  other arithmetic  1.74 us (3%)
    pallas_call x1, Pallas kernels, main_call(): pl.pallas_call(main_kernel, grid=(count + 1,), in_specs=in_specs, out_spe...  26 us
    ppermute x3, waiting for transfers between devices, local(): came = lax.ppermute(state, ('slices', 'ering'), pairs)  11.8 us
    ppermute x3, starting transfers between devices, local(): came = lax.ppermute(state, ('slices', 'ering'), pairs)  7.04 us
    unnamed x18, local copies, waits for them, and re-layouts  3.88 us
    pallas_call x2, Pallas kernels, mix_call(): pl.pallas_call(mix_kernel, in_specs=[VMEM] * 2, out_specs=VMEM, out_shape...  3.23 us
    pallas_call x1, Pallas kernels, back_call(): pl.pallas_call(back_kernel, in_specs=[VMEM] * len(args), out_specs=[VMEM]...  3.05 us
    ppermute x4, waiting for transfers between devices, swap(): return lax.ppermute(array, 'ering', [(0, 1), (1, 0)])  2.55 us
    pallas_call x1, Pallas kernels, end_call(): pl.pallas_call(body, in_specs=[SMEM, VMEM, VMEM], out_specs=[VMEM] * 4, o...  1.92 us
  transfers between devices with their start and end apart: 7, of which 5 were waited for; matrix products, arithmetic and copies ran while one was open for 3% of the time, Pallas kernels for 7%

profile of v2, /device:TPU:0, one launch (start us, length us, event | category | flops | bytes accessed | tf_op | source)
XLA Modules:
  0.0 68.0 jit_solution(13964104763302837946)
XLA Ops:
  0.6 0.5 collective-permute-start
  1.1 1.1 %convert_reduce_fusion.sum_a_ref = f32[8,256]{1,0:T(8,128)S(1)} fusion(bf16[8,128,256]{2,1,0:T(8,128)(2,1)} %hid_ref.1), kind=kLoop, calls=%fused_computation | loop fusion | flops 522240 | bytes 532480 | tf_op jit(solution)/shard_map/reduce_sum | solution.py:544
  2.3 0.0 copy-start.5
  2.3 0.1 collective-permute-start.1
  2.4 1.1 %collective-permute-done.1.sum_b_ref = f32[8,256]{1,0:T(8,128)S(1)} collective-permute-done((f32[8,256]{1,0:T(8,128)S(1)}, f32[8,256]{1,0:T(8,128)S(1)}, u32[]{:S(2)}, u32[]{:S(2)}) %collective-permute-start.1) | collective-permute-done | bytes 8224 | tf_op jit(solution)/shard_map/ppermute | solution.py:526
  3.5 0.0 collective-permute-done.other_ref
  3.5 0.6 copy-done.7
  4.1 0.0 copy-done.6
  4.1 26.0 %pair_and_one.1 = (bf16[1024,256]{1,0:T(8,128)(2,1)}, bf16[1024,256]{1,0:T(8,128)(2,1)}, f32[160,256]{1,0:T(8,128)}, f32[160,256]{1,0:T(8,128)}, bf16[8,256]{1,0:T(8,128)(2,1)}) custom-call(s32[1]{0:T(128)} %bitcast.core_ref.refs_0_, f32[3,8,128]{2,1,0:T(8,128)} %pos_ref.3, f32[3,8,128]{2,1,0:T(8,128)} %copy-done.6, f32[4,32]{1,0:T(4,128)} %bitcast.13, ...), custom_call_target="tpu_custom_call" | custom-call | tf_op jit(solution)/shard_map/pair_and_one/pallas_call | solution.py:269
  30.1 0.2 collective-permute-start.2
  30.4 1.4 %collective-permute-done.2.came_ref = f32[160,256]{1,0:T(8,128)S(1)} collective-permute-done((f32[160,256]{1,0:T(8,128)}, f32[160,256]{1,0:T(8,128)S(1)}, u32[]{:S(2)}, u32[]{:S(2)}) %collective-permute-start.2) | collective-permute-done | bytes 163872 | tf_op jit(solution)/shard_map/ppermute | solution.py:526
  31.8 0.7 copy-done.1
  32.4 1.7 %first_mix.1 = (bf16[184,256]{1,0:T(8,128)(2,1)}, f32[8,256]{1,0:T(8,128)}) custom-call(f32[160,256]{1,0:T(8,128)} %get-tuple-element.26.keep_ref, f32[160,256]{1,0:T(8,128)} %copy-done.1, bf16[8,256]{1,0:T(8,128)(2,1)} %get-tuple-element.28.mean_ref, f32[3,8,128]{2,1,0:T(8,128)} %pos_ref.3), custom_call_target="tpu_custom_call" | custom-call | tf_op jit(solution)/shard_map/first_mix/pallas_call | solution.py:334
  34.1 2.7 %collective-permute-start.3 = (bf16[184,256]{1,0:T(8,128)(2,1)}, bf16[184,256]{1,0:T(8,128)(2,1)S(1)}, u32[]{:S(2)}, u32[]{:S(2)}) collective-permute-start(bf16[184,256]{1,0:T(8,128)(2,1)} %get-tuple-element.31.own_ref), channel_id=1, source_target_pairs={{0,2},{1,5},{2,0},{3,7},{4,6},{5,1},{6,4},{7,3},{8,10},{9,13},{10,... | collective-permute-start | bytes 282632 | tf_op jit(solution)/shard_map/ppermute | solution.py:559
  36.8 2.8 %collective-permute-done.3.came_ref = bf16[184,256]{1,0:T(8,128)(2,1)S(1)} collective-permute-done((bf16[184,256]{1,0:T(8,128)(2,1)}, bf16[184,256]{1,0:T(8,128)(2,1)S(1)}, u32[]{:S(2)}, u32[]{:S(2)}) %collective-permute-start.3) | collective-permute-done | bytes 94240 | tf_op jit(solution)/shard_map/ppermute | solution.py:559
  39.5 0.6 copy-done.4
  40.2 1.6 %mix.2.own_ref = bf16[208,256]{1,0:T(8,128)(2,1)} custom-call(bf16[184,256]{1,0:T(8,128)(2,1)} %get-tuple-element.31.own_ref, bf16[184,256]{1,0:T(8,128)(2,1)} %copy-done.4), custom_call_target="tpu_custom_call" | custom-call | tf_op jit(solution)/shard_map/mix/pallas_call | solution.py:359
  41.8 2.1 %collective-permute-start.4 = (bf16[208,256]{1,0:T(8,128)(2,1)}, bf16[208,256]{1,0:T(8,128)(2,1)S(1)}, u32[]{:S(2)}, u32[]{:S(2)}) collective-permute-start(bf16[208,256]{1,0:T(8,128)(2,1)} %mix.2.own_ref), channel_id=1, source_target_pairs={{0,4},{1,9},{2,6},{3,11},{4,0},{5,13},{6,2},{7,15},{8,12},{9,1},{1... | collective-permute-start | bytes 319496 | tf_op jit(solution)/shard_map/ppermute | solution.py:559
  43.9 3.9 %collective-permute-done.4.came_ref = bf16[208,256]{1,0:T(8,128)(2,1)S(1)} collective-permute-done((bf16[208,256]{1,0:T(8,128)(2,1)}, bf16[208,256]{1,0:T(8,128)(2,1)S(1)}, u32[]{:S(2)}, u32[]{:S(2)}) %collective-permute-start.4) | collective-permute-done | bytes 106528 | tf_op jit(solution)/shard_map/ppermute | solution.py:559
  47.7 0.6 copy-done.3
  48.4 1.6 %mix.3.refs_1_.own_ref = bf16[256,256]{1,0:T(8,128)(2,1)} custom-call(bf16[208,256]{1,0:T(8,128)(2,1)} %mix.2.own_ref, bf16[208,256]{1,0:T(8,128)(2,1)} %copy-done.3), custom_call_target="tpu_custom_call" | custom-call | tf_op jit(solution)/shard_map/mix/pallas_call | solution.py:359
  50.0 2.3 %collective-permute-start.5 = (bf16[256,256]{1,0:T(8,128)(2,1)}, bf16[256,256]{1,0:T(8,128)(2,1)S(1)}, u32[]{:S(2)}, u32[]{:S(2)}) collective-permute-start(bf16[256,256]{1,0:T(8,128)(2,1)} %mix.3.refs_1_.own_ref), channel_id=1, source_target_pairs={{0,8},{1,3},{2,10},{3,1},{4,12},{5,7},{6,14},{7,5},{8,0},{9,11},{1... | collective-permute-start | bytes 393224 | tf_op jit(solution)/shard_map/ppermute | solution.py:559
  52.3 5.2 %collective-permute-done.5.refs_2_.came_ref = bf16[256,256]{1,0:T(8,128)(2,1)S(1)} collective-permute-done((bf16[256,256]{1,0:T(8,128)(2,1)}, bf16[256,256]{1,0:T(8,128)(2,1)S(1)}, u32[]{:S(2)}, u32[]{:S(2)}) %collective-permute-start.5) | collective-permute-done | bytes 131104 | tf_op jit(solution)/shard_map/ppermute | solution.py:559
  57.5 0.7 copy-done
  58.2 1.6 %last_mix.1.refs_1_ = f32[152,256]{1,0:T(8,128)} custom-call(bf16[256,256]{1,0:T(8,128)(2,1)} %mix.3.refs_1_.own_ref, bf16[256,256]{1,0:T(8,128)(2,1)} %copy-done), custom_call_target="tpu_custom_call" | custom-call | tf_op jit(solution)/shard_map/last_mix/pallas_call | solution.py:374
  59.8 0.0 collective-permute-start.6
  59.8 0.6 pad_add_fusion.refs_0_
  60.4 3.1 %hidden_back.1 = (bf16[1024,256]{1,0:T(8,128)(2,1)}, f32[8,128]{1,0:T(8,128)}, f32[8,128]{1,0:T(8,128)}) custom-call(bf16[1024,256]{1,0:T(8,128)(2,1)} %bitcast.11, bf16[1024,256]{1,0:T(8,128)(2,1)} %get-tuple-element.25.pre_ref, bf16[1024,256]{1,0:T(8,128)(2,1)} %get-tuple-element.24.upd_ref, f32[8,256]{1,0:T(8,128)} %get-tuple-element.29.col_ref, ...), custom_call_target="tpu_custom_call" | custom-call | tf_op jit(solution)/shard_map/hidden_back/pallas_call | solution.py:409
  63.5 1.9 %mean_and_link.1 = (f32[256,256]{1,0:T(8,128)}, f32[8,128]{1,0:T(8,128)}) custom-call(s32[10]{0:T(128)} %pad_add_fusion.refs_0_, bf16[256,256]{1,0:T(8,128)(2,1)} %mix.3.refs_1_.own_ref, bf16[256,256]{1,0:T(8,128)(2,1)} %copy-done, f32[8,128]{1,0:T(8,128)} %get-tuple-element.32.refs_3_, f32[8,128]{1,0:T(8,128)} %get-tuple-element.33.refs_4_), custom_call_target="tpu_custom_call" | custom-call | tf_op jit(solution)/shard_map/mean_and_link/pallas_call | solution.py:454
  65.4 0.0 collective-permute-done.6.refs_2_
  65.4 0.7 copy-done.2
  66.1 1.9 %unpack.1 = (f32[256,256]{1,0:T(8,128)}, f32[32,256]{1,0:T(8,128)}, f32[32,32]{1,0:T(8,128)}, f32[1,32]{1,0:T(1,128)}) custom-call(s32[1]{0:T(128)} %bitcast.core_ref.refs_0_, f32[152,256]{1,0:T(8,128)} %last_mix.1.refs_1_, f32[152,256]{1,0:T(8,128)} %copy-done.2), custom_call_target="tpu_custom_call" | custom-call | tf_op jit(solution)/shard_map/unpack/pallas_call | solution.py:499
  (11 shorter events, 0.0 us)
Async XLA Ops:
  0.6 2.9 %collective-permute-start = (f32[3,8,128]{2,1,0:T(8,128)}, f32[3,8,128]{2,1,0:T(8,128)S(1)}, u32[]{:S(2)}, u32[]{:S(2)}) collective-permute-start(f32[3,8,128]{2,1,0:T(8,128)} %pos_ref.3), channel_id=1, source_target_pairs={{0,1},{1,0},{2,3},{3,2},{4,5},{5,4},{6,7},{7,6},{8,9},{9,8},{10,11... | collective-permute-start | bytes 36872 | tf_op jit(solution)/shard_map/ppermute | solution.py:526
  2.3 1.3 %copy-start.5 = (f32[8,256]{1,0:T(8,128)}, f32[8,256]{1,0:T(8,128)S(1)}, u32[]{:S(2)}) copy-start(f32[8,256]{1,0:T(8,128)S(1)} %convert_reduce_fusion.sum_a_ref) | copy-start | bytes 24580
  2.3 1.2 %collective-permute-start.1 = (f32[8,256]{1,0:T(8,128)S(1)}, f32[8,256]{1,0:T(8,128)S(1)}, u32[]{:S(2)}, u32[]{:S(2)}) collective-permute-start(f32[8,256]{1,0:T(8,128)S(1)} %convert_reduce_fusion.sum_a_ref), channel_id=1, source_target_pairs={{0,1},{1,0},{2,3},{3,2},{4,5},{5,4},{6,7},{7,6},{8,9},{9,8},{10,11... | collective-permute-start | bytes 24584 | tf_op jit(solution)/shard_map/ppermute | solution.py:526
  3.5 0.6 copy-start.7
  3.5 0.6 copy-start.6
  30.1 1.7 %collective-permute-start.2 = (f32[160,256]{1,0:T(8,128)}, f32[160,256]{1,0:T(8,128)S(1)}, u32[]{:S(2)}, u32[]{:S(2)}) collective-permute-start(f32[160,256]{1,0:T(8,128)} %get-tuple-element.27), channel_id=1, source_target_pairs={{0,1},{1,0},{2,3},{3,2},{4,5},{5,4},{6,7},{7,6},{8,9},{9,8},{10,11... | collective-permute-start | bytes 491528 | tf_op jit(solution)/shard_map/ppermute | solution.py:526
  31.8 0.7 copy-start.1
  34.1 5.4 %collective-permute-start.3 = (bf16[184,256]{1,0:T(8,128)(2,1)}, bf16[184,256]{1,0:T(8,128)(2,1)S(1)}, u32[]{:S(2)}, u32[]{:S(2)}) collective-permute-start(bf16[184,256]{1,0:T(8,128)(2,1)} %get-tuple-element.31.own_ref), channel_id=1, source_target_pairs={{0,2},{1,5},{2,0},{3,7},{4,6},{5,1},{6,4},{7,3},{8,10},{9,13},{10,... | collective-permute-start | bytes 282632 | tf_op jit(solution)/shard_map/ppermute | solution.py:559
  39.5 0.6 copy-start.4
  41.8 6.0 %collective-permute-start.4 = (bf16[208,256]{1,0:T(8,128)(2,1)}, bf16[208,256]{1,0:T(8,128)(2,1)S(1)}, u32[]{:S(2)}, u32[]{:S(2)}) collective-permute-start(bf16[208,256]{1,0:T(8,128)(2,1)} %mix.2.own_ref), channel_id=1, source_target_pairs={{0,4},{1,9},{2,6},{3,11},{4,0},{5,13},{6,2},{7,15},{8,12},{9,1},{1... | collective-permute-start | bytes 319496 | tf_op jit(solution)/shard_map/ppermute | solution.py:559
  47.7 0.6 copy-start.3
  50.0 7.5 %collective-permute-start.5 = (bf16[256,256]{1,0:T(8,128)(2,1)}, bf16[256,256]{1,0:T(8,128)(2,1)S(1)}, u32[]{:S(2)}, u32[]{:S(2)}) collective-permute-start(bf16[256,256]{1,0:T(8,128)(2,1)} %mix.3.refs_1_.own_ref), channel_id=1, source_target_pairs={{0,8},{1,3},{2,10},{3,1},{4,12},{5,7},{6,14},{7,5},{8,0},{9,11},{1... | collective-permute-start | bytes 393224 | tf_op jit(solution)/shard_map/ppermute | solution.py:559
  52.3 7.5 %copy-start.8 = (s32[8]{0:T(128)S(1)}, s32[8]{0:T(128)}, u32[]{:S(2)}) copy-start(s32[8]{0:T(128)} %constant.20.clone) | copy-start | bytes 100
  57.5 0.7 copy-start
  59.8 5.6 %collective-permute-start.6 = (f32[152,256]{1,0:T(8,128)}, f32[152,256]{1,0:T(8,128)S(1)}, u32[]{:S(2)}, u32[]{:S(2)}) collective-permute-start(f32[152,256]{1,0:T(8,128)} %last_mix.1.refs_1_), channel_id=1, source_target_pairs={{0,1},{1,0},{2,3},{3,2},{4,5},{5,4},{6,7},{7,6},{8,9},{9,8},{10,11... | collective-permute-start | bytes 466952 | tf_op jit(solution)/shard_map/ppermute | solution.py:526
  65.4 0.7 copy-start.2

commit v3 on v2

--- a/solution.py
+++ b/solution.py
@@ -11,14 +11,21 @@
 f32 = jnp.float32
 bf16 = jnp.bfloat16
 step_tau = 0.5
-VMEM_LIMIT = 56 << 20
 ONE, POOL, SMALL = 128, 16, 8
 HALF = ONE + POOL + SMALL
 SENT = HALF + SMALL
 GATH = 24
-PARAMS = pltpu.CompilerParams(vmem_limit_bytes=VMEM_LIMIT)
+PARAMS = pltpu.CompilerParams(vmem_limit_bytes=16 << 20)
 VMEM = pl.BlockSpec(memory_space=pltpu.VMEM)
 SMEM = pl.BlockSpec(memory_space=pltpu.SMEM)
+
+
+def near(array):
+    return pltpu.with_memory_space_constraint(array, pltpu.VMEM)
+
+
+def far(array):
+    return pltpu.with_memory_space_constraint(array, pltpu.HBM)
 
 
 def dot(a, b, ca, cb, precision=None):
@@ -253,25 +260,23 @@
 def main_call(core, own, other, ew, eb, pw, pb, hid, cot, sum_a, sum_b, ow, qw, mw, ob):
     count, rows, width = hid.shape
     args = (
-        core, own, other, ew.T, eb.reshape(1, 32), pw, pb.reshape(1, 32), hid, cot,
-        sum_a, sum_b, ow, qw, mw, ob.reshape(1, width),
-    )
-    whole = [pl.BlockSpec(a.shape, lambda s, n=a.ndim: (0,) * n) for a in args]
+        core, far(own), near(other), far(ew.T), far(eb.reshape(1, 32)), far(pw),
+        far(pb.reshape(1, 32)), far(hid), far(cot), near(sum_a), near(sum_b), far(ow), far(qw),
+        far(mw), far(ob.reshape(1, width)),
+    )
     by_slice = pl.BlockSpec((1, rows, width), lambda s: (jnp.minimum(s, count - 1), 0, 0))
-    in_specs = [SMEM] + whole[1:7] + [by_slice, by_slice] + whole[9:]
-    shapes = [
-        jax.ShapeDtypeStruct((count * rows, width), bf16),
-        jax.ShapeDtypeStruct((count * rows, width), bf16),
-        jax.ShapeDtypeStruct((HALF + count, width), f32),
-        jax.ShapeDtypeStruct((HALF + count, width), f32),
-        jax.ShapeDtypeStruct((count, width), bf16),
-    ]
     return pl.pallas_call(
         main_kernel,
         grid=(count + 1,),
-        in_specs=in_specs,
-        out_specs=[pl.BlockSpec(a.shape, lambda s: (0, 0)) for a in shapes],
-        out_shape=shapes,
+        in_specs=[SMEM] + [VMEM] * 6 + [by_slice, by_slice] + [VMEM] * 6,
+        out_specs=[VMEM] * 5,
+        out_shape=[
+            jax.ShapeDtypeStruct((count * rows, width), bf16),
+            pltpu.VMEM((count * rows, width), bf16),
+            pltpu.VMEM((HALF + count, width), f32),
+            pltpu.VMEM((HALF + count, width), f32),
+            pltpu.VMEM((count, width), bf16),
+        ],
         scratch_shapes=[
             pltpu.VMEM((256, 2048), bf16),
             pltpu.VMEM((256, 256), bf16),
@@ -296,7 +301,7 @@
             pltpu.VMEM((count, 128, 256), f32),
             pltpu.VMEM((count, 16, 256), f32),
         ],
-        compiler_params=PARAMS,
+        compiler_params=pltpu.CompilerParams(vmem_limit_bytes=32 << 20),
         name="pair_and_one",
     )(*args)
 
@@ -336,12 +341,12 @@
         in_specs=[VMEM] * 4,
         out_specs=[VMEM] * 2,
         out_shape=[
-            jax.ShapeDtypeStruct((SENT + 2 * count + 8, 256), bf16),
-            jax.ShapeDtypeStruct((count, 256), f32),
+            pltpu.VMEM((SENT + 2 * count + 8, 256), bf16),
+            pltpu.VMEM((count, 256), f32),
         ],
         compiler_params=PARAMS,
         name="first_mix",
-    )(keep, came, mean_rows, pos)
+    )(near(keep), near(came), near(mean_rows), pos)
 
 
 def add_up(own_ref, came_ref):
@@ -360,10 +365,10 @@
         mix_kernel,
         in_specs=[VMEM] * 2,
         out_specs=VMEM,
-        out_shape=jax.ShapeDtypeStruct((rows, 256), bf16),
+        out_shape=pltpu.VMEM((rows, 256), bf16),
         compiler_params=PARAMS,
         name="mix",
-    )(own, came)
+    )(near(own), near(came))
 
 
 def last_kernel(own_ref, came_ref, out_ref):
@@ -375,10 +380,10 @@
         last_kernel,
         in_specs=[VMEM] * 2,
         out_specs=VMEM,
-        out_shape=jax.ShapeDtypeStruct((HALF, 256), f32),
+        out_shape=pltpu.VMEM((HALF, 256), f32),
         compiler_params=PARAMS,
         name="last_mix",
-    )(own, came)
+    )(near(own), near(came))
 
 
 def back_kernel(
@@ -405,15 +410,15 @@
 
 
 def back_call(cot, pre, updated, col, pos, ow, mw, dw):
-    args = (cot, pre, updated, col, pos, ow, mw, dw)
+    args = (cot, near(pre), updated, near(col), pos, ow, mw, dw)
     return pl.pallas_call(
         back_kernel,
         in_specs=[VMEM] * len(args),
         out_specs=[VMEM] * 3,
         out_shape=[
             jax.ShapeDtypeStruct(cot.shape, bf16),
-            jax.ShapeDtypeStruct((col.shape[0], 128), f32),
-            jax.ShapeDtypeStruct((8, 128), f32),
+            pltpu.VMEM((col.shape[0], 128), f32),
+            pltpu.VMEM((8, 128), f32),
         ],
         compiler_params=PARAMS,
         name="hidden_back",
@@ -445,7 +450,7 @@
 
 
 def mean_call(info, own, came, link, last, scale, count):
-    args = (info, own, came, link, last)
+    args = (info, near(own), near(came), near(link), near(last))
     devices = info.shape[0] - 2
 
     def body(*refs):
@@ -508,7 +513,7 @@
         ],
         compiler_params=PARAMS,
         name="unpack",
-    )(core, own, came)
+    )(core, near(own), near(came))
 
 
 def local(
@@ -557,6 +562,8 @@
             (s * 2 + e, (s ^ (1 << orders[e][t])) * 2 + e) for s in range(slices) for e in range(2)
         ]
         came = lax.ppermute(state, ("slices", "ering"), pairs)
+        if t == bits - 1:
+            came, hidden_grad, link, last = lax.optimization_barrier((came, hidden_grad, link, last))
         if t < bits - 1:
             state = mix_call(state, came)
     total = last_call(state, came)

time: 68.4 us -> 52.4 us (0.77)
  Pallas kernels: 39.4 us -> 29.6 us
  waiting for transfers between devices: 14.4 us -> 10.3 us
  local copies, waits for them, and re-layouts: 3.88 us -> 2.29 us
    ppermute x3, waiting for transfers between devices: 11.8 us -> 7.96 us  [local(): came = lax.ppermute(state, ('slices', 'ering'), pairs)]
    pallas_call x2, Pallas kernels: 3.23 us -> 0.05 us  [mix_call(): pl.pallas_call(mix_kernel, in_specs=[VMEM] * 2, out_specs=VMEM, out_shape...]
    pallas_call x1, Pallas kernels: 1.67 us -> 0.03 us  [first_call(): pl.pallas_call(first_kernel, in_specs=[VMEM] * 4, out_specs=[VMEM] * 2, o...]
    pallas_call x1, Pallas kernels: 1.65 us -> 0.02 us  [last_call(): pl.pallas_call(last_kernel, in_specs=[VMEM] * 2, out_specs=VMEM, out_shap...]
    unnamed x18 -> x14, local copies, waits for them, and re-layouts: 3.88 us -> 2.29 us
    pallas_call x1, Pallas kernels: 3.05 us -> 1.61 us  [back_call(): pl.pallas_call(back_kernel, in_specs=[VMEM] * len(args), out_specs=[VMEM]...]
    pallas_call x1, Pallas kernels: 1.92 us -> 0.94 us  [end_call(): pl.pallas_call(body, in_specs=[SMEM, VMEM, VMEM], out_specs=[VMEM] * 4, o...]
  transfers between devices with their start and end apart: 7 -> 7, of which waited for: 5 -> 5; matrix products, arithmetic and copies ran while one was open for 3% -> 2% of each run, Pallas kernels for 7% -> 6%
where the time goes in v3:
time: 52.4 us; the launch traced here: 52.1 us
  Pallas kernels  29.6 us (56%)
  waiting for transfers between devices  10.3 us (20%)
  starting transfers between devices  8.03 us (15%)
  local copies, waits for them, and re-layouts  2.29 us (4%)
  other arithmetic  1.21 us (2%)
  between operations  0.69 us (1%)
    pallas_call x1, Pallas kernels, main_call(): pl.pallas_call(main_kernel, grid=(count + 1,), in_specs=[SMEM] + [VMEM] *...  25.5 us
    ppermute x3, waiting for transfers between devices, local(): came = lax.ppermute(state, ('slices', 'ering'), pairs)  7.96 us
    ppermute x3, starting transfers between devices, local(): came = lax.ppermute(state, ('slices', 'ering'), pairs)  7.13 us
    ppermute x4, waiting for transfers between devices, swap(): return lax.ppermute(array, 'ering', [(0, 1), (1, 0)])  2.33 us
    unnamed x14, local copies, waits for them, and re-layouts  2.29 us
    pallas_call x1, Pallas kernels, back_call(): pl.pallas_call(back_kernel, in_specs=[VMEM] * len(args), out_specs=[VMEM]...  1.61 us
    pallas_call x1, Pallas kernels, mean_call(): pl.pallas_call(body, in_specs=[SMEM] + [VMEM] * 4, out_specs=[VMEM] * 2,...  1.47 us
    reduce_sum x1, other arithmetic, local(): part_sum = jnp.sum(hidden.astype(f32), axis=1)  1.12 us
  transfers between devices with their start and end apart: 7, of which 5 were waited for; matrix products, arithmetic and copies ran while one was open for 2% of the time, Pallas kernels for 6%

profile of v3, /device:TPU:0, one launch (start us, length us, event | category | flops | bytes accessed | tf_op | source)
XLA Modules:
  0.0 52.1 jit_solution(17853869290067498518)
XLA Ops:
  0.6 0.5 collective-permute-start
  1.1 1.1 %convert_reduce_fusion.sum_a_ref = f32[8,256]{1,0:T(8,128)S(1)} fusion(bf16[8,128,256]{2,1,0:T(8,128)(2,1)} %hid_ref.1), kind=kLoop, calls=%fused_computation | loop fusion | flops 522240 | bytes 532480 | tf_op jit(solution)/shard_map/reduce_sum | solution.py:549
  2.3 0.1 collective-permute-start.1
  2.4 1.1 %collective-permute-done.1.sum_b_ref = f32[8,256]{1,0:T(8,128)S(1)} collective-permute-done((f32[8,256]{1,0:T(8,128)S(1)}, f32[8,256]{1,0:T(8,128)S(1)}, u32[]{:S(2)}, u32[]{:S(2)}) %collective-permute-start.1) | collective-permute-done | bytes 8224 | tf_op jit(solution)/shard_map/ppermute | solution.py:531
  3.5 0.0 collective-permute-done.other_ref
  3.5 0.0 copy-start.4
  3.5 25.5 %pair_and_one.1 = (bf16[1024,256]{1,0:T(8,128)(2,1)}, bf16[1024,256]{1,0:T(8,128)(2,1)S(1)}, f32[160,256]{1,0:T(8,128)S(1)}, f32[160,256]{1,0:T(8,128)S(1)}, bf16[8,256]{1,0:T(8,128)(2,1)S(1)}) custom-call(s32[1]{0:T(128)} %bitcast.core_ref.refs_0_, f32[3,8,128]{2,1,0:T(8,128)} %pos_ref.3, f32[3,8,128]{2,1,0:T(8,128)S(1)} %collective-permute-done.other_ref, ...), custom_call_target="tpu_custom_call" | custom-call | tf_op jit(solution)/shard_map/pair_and_one/pallas_call | solution.py:268
  29.0 0.0 copy-start
  29.0 0.2 collective-permute-start.2
  29.2 1.2 %collective-permute-done.2.came_ref = f32[160,256]{1,0:T(8,128)S(1)} collective-permute-done((f32[160,256]{1,0:T(8,128)S(1)}, f32[160,256]{1,0:T(8,128)S(1)}, u32[]{:S(2)}, u32[]{:S(2)}) %collective-permute-start.2) | collective-permute-done | bytes 163872 | tf_op jit(solution)/shard_map/ppermute | solution.py:531
  30.4 0.0 copy-done.4
  30.4 2.7 %collective-permute-start.3 = (bf16[184,256]{1,0:T(8,128)(2,1)S(1)}, bf16[184,256]{1,0:T(8,128)(2,1)S(1)}, u32[]{:S(2)}, u32[]{:S(2)}) collective-permute-start(bf16[184,256]{1,0:T(8,128)(2,1)S(1)} %get-tuple-element.32.own_ref), channel_id=1, source_target_pairs={{0,2},{1,5},{2,0},{3,7},{4,6},{5,1},{6,4},{7,3},{8,10},{9,13},{10,... | collective-permute-start | bytes 282632 | tf_op jit(solution)/shard_map/ppermute | solution.py:564
  33.1 2.6 %collective-permute-done.3.came_ref = bf16[184,256]{1,0:T(8,128)(2,1)S(1)} collective-permute-done((bf16[184,256]{1,0:T(8,128)(2,1)S(1)}, bf16[184,256]{1,0:T(8,128)(2,1)S(1)}, u32[]{:S(2)}, u32[]{:S(2)}) %collective-permute-start.3) | collective-permute-done | bytes 94240 | tf_op jit(solution)/shard_map/ppermute | solution.py:564
  35.7 0.0 copy-start.2
  35.7 0.0 copy-start.3
  35.8 2.2 %collective-permute-start.4 = (bf16[208,256]{1,0:T(8,128)(2,1)S(1)}, bf16[208,256]{1,0:T(8,128)(2,1)S(1)}, u32[]{:S(2)}, u32[]{:S(2)}) collective-permute-start(bf16[208,256]{1,0:T(8,128)(2,1)S(1)} %mix.2.own_ref), channel_id=1, source_target_pairs={{0,4},{1,9},{2,6},{3,11},{4,0},{5,13},{6,2},{7,15},{8,12},{9,1},{1... | collective-permute-start | bytes 319496 | tf_op jit(solution)/shard_map/ppermute | solution.py:564
  37.9 3.7 %collective-permute-done.4.came_ref = bf16[208,256]{1,0:T(8,128)(2,1)S(1)} collective-permute-done((bf16[208,256]{1,0:T(8,128)(2,1)S(1)}, bf16[208,256]{1,0:T(8,128)(2,1)S(1)}, u32[]{:S(2)}, u32[]{:S(2)}) %collective-permute-start.4) | collective-permute-done | bytes 106528 | tf_op jit(solution)/shard_map/ppermute | solution.py:564
  41.6 2.2 %collective-permute-start.5 = (bf16[256,256]{1,0:T(8,128)(2,1)S(1)}, bf16[256,256]{1,0:T(8,128)(2,1)S(1)}, u32[]{:S(2)}, u32[]{:S(2)}) collective-permute-start(bf16[256,256]{1,0:T(8,128)(2,1)S(1)} %mix.3.refs_1_.own_ref), channel_id=1, source_target_pairs={{0,8},{1,3},{2,10},{3,1},{4,12},{5,7},{6,14},{7,5},{8,0},{9,11},{1... | collective-permute-start | bytes 393224 | tf_op jit(solution)/shard_map/ppermute | solution.py:564
  43.9 0.0 copy-start.5
  43.9 0.0 copy-done
  43.9 0.0 copy-done.2
  43.9 0.0 copy-done.3
  43.9 0.7 %copy-done.5 = bf16[3,256]{1,0:T(4,128)(2,1)S(1)} copy-done((bf16[3,256]{1,0:T(4,128)(2,1)S(1)}, bf16[3,256]{1,0:T(4,128)(2,1)}, u32[]{:S(2)}) %copy-start.5) | copy-done | bytes 1560
  44.5 1.0 %copy-done.1 = bf16[1024,256]{1,0:T(8,128)(2,1)S(1)} copy-done((bf16[1024,256]{1,0:T(8,128)(2,1)S(1)}, bf16[1024,256]{1,0:T(8,128)(2,1)}, u32[]{:S(2)}) %copy-start.1) | copy-done | bytes 524312
  45.6 1.6 %hidden_back.1 = (bf16[1024,256]{1,0:T(8,128)(2,1)}, f32[8,128]{1,0:T(8,128)S(1)}, f32[8,128]{1,0:T(8,128)S(1)}) custom-call(bf16[1024,256]{1,0:T(8,128)(2,1)S(1)} %bitcast.11, bf16[1024,256]{1,0:T(8,128)(2,1)S(1)} %get-tuple-element.33.pre_ref, bf16[1024,256]{1,0:T(8,128)(2,1)S(1)} %copy-done.1, f32[8,256]{1,0:T(8,128)S(1)} %get-tuple-element.34.col_ref, ...), custom_call_target="tpu_custom_call" | custom-call | tf_op jit(solution)/shard_map/hidden_back/pallas_call | solution.py:414
  47.2 1.8 %collective-permute-done.5.refs_2_.came_ref = bf16[256,256]{1,0:T(8,128)(2,1)S(1)} collective-permute-done((bf16[256,256]{1,0:T(8,128)(2,1)S(1)}, bf16[256,256]{1,0:T(8,128)(2,1)S(1)}, u32[]{:S(2)}, u32[]{:S(2)}) %collective-permute-start.5) | collective-permute-done | bytes 131104 | tf_op jit(solution)/shard_map/ppermute | solution.py:564
  49.0 0.1 collective-permute-start.6
  49.1 0.6 %copy-done.6 = s32[8]{0:T(128)S(1)} copy-done((s32[8]{0:T(128)S(1)}, s32[8]{0:T(128)}, u32[]{:S(2)}) %copy-start.6) | copy-done | bytes 56
  49.6 0.1 pad_add_fusion.refs_0_
  49.7 1.5 %mean_and_link.1 = (f32[256,256]{1,0:T(8,128)}, f32[8,128]{1,0:T(8,128)}) custom-call(s32[10]{0:T(128)S(1)} %pad_add_fusion.refs_0_, bf16[256,256]{1,0:T(8,128)(2,1)S(1)} %mix.3.refs_1_.own_ref, bf16[256,256]{1,0:T(8,128)(2,1)S(1)} %collective-permute-done.5.refs_2_.came_ref, f32[8,128]{1,0:T(8,128)S(1)} %get-tuple-element.40.refs_3_, ...), custom_call_target="tpu_custom_call" | custom-call | tf_op jit(solution)/shard_map/mean_and_link/pallas_call | solution.py:459
  51.2 0.0 collective-permute-done.6.refs_2_
  51.2 0.9 %unpack.1 = (f32[256,256]{1,0:T(8,128)}, f32[32,256]{1,0:T(8,128)}, f32[32,32]{1,0:T(8,128)}, f32[1,32]{1,0:T(1,128)}) custom-call(s32[1]{0:T(128)} %bitcast.core_ref.refs_0_, f32[152,256]{1,0:T(8,128)S(1)} %last_mix.1.refs_1_, f32[152,256]{1,0:T(8,128)S(1)} %collective-permute-done.6.refs_2_), custom_call_target="tpu_custom_call" | custom-call | tf_op jit(solution)/shard_map/unpack/pallas_call | solution.py:504
  (7 shorter events, 0.1 us)
Async XLA Ops:
  0.6 2.9 %collective-permute-start = (f32[3,8,128]{2,1,0:T(8,128)}, f32[3,8,128]{2,1,0:T(8,128)S(1)}, u32[]{:S(2)}, u32[]{:S(2)}) collective-permute-start(f32[3,8,128]{2,1,0:T(8,128)} %pos_ref.3), channel_id=1, source_target_pairs={{0,1},{1,0},{2,3},{3,2},{4,5},{5,4},{6,7},{7,6},{8,9},{9,8},{10,11... | collective-permute-start | bytes 36872 | tf_op jit(solution)/shard_map/ppermute | solution.py:531
  2.3 1.2 %collective-permute-start.1 = (f32[8,256]{1,0:T(8,128)S(1)}, f32[8,256]{1,0:T(8,128)S(1)}, u32[]{:S(2)}, u32[]{:S(2)}) collective-permute-start(f32[8,256]{1,0:T(8,128)S(1)} %convert_reduce_fusion.sum_a_ref), channel_id=1, source_target_pairs={{0,1},{1,0},{2,3},{3,2},{4,5},{5,4},{6,7},{7,6},{8,9},{9,8},{10,11... | collective-permute-start | bytes 24584 | tf_op jit(solution)/shard_map/ppermute | solution.py:531
  3.5 26.9 %copy-start.4 = (f32[3,8,128]{2,1,0:T(8,128)S(1)}, f32[3,8,128]{2,1,0:T(8,128)}, u32[]{:S(2)}) copy-start(f32[3,8,128]{2,1,0:T(8,128)} %pos_ref.3) | copy-start | bytes 36868
  29.0 14.9 %copy-start = (bf16[8,128,256]{2,1,0:T(8,128)(2,1)S(1)}, bf16[8,128,256]{2,1,0:T(8,128)(2,1)}, u32[]{:S(2)}) copy-start(bf16[8,128,256]{2,1,0:T(8,128)(2,1)} %cot_ref.1) | copy-start | bytes 1572868
  29.0 1.4 %collective-permute-start.2 = (f32[160,256]{1,0:T(8,128)S(1)}, f32[160,256]{1,0:T(8,128)S(1)}, u32[]{:S(2)}, u32[]{:S(2)}) collective-permute-start(f32[160,256]{1,0:T(8,128)S(1)} %get-tuple-element.30), channel_id=1, source_target_pairs={{0,1},{1,0},{2,3},{3,2},{4,5},{5,4},{6,7},{7,6},{8,9},{9,8},{10,11... | collective-permute-start | bytes 491528 | tf_op jit(solution)/shard_map/ppermute | solution.py:531
  30.4 5.3 %collective-permute-start.3 = (bf16[184,256]{1,0:T(8,128)(2,1)S(1)}, bf16[184,256]{1,0:T(8,128)(2,1)S(1)}, u32[]{:S(2)}, u32[]{:S(2)}) collective-permute-start(bf16[184,256]{1,0:T(8,128)(2,1)S(1)} %get-tuple-element.32.own_ref), channel_id=1, source_target_pairs={{0,2},{1,5},{2,0},{3,7},{4,6},{5,1},{6,4},{7,3},{8,10},{9,13},{10,... | collective-permute-start | bytes 282632 | tf_op jit(solution)/shard_map/ppermute | solution.py:564
  35.7 8.1 %copy-start.2 = (bf16[256,256]{1,0:T(8,128)(2,1)S(1)}, bf16[256,256]{1,0:T(8,128)(2,1)}, u32[]{:S(2)}) copy-start(bf16[256,256]{1,0:T(8,128)(2,1)} %ow_ref.3) | copy-start | bytes 393220
  35.7 8.1 %copy-start.3 = (bf16[256,256]{1,0:T(8,128)(2,1)S(1)}, bf16[256,256]{1,0:T(8,128)(2,1)}, u32[]{:S(2)}) copy-start(bf16[256,256]{1,0:T(8,128)(2,1)} %mw_ref.3) | copy-start | bytes 393220
  35.8 5.8 %collective-permute-start.4 = (bf16[208,256]{1,0:T(8,128)(2,1)S(1)}, bf16[208,256]{1,0:T(8,128)(2,1)S(1)}, u32[]{:S(2)}, u32[]{:S(2)}) collective-permute-start(bf16[208,256]{1,0:T(8,128)(2,1)S(1)} %mix.2.own_ref), channel_id=1, source_target_pairs={{0,4},{1,9},{2,6},{3,11},{4,0},{5,13},{6,2},{7,15},{8,12},{9,1},{1... | collective-permute-start | bytes 319496 | tf_op jit(solution)/shard_map/ppermute | solution.py:564
  41.6 7.3 %collective-permute-start.5 = (bf16[256,256]{1,0:T(8,128)(2,1)S(1)}, bf16[256,256]{1,0:T(8,128)(2,1)S(1)}, u32[]{:S(2)}, u32[]{:S(2)}) collective-permute-start(bf16[256,256]{1,0:T(8,128)(2,1)S(1)} %mix.3.refs_1_.own_ref), channel_id=1, source_target_pairs={{0,8},{1,3},{2,10},{3,1},{4,12},{5,7},{6,14},{7,5},{8,0},{9,11},{1... | collective-permute-start | bytes 393224 | tf_op jit(solution)/shard_map/ppermute | solution.py:564
  43.9 0.7 %copy-start.5 = (bf16[3,256]{1,0:T(4,128)(2,1)S(1)}, bf16[3,256]{1,0:T(4,128)(2,1)}, u32[]{:S(2)}) copy-start(bf16[3,256]{1,0:T(4,128)(2,1)} %dw_ref.1) | copy-start | bytes 4612
  44.5 1.0 %copy-start.1 = (bf16[1024,256]{1,0:T(8,128)(2,1)S(1)}, bf16[1024,256]{1,0:T(8,128)(2,1)}, u32[]{:S(2)}) copy-start(bf16[1024,256]{1,0:T(8,128)(2,1)} %get-tuple-element.28.upd_ref) | copy-start | bytes 1572868
  48.9 0.7 %copy-start.6 = (s32[8]{0:T(128)S(1)}, s32[8]{0:T(128)}, u32[]{:S(2)}) copy-start(s32[8]{0:T(128)} %constant.20.clone) | copy-start | bytes 100
  49.0 2.2 %collective-permute-start.6 = (f32[152,256]{1,0:T(8,128)S(1)}, f32[152,256]{1,0:T(8,128)S(1)}, u32[]{:S(2)}, u32[]{:S(2)}) collective-permute-start(f32[152,256]{1,0:T(8,128)S(1)} %last_mix.1.refs_1_), channel_id=1, source_target_pairs={{0,1},{1,0},{2,3},{3,2},{4,5},{5,4},{6,7},{7,6},{8,9},{9,8},{10,11... | collective-permute-start | bytes 466952 | tf_op jit(solution)/shard_map/ppermute | solution.py:531

commit v4 on v3

v4 whole, which is shorter than its diff:
```python
import math

import jax
import jax.numpy as jnp
from jax import lax
from jax.experimental import pallas as pl
from jax.experimental.pallas import tpu as pltpu
from jax.sharding import PartitionSpec as P

HIGH = lax.Precision.HIGHEST
f32 = jnp.float32
bf16 = jnp.bfloat16
step_tau = 0.5
ONE, POOL, SMALL = 128, 16, 8
HALF = ONE + POOL + SMALL
SENT = HALF + SMALL
COPIED = 5
PARAMS = pltpu.CompilerParams(vmem_limit_bytes=16 << 20)
VMEM = pl.BlockSpec(memory_space=pltpu.VMEM)
SMEM = pl.BlockSpec(memory_space=pltpu.SMEM)


def near(array):
    return pltpu.with_memory_space_constraint(array, pltpu.VMEM)


def far(array):
    return pltpu.with_memory_space_constraint(array, pltpu.HBM)


def dot(a, b, ca, cb, precision=None):
    return lax.dot_general(
        a, b, (((ca,), (cb,)), ((), ())), preferred_element_type=f32, precision=precision
    )


def split3(x):
    first = x.astype(bf16).astype(f32)
    rest = x - first
    second = rest.astype(bf16).astype(f32)
    return first, second, rest - second


def iota(shape, dim):
    return lax.broadcasted_iota(jnp.int32, shape, dim)


def pair_kernel(
    own_ref, other_ref, ew_ref, eb_ref, pw_ref, pb_ref, *refs
):
    pooled_ref, h_ref, g_ref, pre_ref = refs[COPIED : COPIED + 4]
    near_refs = refs[COPIED + 4 : 2 * COPIED + 4]
    copies = [
        pltpu.make_async_copy(refs[n], near_refs[n], refs[-1].at[n]) for n in range(COPIED)
    ]
    for copy in copies:
        copy.start()

    def ready():
        for copy in copies:
            copy.wait()

    def weigh(step):
        at = pl.ds(2 * step, 2)
        rows = near_refs[0][at].reshape(256, 256)
        pre_ref[at] = dot(rows, near_refs[2][...], 1, 0).reshape(2, 128, 256)

    pair_steps(
        own_ref, other_ref, ew_ref, eb_ref, pw_ref, pb_ref, pooled_ref, h_ref, g_ref,
        ready, weigh, *refs[2 * COPIED + 4 : -1],
    )


def pair_steps(
    own_ref, other_ref, ew_ref, eb_ref, pw_ref, pb_ref,
    pooled_ref, h_ref, g_ref, ready, weigh,
    embed_mat, block_mat, a_rows, feat_a, feat_b, bias_row, columns, misc_all,
    pre_a, pre_b, act_a, act_b, in_a, in_b, in_c, in_d, slope_a, slope_b, sum_a, sum_b, sum_c, sum_d,
):
    count = own_ref.shape[1]
    feats = (feat_a, feat_b)
    pre, acts, slopes = (pre_a, pre_b), (act_a, act_b), (slope_a, slope_b)
    ins, sums = (in_a, in_b, in_c, in_d), (sum_a, sum_b, sum_c, sum_d)

    def features(feat, at, first, size):
        lane = iota((size, 128), 1)
        square = jnp.ones((size, 128), f32)
        for c in range(3):
            spread = jnp.broadcast_to(
                columns[at, first : first + size, c : c + 1], (size, 128)
            )
            offset = spread - own_ref[c, pl.ds(at, 1), :]
            square = square + offset * offset
        radial = square * lax.rsqrt(square)
        misc = misc_all[at, first : first + size, :]
        high = radial.astype(bf16).astype(f32)
        low = radial - high
        high_turned = pltpu.roll(high, 64, 1)
        low_turned = pltpu.roll(low, 64, 1)
        left = lane < 64
        rows = slice(first, first + size)
        feat[0, rows, :128] = jnp.where(left, high, low_turned).astype(bf16)
        feat[0, rows, 128:] = jnp.where(left, high, misc).astype(bf16)
        feat[1, rows, :128] = jnp.where(left, high_turned, low).astype(bf16)
        feat[1, rows, 128:] = jnp.where(left, high_turned, misc).astype(bf16)

    wide = jnp.concatenate([ew_ref[...]] * 8, axis=1)
    w1, w2, w3 = split3(wide)
    row = iota((64, 256), 0)
    lane = iota((64, 256), 1)
    pieces = (w1, w2, w3, w1, w2, w1)
    misc = jnp.zeros((64, 256), f32)
    for c in range(3):
        for p in range(6):
            misc = jnp.where(row == 6 * c + p, -pieces[p][c : c + 1, :], misc)
    misc = misc.astype(bf16)
    for g in range(8):
        hit = row == g * 8 + lane // 32
        first = jnp.where(hit, w1[3:4, :], 0.0).astype(bf16)
        embed_mat[0:64, g * 256 : (g + 1) * 256] = first
        embed_mat[64:128, g * 256 : (g + 1) * 256] = first
        embed_mat[128:192, g * 256 : (g + 1) * 256] = jnp.where(hit, w2[3:4, :], 0.0).astype(bf16)
        embed_mat[192:256, g * 256 : (g + 1) * 256] = misc
    row = iota((256, 256), 0)
    lane = iota((256, 256), 1)
    tiled = jnp.concatenate([pw_ref[...].astype(f32).T] * 8, axis=1)
    tiled = jnp.concatenate([tiled] * 8, axis=0)
    block_mat[...] = jnp.where(row // 32 == lane // 32, tiled, 0.0).astype(bf16)
    bias_row[...] = jnp.broadcast_to(jnp.concatenate([pb_ref[...]] * 8, axis=1), (8, 256))
    wide_bias = jnp.concatenate([eb_ref[...]] * 8, axis=1)
    electron = iota((128, 256), 0)
    lane128 = iota((128, 256), 1)
    points = jnp.concatenate(
        [piece for c in range(3) for piece in split3(own_ref[c])], axis=0
    ).astype(bf16)
    for g in range(16):
        pick = jnp.where(electron == g * 8 + lane128 // 32, 1.0, 0.0).astype(bf16)
        spread = dot(points, pick, 1, 0)
        total = jnp.broadcast_to(wide_bias, (count, 256))
        for c in range(3):
            base = 3 * c * count
            point = (
                spread[base : base + count]
                + spread[base + count : base + 2 * count]
                + spread[base + 2 * count : base + 3 * count]
            )
            total = total + point * wide[c : c + 1, :]
        a_rows[:, g * 256 : (g + 1) * 256] = total
    blank = jnp.zeros((5, 256), f32)
    for at in range(count):
        stacked = jnp.concatenate(
            [
                jnp.concatenate(
                    [own_ref[c, at : at + 1, :], other_ref[c, at : at + 1, :]], axis=1
                )
                for c in range(3)
            ]
            + [blank],
            axis=0,
        )
        columns[at] = stacked.T
        spread = jnp.zeros((24, 256), f32)
        row = iota((24, 256), 0)
        for c in range(3):
            s1, s2, s3 = split3(stacked[c : c + 1, :])
            for p, piece in enumerate((s1, s1, s1, s2, s2, s3)):
                spread = jnp.where(row == 6 * c + p, piece, spread)
        zeros = jnp.zeros((64, 256), f32)
        misc_all[at] = jnp.concatenate([zeros, spread, zeros[0:40]], axis=0).T
    features(feat_a, 0, 0, 256)
    diagonal = iota((8, 256), 0) == iota((8, 256), 1) // 32
    block = iota((32, 256), 1) // 32

    def turn(step, places, started):
        def embed(n):
            at = 2 * step + n // 16
            half, inner = n % 16 // 8, n % 8
            out = dot(feats[n // 16][half], embed_mat[:, inner * 256 : (inner + 1) * 256], 1, 0)
            pre[n % 2][...] = out + a_rows[pl.ds(at, 1), n % 16 * 256 : (n % 16 + 1) * 256]

        def first_tanh(n):
            out = jnp.tanh(pre[n % 2][...])
            ins[n % 4][...] = out.astype(bf16)
            sums[n % 4][...] = jnp.sum(out.reshape(32, 8, 256), axis=0)

        def layer(n):
            acts[n % 2][...] = dot(ins[n % 4][...], block_mat[...], 1, 0) + bias_row[0:1, :]

        def slice_of(n):
            return jnp.maximum(2 * step - 1, 0) if n < 0 else 2 * step + n // 16

        def second_tanh(n):
            at, g = slice_of(n), n % 16
            act = jnp.tanh(acts[n % 2][...])
            total = sums[n % 4][...] + jnp.sum(act.reshape(32, 8, 256), axis=0)
            mean = jnp.sum(total, axis=0, keepdims=True) * (1.0 / 256)
            slope = 1.0 - act * act
            h_ref[at, g : g + 1, :] = jnp.sum(slope, axis=0, keepdims=True)
            pooled_ref[at, g * 8 : (g + 1) * 8, :] = jnp.where(diagonal, mean, 0.0)
            slopes[n % 2][...] = slope.astype(bf16)

        def outer(n):
            at, g = slice_of(n), n % 16
            product = dot(ins[n % 4][...], slopes[n % 2][...], 0, 0)
            picked = product[0:32]
            for q in range(1, 8):
                picked = jnp.where(block == q, product[q * 32 : (q + 1) * 32], picked)
            g_ref[at, g * 32 : (g + 1) * 32, :] = picked

        for place in places:
            for lag, stage in enumerate((embed, first_tanh, layer, second_tanh, outer)):
                if place - lag < started:
                    stage(place - lag)
            if started and place % 16 == 0:
                upcoming = jnp.minimum(2 * step + place // 16 + 1, count - 1)
                features(feats[1 - place // 16], upcoming, 0, 256)

    turns = count // 2

    def body(step, carry):
        weigh(step)
        turn(step, range(32), 32)
        return carry

    ready()
    lax.fori_loop(0, turns, body, 0)
    turn(turns, range(4), 0)


def pair_call(own, other, ew, eb, pw, pb, later):
    count = own.shape[1]
    args = (
        far(own), near(other), far(ew.T), far(eb.reshape(1, 32)), far(pw), far(pb.reshape(1, 32)),
    ) + tuple(far(a) for a in later)
    return pl.pallas_call(
        pair_kernel,
        in_specs=[VMEM] * 6 + [pl.BlockSpec(memory_space=pltpu.HBM)] * COPIED,
        out_specs=[VMEM] * (4 + COPIED),
        out_shape=[
            pltpu.VMEM((count, 128, 256), f32),
            pltpu.VMEM((count, 16, 256), f32),
            pltpu.VMEM((count, 512, 256), f32),
            pltpu.VMEM((count, 128, 256), f32),
        ]
        + [pltpu.VMEM(a.shape, a.dtype) for a in later],
        scratch_shapes=[
            pltpu.VMEM((256, 2048), bf16),
            pltpu.VMEM((256, 256), bf16),
            pltpu.VMEM((count, 4096), f32),
            pltpu.VMEM((2, 256, 256), bf16),
            pltpu.VMEM((2, 256, 256), bf16),
            pltpu.VMEM((8, 256), f32),
            pltpu.VMEM((count, 256, 8), f32),
            pltpu.VMEM((count, 256, 128), f32),
        ]
        + [pltpu.VMEM((256, 256), f32)] * 4
        + [pltpu.VMEM((256, 256), bf16)] * 6
        + [pltpu.VMEM((8, 256), f32)] * 4
        + [pltpu.SemaphoreType.DMA((COPIED,))],
        compiler_params=pltpu.CompilerParams(vmem_limit_bytes=24 << 20),
        name="pair_stage",
    )(*args)


def one_kernel(
    core_ref, hid_ref, cot_ref, one_pre_ref, pooled_ref, h_ref, g_ref, sum_a_ref, sum_b_ref,
    qw_ref, mw_ref, ob_ref,
    updated_ref, grad_ref, keep_ref, send_ref, mean_ref,
    back_all,
):
    count = sum_a_ref.shape[0]
    pool_mat = jnp.concatenate([qw_ref[...]] * 8, axis=0)
    mean_rows = ((sum_a_ref[...] + sum_b_ref[...]) * (1.0 / 256)).astype(bf16)
    mean_ref[...] = mean_rows
    per_slice = dot(mean_rows, mw_ref[...], 1, 0) + ob_ref[...]
    own_lanes = iota((256, 256), 0) % 8 == iota((256, 256), 1) // 32
    one_total = jnp.zeros((256, 256), f32)
    pool_total = jnp.zeros((256, 256), f32)
    pair_total = jnp.zeros((32, 256), f32)
    bias_total = jnp.zeros((32, 256), f32)
    parts = []

    def two(ref, n):
        value = ref[2 * n : 2 * n + 2]
        return value.reshape(2 * value.shape[1], 256)

    for step in range(count // 2 + 2):
        if step < count // 2:
            rows = slice(step * 256, (step + 1) * 256)
            shift = jnp.concatenate(
                [
                    jnp.broadcast_to(per_slice[n : n + 1, :], (128, 256))
                    for n in (2 * step, 2 * step + 1)
                ],
                axis=0,
            )
            pooled = two(pooled_ref, step).astype(bf16)
            act = jnp.tanh(two(one_pre_ref, step) + dot(pooled, pool_mat, 1, 0) + shift)
            updated_ref[rows, :] = (act + two(hid_ref, step).astype(f32)).astype(bf16)
            grad = (two(cot_ref, step).astype(f32) * (1.0 - act * act)).astype(bf16)
            grad_ref[rows, :] = grad
            wide = grad.astype(f32)
            parts.append(jnp.sum(wide[0:128], axis=0, keepdims=True))
            parts.append(jnp.sum(wide[128:], axis=0, keepdims=True))
        n = step - 1
        if 0 <= n < count // 2:
            grad = grad_ref[n * 256 : (n + 1) * 256, :]
            back = jnp.where(own_lanes, dot(grad, pool_mat, 1, 1), 0.0)
            back_all[n] = jnp.sum(back.reshape(32, 8, 256), axis=1)
            one_total = one_total + dot(two(hid_ref, n), grad, 0, 0)
            pool_total = pool_total + dot(two(pooled_ref, n).astype(bf16), grad, 0, 0)
        n = step - 2
        if 0 <= n < count // 2:
            bias_total = bias_total + back_all[n] * two(h_ref, n)
            for g in range(32):
                part = g_ref[2 * n + g // 16, g % 16 * 32 : (g % 16 + 1) * 32, :]
                pair_total = pair_total + part * back_all[n, g : g + 1, :]
    fold = jnp.where(iota((256, 256), 0) % 32 == iota((256, 256), 1) % 32, 1.0, 0.0)
    pool = pool_total[0:32]
    for q in range(1, 8):
        pool = pool + pool_total[q * 32 : (q + 1) * 32]
    bias_one = jnp.broadcast_to(jnp.sum(bias_total, axis=0, keepdims=True), (8, 256))
    folded = dot(jnp.concatenate([pair_total, bias_one], axis=0), fold, 1, 0, HIGH)
    picked = jnp.where(iota((32, 256), 0) % 8 == iota((32, 256), 1) // 32, folded[0:32], 0.0)
    packed = jnp.sum(picked.reshape(4, 8, 256), axis=1)
    small = jnp.concatenate([packed, folded[32:36]], axis=0)
    core = core_ref[0]

    @pl.when(core == 0)
    def _():
        keep_ref[0:ONE, :] = one_total[0:ONE]
        send_ref[0:ONE, :] = one_total[ONE:]
        keep_ref[ONE : ONE + POOL, :] = pool[0:POOL]
        send_ref[ONE : ONE + POOL, :] = pool[POOL:]

    @pl.when(core == 1)
    def _():
        send_ref[0:ONE, :] = one_total[0:ONE]
        keep_ref[0:ONE, :] = one_total[ONE:]
        send_ref[ONE : ONE + POOL, :] = pool[0:POOL]
        keep_ref[ONE : ONE + POOL, :] = pool[POOL:]

    keep_ref[ONE + POOL : HALF, :] = small
    send_ref[ONE + POOL : HALF, :] = small
    sums = jnp.concatenate(parts, axis=0)
    keep_ref[HALF:, :] = sums
    send_ref[HALF:, :] = sums


def one_call(core, hid, cot, one_pre, pooled, h_sums, g_sums, sum_a, sum_b, qw, mw, ob):
    count, rows, width = hid.shape
    args = (
        core, near(hid), near(cot), near(one_pre), near(pooled), near(h_sums), near(g_sums), near(sum_a),
        near(sum_b), near(qw), near(mw), far(ob.reshape(1, width)),
    )
    return pl.pallas_call(
        one_kernel,
        in_specs=[SMEM] + [VMEM] * 11,
        out_specs=[VMEM] * 5,
        out_shape=[
            jax.ShapeDtypeStruct((count * rows, width), bf16),
            pltpu.VMEM((count * rows, width), bf16),
            pltpu.VMEM((HALF + count, width), f32),
            pltpu.VMEM((HALF + count, width), f32),
            pltpu.VMEM((count, width), bf16),
        ],
        scratch_shapes=[pltpu.VMEM((count // 2, 32, 256), f32)],
        compiler_params=PARAMS,
        name="one_stage",
    )(*args)


def pack(total, gath, out_ref):
    out_ref[0:HALF, :] = total.astype(bf16)
    small = total[ONE + POOL :]
    out_ref[HALF:SENT, :] = (small - small.astype(bf16).astype(f32)).astype(bf16)
    at = SENT
    for piece in gath:
        out_ref[at : at + piece.shape[0], :] = piece
        at += piece.shape[0]


def first_kernel(keep_ref, came_ref, mean_ref, pos_ref, out_ref, col_ref):
    both = keep_ref[...] + came_ref[...]
    col = both[HALF:]
    col_ref[...] = col
    p1, p2, p3 = split3(pos_ref[:, 0, :])
    blank = jnp.zeros((2, 256), f32)
    border = jnp.concatenate(
        [
            jnp.concatenate([p1, p2], axis=1),
            jnp.concatenate([p3, jnp.zeros_like(p3)], axis=1),
            blank,
        ],
        axis=0,
    )
    gath = jnp.concatenate([mean_ref[...].astype(f32), col, border], axis=0).astype(bf16)
    pack(both[0:HALF], [gath], out_ref)


def first_call(keep, came, mean_rows, pos):
    count = mean_rows.shape[0]
    return pl.pallas_call(
        first_kernel,
        in_specs=[VMEM] * 4,
        out_specs=[VMEM] * 2,
        out_shape=[
            pltpu.VMEM((SENT + 2 * count + 8, 256), bf16),
            pltpu.VMEM((count, 256), f32),
        ],
        compiler_params=PARAMS,
        name="first_mix",
    )(near(keep), near(came), near(mean_rows), pos)


def add_up(own_ref, came_ref):
    total = own_ref[0:HALF, :].astype(f32) + came_ref[0:HALF, :].astype(f32)
    rest = own_ref[HALF:SENT, :].astype(f32) + came_ref[HALF:SENT, :].astype(f32)
    return jnp.concatenate([total[0 : ONE + POOL], total[ONE + POOL :] + rest], axis=0)


def mix_kernel(own_ref, came_ref, out_ref):
    pack(add_up(own_ref, came_ref), [own_ref[SENT:, :], came_ref[SENT:, :]], out_ref)


def mix_call(own, came):
    rows = SENT + 2 * (own.shape[0] - SENT)
    return pl.pallas_call(
        mix_kernel,
        in_specs=[VMEM] * 2,
        out_specs=VMEM,
        out_shape=pltpu.VMEM((rows, 256), bf16),
        compiler_params=PARAMS,
        name="mix",
    )(near(own), near(came))


def last_kernel(own_ref, came_ref, out_ref):
    out_ref[...] = add_up(own_ref, came_ref)


def last_call(own, came):
    return pl.pallas_call(
        last_kernel,
        in_specs=[VMEM] * 2,
        out_specs=VMEM,
        out_shape=pltpu.VMEM((HALF, 256), f32),
        compiler_params=PARAMS,
        name="last_mix",
    )(near(own), near(came))


def back_kernel(
    cot_ref, pre_ref, upd_ref, col_ref, pos_ref, ow_ref, mw_ref, dw_ref,
    grad_ref, link_ref, last_ref,
):
    count = col_ref.shape[0]
    back = dot(col_ref[...], mw_ref[...].astype(f32), 1, 1, HIGH) * (1.0 / 256)
    drifts = []
    for s in range(count):
        at = slice(s * 128, (s + 1) * 128)
        grad = cot_ref[at, :].astype(f32) + dot(pre_ref[at, :], ow_ref[...], 1, 1)
        grad_ref[at, :] = (grad + back[s : s + 1, :]).astype(bf16)
        drifts.append(dot(dw_ref[...], upd_ref[at, :], 1, 1))
    for s in range(count):
        here = [-pos_ref[c, s : s + 1, :] - step_tau * drifts[s][c : c + 1, :] for c in range(3)]
        if s < count - 1:
            jumps = [here[c] + pos_ref[c, s + 1 : s + 2, :] for c in range(3)]
            total = jumps[0] * jumps[0] + jumps[1] * jumps[1] + jumps[2] * jumps[2]
            link_ref[s : s + 1, :] = total * (1.0 / (12.0 * step_tau))
        else:
            link_ref[s : s + 1, :] = jnp.zeros((1, 128), f32)
            last_ref[...] = jnp.concatenate(here + [jnp.zeros((5, 128), f32)], axis=0)


def back_call(cot, pre, updated, col, pos, ow, mw, dw):
    args = (near(cot), near(pre), far(updated), near(col), far(pos), near(ow), near(mw), far(dw))
    return pl.pallas_call(
        back_kernel,
        in_specs=[VMEM] * len(args),
        out_specs=[VMEM] * 3,
        out_shape=[
            jax.ShapeDtypeStruct(cot.shape, bf16),
            pltpu.VMEM((col.shape[0], 128), f32),
            pltpu.VMEM((8, 128), f32),
        ],
        compiler_params=PARAMS,
        name="hidden_back",
    )(*args)


def mean_kernel(
    info_ref, own_ref, came_ref, link_ref, last_ref,
    mean_ref, out_link_ref,
    mean_all, col_all, border, *, scale, count, masks,
):
    stride = 2 * count + 8
    half = (own_ref.shape[0] - SENT) // stride
    place, core = info_ref[0], info_ref[1]
    for d in range(2 * half):
        owner = place ^ jnp.where(core == 0, masks[0][d], masks[1][d])
        ref = own_ref if d < half else came_ref
        base = SENT + (d % half) * stride
        block = ref[base : base + stride, :].astype(f32)
        at = pl.ds(pl.multiple_of(owner * count, 8), count)
        mean_all[at, :] = block[0:count]
        col_all[at, :] = block[count : 2 * count]
        border[pl.ds(pl.multiple_of(owner * 8, 8), 8), :] = block[2 * count :]
    mean_ref[...] = scale * dot(mean_all[...].astype(bf16), col_all[...].astype(bf16), 0, 0)
    out_link_ref[...] = link_ref[...]
    pieces = border[pl.ds(pl.multiple_of(jnp.minimum(place + 1, 2 * half - 1) * 8, 8), 8), :]
    point = pieces[0:3, 0:128] + pieces[0:3, 128:] + pieces[3:6, 0:128]
    jump = point + last_ref[0:3, :]
    total = jnp.sum(jump * jump, axis=0, keepdims=True) * (1.0 / (12.0 * step_tau))
    out_link_ref[count - 1 : count, :] = jnp.where(place == 2 * half - 1, 0.0, total)


def mean_call(info, own, came, link, last, scale, count, masks):
    args = (info, near(own), near(came), near(link), near(last))
    devices = len(masks[0])

    def body(*refs):
        mean_kernel(*refs, scale=scale, count=count, masks=masks)

    return pl.pallas_call(
        body,
        in_specs=[SMEM] + [VMEM] * 4,
        out_specs=[VMEM] * 2,
        out_shape=[
            jax.ShapeDtypeStruct((256, 256), f32),
            jax.ShapeDtypeStruct((count, 128), f32),
        ],
        scratch_shapes=[
            pltpu.VMEM((devices * count, 256), f32),
            pltpu.VMEM((devices * count, 256), f32),
            pltpu.VMEM((devices * 8, 256), f32),
        ],
        compiler_params=PARAMS,
        name="mean_and_link",
    )(*args)


def end_kernel(core_ref, own_ref, came_ref, one_ref, pool_ref, pair_ref, bias_ref, *, scale):
    def write(low_ref, high_ref):
        one_ref[0:ONE, :] = scale * low_ref[0:ONE, :]
        one_ref[ONE:, :] = scale * high_ref[0:ONE, :]
        pool_ref[0:POOL, :] = scale * low_ref[ONE : ONE + POOL, :]
        pool_ref[POOL:, :] = scale * high_ref[ONE : ONE + POOL, :]

        small = low_ref[ONE + POOL : HALF, :]
        rows = jnp.concatenate(
            [jnp.broadcast_to(small[r : r + 1], (8, 256)) for r in range(4)], axis=0
        )
        rows = jnp.where(iota((32, 256), 0) % 8 == iota((32, 256), 1) // 32, rows, 0.0)
        total = rows[:, 0:128] + rows[:, 128:]
        total = total + pltpu.roll(total, 64, 1)
        total = total + pltpu.roll(total, 32, 1)
        pair_ref[...] = (scale / 256.0) * total[:, 0:32].T
        bias_ref[...] = (scale / 256.0) * small[4:5, 0:32]

    core = core_ref[0]
    pl.when(core == 0)(lambda: write(own_ref, came_ref))
    pl.when(core == 1)(lambda: write(came_ref, own_ref))


def end_call(core, own, came, scale):
    def body(*refs):
        end_kernel(*refs, scale=scale)

    return pl.pallas_call(
        body,
        in_specs=[SMEM, VMEM, VMEM],
        out_specs=[VMEM] * 4,
        out_shape=[
            jax.ShapeDtypeStruct((256, 256), f32),
            jax.ShapeDtypeStruct((32, 256), f32),
            jax.ShapeDtypeStruct((32, 32), f32),
            jax.ShapeDtypeStruct((1, 32), f32),
        ],
        compiler_params=PARAMS,
        name="unpack",
    )(core, near(own), near(came))


def local(
    positions, hidden, cotangent, embed_weight, embed_bias, pair_weight, pair_bias,
    one_weight, pool_weight, mean_weight, one_bias, drift_weight,
):
    count, own_count, width = hidden.shape
    slices = lax.axis_size("slices")
    bits = slices.bit_length() - 1
    scale = 1.0 / math.sqrt(count * slices * own_count * lax.axis_size("ering"))
    core = lax.axis_index("ering").astype(jnp.int32)
    place = lax.axis_index("slices").astype(jnp.int32)

    def swap(array):
        return lax.ppermute(array, "ering", [(0, 1), (1, 0)])

    orders = [[(t + e) % bits for t in range(bits)] for e in range(2)]
    masks = [
        [sum(((d >> t) & 1) << orders[e][t] for t in range(bits)) for d in range(slices)]
        for e in range(2)
    ]
    info = jnp.stack([place, core])
    core = core.reshape(1)

    other_pos = swap(positions)
    part_sum = jnp.sum(hidden.astype(f32), axis=1)
    other_sum = swap(part_sum)
    pooled, h_sums, g_sums, one_pre, hid_near, cot_near, one_near, pool_near, mean_near = pair_call(
        positions, other_pos, embed_weight, embed_bias, pair_weight, pair_bias,
        (hidden, cotangent, one_weight, pool_weight, mean_weight),
    )
    updated, pre, keep, send, mean_rows = one_call(
        core, hid_near, cot_near, one_pre, pooled, h_sums, g_sums, part_sum, other_sum,
        pool_near, mean_near, one_bias,
    )
    state, col_total = first_call(keep, swap(send), mean_rows, positions)
    hidden_grad, link, last = back_call(
        cot_near.reshape(pre.shape), pre, updated, col_total, positions, one_near,
        mean_near, drift_weight,
    )
    for t in range(bits):
        pairs = [
            (s * 2 + e, (s ^ (1 << orders[e][t])) * 2 + e) for s in range(slices) for e in range(2)
        ]
        came = lax.ppermute(state, ("slices", "ering"), pairs)
        if t == bits - 1:
            came, hidden_grad, link, last = lax.optimization_barrier((came, hidden_grad, link, last))
        if t < bits - 1:
            state = mix_call(state, came)
    total = last_call(state, came)
    other_total = swap(total)
    mean_grad, link_terms = mean_call(info, state, came, link, last, scale, count, masks)
    one_grad, pool_grad, pair_grad, bias_grad = end_call(core, total, other_total, scale)
    return (
        updated.reshape(hidden.shape),
        hidden_grad.reshape(hidden.shape),
        link_terms,
        pair_grad,
        bias_grad.reshape(-1),
        one_grad,
        pool_grad,
        mean_grad,
    )


def solution(mesh):
    in_specs = (
        P(None, ("groups", "slices"), "ering"),
        P(("groups", "slices"), "ering", None),
        P(("groups", "slices"), "ering", None),
    ) + (P(),) * 9
    out_specs = (
        P(("groups", "slices"), "ering", None),
        P(("groups", "slices"), "ering", None),
        P(("groups", "slices"), "ering"),
        P("groups", None),
        P("groups"),
        P("groups", None),
        P("groups", None),
        P("groups", None),
    )
    return jax.shard_map(local, mesh=mesh, in_specs=in_specs, out_specs=out_specs, check_vma=False)
```

time: 52.4 us -> 47 us (0.90)
  waiting for transfers between devices: 10.3 us -> 7.85 us
  local copies, waits for them, and re-layouts: 2.29 us -> 0.01 us
  Pallas kernels: 29.6 us -> 28 us
  starting transfers between devices: 8.03 us -> 8.71 us
    pallas_call x1 -> x2, Pallas kernels: 25.5 us -> 22.8 us  [the longest x1 19.5 us: pair_call(): pl.pallas_call(pair_kernel, in_specs=[VMEM] * 6 + [pl.BlockSpec(memory_sp...]
    unnamed x14 -> x2, local copies, waits for them, and re-layouts: 2.29 us -> 0.01 us
    ppermute x4, waiting for transfers between devices: 2.33 us -> 1.04 us  [swap(): return lax.ppermute(array, 'ering', [(0, 1), (1, 0)])]
    ppermute x3, waiting for transfers between devices: 7.96 us -> 6.81 us  [local(): came = lax.ppermute(state, ('slices', 'ering'), pairs)]
    pallas_call x1, Pallas kernels: 1.61 us -> 2.67 us  [back_call(): pl.pallas_call(back_kernel, in_specs=[VMEM] * len(args), out_specs=[VMEM]...]
  transfers between devices with their start and end apart: 7 -> 7, of which waited for: 5 -> 4; matrix products, arithmetic and copies ran while one was open for 2% -> 3% of each run, Pallas kernels for 6% -> 51%
where the time goes in v4:
time: 47 us; the launch traced here: 46.5 us
  Pallas kernels  28 us (60%)
  starting transfers between devices  8.71 us (19%)
  waiting for transfers between devices  7.85 us (17%)
  other arithmetic  1.2 us (3%)
  between operations  0.68 us (1%)
    pallas_call x1, Pallas kernels, pair_call(): pl.pallas_call(pair_kernel, in_specs=[VMEM] * 6 + [pl.BlockSpec(memory_sp...  19.5 us
    ppermute x3, starting transfers between devices, local(): came = lax.ppermute(state, ('slices', 'ering'), pairs)  7.52 us
    ppermute x3, waiting for transfers between devices, local(): came = lax.ppermute(state, ('slices', 'ering'), pairs)  6.81 us
    pallas_call x1, Pallas kernels, one_call(): pl.pallas_call(one_kernel, in_specs=[SMEM] + [VMEM] * 11, out_specs=[VMEM...  3.33 us
    pallas_call x1, Pallas kernels, back_call(): pl.pallas_call(back_kernel, in_specs=[VMEM] * len(args), out_specs=[VMEM]...  2.67 us
    pallas_call x1, Pallas kernels, mean_call(): pl.pallas_call(body, in_specs=[SMEM] + [VMEM] * 4, out_specs=[VMEM] * 2,...  1.48 us
    ppermute x4, starting transfers between devices, swap(): return lax.ppermute(array, 'ering', [(0, 1), (1, 0)])  1.19 us
    reduce_sum x1, other arithmetic, local(): part_sum = jnp.sum(hidden.astype(f32), axis=1)  1.12 us
  transfers between devices with their start and end apart: 7, of which 4 were waited for; matrix products, arithmetic and copies ran while one was open for 3% of the time, Pallas kernels for 51%

profile of v4, /device:TPU:0, one launch (start us, length us, event | category | flops | bytes accessed | tf_op | source)
XLA Modules:
  0.0 46.5 jit_solution(17593857459071527901)
XLA Ops:
  0.6 0.5 %collective-permute-start = (f32[3,8,128]{2,1,0:T(8,128)}, f32[3,8,128]{2,1,0:T(8,128)S(1)}, u32[]{:S(2)}, u32[]{:S(2)}) collective-permute-start(f32[3,8,128]{2,1,0:T(8,128)} %pos_ref.3), channel_id=1, source_target_pairs={{0,1},{1,0},{2,3},{3,2},{4,5},{5,4},{6,7},{7,6},{8,9},{9,8},{10,11... | collective-permute-start | bytes 36872 | tf_op jit(solution)/shard_map/ppermute | solution.py:597
  1.1 1.1 %convert_reduce_fusion.sum_a_ref = f32[8,256]{1,0:T(8,128)S(1)} fusion(bf16[8,128,256]{2,1,0:T(8,128)(2,1)} %refs_0_.1), kind=kLoop, calls=%fused_computation | loop fusion | flops 522240 | bytes 532480 | tf_op jit(solution)/shard_map/reduce_sum | solution.py:608
  2.3 0.1 collective-permute-start.1
  2.4 0.0 collective-permute-done.other_ref
  2.4 0.0 copy-start
  2.4 19.5 %pair_stage.1 = (f32[8,128,256]{2,1,0:T(8,128)S(1)}, f32[8,16,256]{2,1,0:T(8,128)S(1)}, f32[8,512,256]{2,1,0:T(8,128)S(1)}, f32[8,128,256]{2,1,0:T(8,128)S(1)}, ...) custom-call(f32[3,8,128]{2,1,0:T(8,128)} %pos_ref.3, ...), custom_call_target="tpu_custom_call" | custom-call | tf_op jit(solution)/shard_map/pair_stage/pallas_call | solution.py:235
  21.9 0.0 collective-permute-done.1.sum_b_ref
  21.9 3.3 %one_stage.1 = (bf16[1024,256]{1,0:T(8,128)(2,1)}, bf16[1024,256]{1,0:T(8,128)(2,1)S(1)}, f32[160,256]{1,0:T(8,128)S(1)}, f32[160,256]{1,0:T(8,128)S(1)}, bf16[8,256]{1,0:T(8,128)(2,1)S(1)}) custom-call(s32[1]{0:T(128)} %bitcast.core_ref.refs_0_, bf16[8,128,256]{2,1,0:T(8,128)(2,1)S(1)} %get-tuple-element.37.hid_ref, ...), custom_call_target="tpu_custom_call" | custom-call | tf_op jit(solution)/shard_map/one_stage/pallas_call | solution.py:356
  25.2 0.5 %collective-permute-start.2 = (f32[160,256]{1,0:T(8,128)S(1)}, f32[160,256]{1,0:T(8,128)S(1)}, u32[]{:S(2)}, u32[]{:S(2)}) collective-permute-start(f32[160,256]{1,0:T(8,128)S(1)} %get-tuple-element.47), channel_id=1, source_target_pairs={{0,1},{1,0},{2,3},{3,2},{4,5},{5,4},{6,7},{7,6},{8,9},{9,8},{10,11... | collective-permute-start | bytes 491528 | tf_op jit(solution)/shard_map/ppermute | solution.py:597
  25.7 1.0 %collective-permute-done.2.came_ref = f32[160,256]{1,0:T(8,128)S(1)} collective-permute-done((f32[160,256]{1,0:T(8,128)S(1)}, f32[160,256]{1,0:T(8,128)S(1)}, u32[]{:S(2)}, u32[]{:S(2)}) %collective-permute-start.2) | collective-permute-done | bytes 163872 | tf_op jit(solution)/shard_map/ppermute | solution.py:597
  26.7 0.0 copy-done
  26.8 2.9 %collective-permute-start.3 = (bf16[184,256]{1,0:T(8,128)(2,1)S(1)}, bf16[184,256]{1,0:T(8,128)(2,1)S(1)}, u32[]{:S(2)}, u32[]{:S(2)}) collective-permute-start(bf16[184,256]{1,0:T(8,128)(2,1)S(1)} %get-tuple-element.49.own_ref), channel_id=1, source_target_pairs={{0,2},{1,5},{2,0},{3,7},{4,6},{5,1},{6,4},{7,3},{8,10},{9,13},{10,... | collective-permute-start | bytes 282632 | tf_op jit(solution)/shard_map/ppermute | solution.py:627
  29.7 2.6 %collective-permute-done.3.came_ref = bf16[184,256]{1,0:T(8,128)(2,1)S(1)} collective-permute-done((bf16[184,256]{1,0:T(8,128)(2,1)S(1)}, bf16[184,256]{1,0:T(8,128)(2,1)S(1)}, u32[]{:S(2)}, u32[]{:S(2)}) %collective-permute-start.3) | collective-permute-done | bytes 94240 | tf_op jit(solution)/shard_map/ppermute | solution.py:627
  32.3 2.2 %collective-permute-start.4 = (bf16[208,256]{1,0:T(8,128)(2,1)S(1)}, bf16[208,256]{1,0:T(8,128)(2,1)S(1)}, u32[]{:S(2)}, u32[]{:S(2)}) collective-permute-start(bf16[208,256]{1,0:T(8,128)(2,1)S(1)} %mix.2.own_ref), channel_id=1, source_target_pairs={{0,4},{1,9},{2,6},{3,11},{4,0},{5,13},{6,2},{7,15},{8,12},{9,1},{1... | collective-permute-start | bytes 319496 | tf_op jit(solution)/shard_map/ppermute | solution.py:627
  34.5 3.4 %collective-permute-done.4.came_ref = bf16[208,256]{1,0:T(8,128)(2,1)S(1)} collective-permute-done((bf16[208,256]{1,0:T(8,128)(2,1)S(1)}, bf16[208,256]{1,0:T(8,128)(2,1)S(1)}, u32[]{:S(2)}, u32[]{:S(2)}) %collective-permute-start.4) | collective-permute-done | bytes 106528 | tf_op jit(solution)/shard_map/ppermute | solution.py:627
  37.9 2.4 %collective-permute-start.5 = (bf16[256,256]{1,0:T(8,128)(2,1)S(1)}, bf16[256,256]{1,0:T(8,128)(2,1)S(1)}, u32[]{:S(2)}, u32[]{:S(2)}) collective-permute-start(bf16[256,256]{1,0:T(8,128)(2,1)S(1)} %mix.3.refs_1_.own_ref), channel_id=1, source_target_pairs={{0,8},{1,3},{2,10},{3,1},{4,12},{5,7},{6,14},{7,5},{8,0},{9,11},{1... | collective-permute-start | bytes 393224 | tf_op jit(solution)/shard_map/ppermute | solution.py:627
  40.4 2.7 %hidden_back.1 = (bf16[1024,256]{1,0:T(8,128)(2,1)}, f32[8,128]{1,0:T(8,128)S(1)}, f32[8,128]{1,0:T(8,128)S(1)}) custom-call(bf16[1024,256]{1,0:T(8,128)(2,1)S(1)} %bitcast.10, bf16[1024,256]{1,0:T(8,128)(2,1)S(1)} %get-tuple-element.50.pre_ref, bf16[1024,256]{1,0:T(8,128)(2,1)} %get-tuple-element.45.upd_ref, f32[8,256]{1,0:T(8,128)S(1)} %get-tuple-element.51.col_ref, ...), custom_call_target="tpu_custom_call" | custom-call | tf_op jit(solution)/shard_map/hidden_back/pallas_call | solution.py:478
  43.0 0.8 %collective-permute-done.5.refs_2_.came_ref = bf16[256,256]{1,0:T(8,128)(2,1)S(1)} collective-permute-done((bf16[256,256]{1,0:T(8,128)(2,1)S(1)}, bf16[256,256]{1,0:T(8,128)(2,1)S(1)}, u32[]{:S(2)}, u32[]{:S(2)}) %collective-permute-start.5) | collective-permute-done | bytes 131104 | tf_op jit(solution)/shard_map/ppermute | solution.py:627
  43.9 0.1 collective-permute-start.6
  44.0 0.1 pad_add_fusion.refs_0_
  44.0 1.5 %mean_and_link.1 = (f32[256,256]{1,0:T(8,128)}, f32[8,128]{1,0:T(8,128)}) custom-call(s32[2]{0:T(128)S(1)} %pad_add_fusion.refs_0_, bf16[256,256]{1,0:T(8,128)(2,1)S(1)} %mix.3.refs_1_.own_ref, bf16[256,256]{1,0:T(8,128)(2,1)S(1)} %collective-permute-done.5.refs_2_.came_ref, f32[8,128]{1,0:T(8,128)S(1)} %get-tuple-element.58.refs_3_, ...), custom_call_target="tpu_custom_call" | custom-call | tf_op jit(solution)/shard_map/mean_and_link/pallas_call | solution.py:525
  45.5 0.0 collective-permute-done.6.refs_2_
  45.5 0.9 %unpack.1 = (f32[256,256]{1,0:T(8,128)}, f32[32,256]{1,0:T(8,128)}, f32[32,32]{1,0:T(8,128)}, f32[1,32]{1,0:T(1,128)}) custom-call(s32[1]{0:T(128)} %bitcast.core_ref.refs_0_, f32[152,256]{1,0:T(8,128)S(1)} %last_mix.1.refs_1_, f32[152,256]{1,0:T(8,128)S(1)} %collective-permute-done.6.refs_2_), custom_call_target="tpu_custom_call" | custom-call | tf_op jit(solution)/shard_map/unpack/pallas_call | solution.py:570
  (4 shorter events, 0.1 us)
Async XLA Ops:
  0.6 1.8 %collective-permute-start = (f32[3,8,128]{2,1,0:T(8,128)}, f32[3,8,128]{2,1,0:T(8,128)S(1)}, u32[]{:S(2)}, u32[]{:S(2)}) collective-permute-start(f32[3,8,128]{2,1,0:T(8,128)} %pos_ref.3), channel_id=1, source_target_pairs={{0,1},{1,0},{2,3},{3,2},{4,5},{5,4},{6,7},{7,6},{8,9},{9,8},{10,11... | collective-permute-start | bytes 36872 | tf_op jit(solution)/shard_map/ppermute | solution.py:597
  2.3 19.6 %collective-permute-start.1 = (f32[8,256]{1,0:T(8,128)S(1)}, f32[8,256]{1,0:T(8,128)S(1)}, u32[]{:S(2)}, u32[]{:S(2)}) collective-permute-start(f32[8,256]{1,0:T(8,128)S(1)} %convert_reduce_fusion.sum_a_ref), channel_id=1, source_target_pairs={{0,1},{1,0},{2,3},{3,2},{4,5},{5,4},{6,7},{7,6},{8,9},{9,8},{10,11... | collective-permute-start | bytes 24584 | tf_op jit(solution)/shard_map/ppermute | solution.py:597
  2.4 24.3 %copy-start = (f32[3,8,128]{2,1,0:T(8,128)S(1)}, f32[3,8,128]{2,1,0:T(8,128)}, u32[]{:S(2)}) copy-start(f32[3,8,128]{2,1,0:T(8,128)} %pos_ref.3) | copy-start | bytes 36868
  25.2 1.5 %collective-permute-start.2 = (f32[160,256]{1,0:T(8,128)S(1)}, f32[160,256]{1,0:T(8,128)S(1)}, u32[]{:S(2)}, u32[]{:S(2)}) collective-permute-start(f32[160,256]{1,0:T(8,128)S(1)} %get-tuple-element.47), channel_id=1, source_target_pairs={{0,1},{1,0},{2,3},{3,2},{4,5},{5,4},{6,7},{7,6},{8,9},{9,8},{10,11... | collective-permute-start | bytes 491528 | tf_op jit(solution)/shard_map/ppermute | solution.py:597
  26.8 5.5 %collective-permute-start.3 = (bf16[184,256]{1,0:T(8,128)(2,1)S(1)}, bf16[184,256]{1,0:T(8,128)(2,1)S(1)}, u32[]{:S(2)}, u32[]{:S(2)}) collective-permute-start(bf16[184,256]{1,0:T(8,128)(2,1)S(1)} %get-tuple-element.49.own_ref), channel_id=1, source_target_pairs={{0,2},{1,5},{2,0},{3,7},{4,6},{5,1},{6,4},{7,3},{8,10},{9,13},{10,... | collective-permute-start | bytes 282632 | tf_op jit(solution)/shard_map/ppermute | solution.py:627
  32.3 5.6 %collective-permute-start.4 = (bf16[208,256]{1,0:T(8,128)(2,1)S(1)}, bf16[208,256]{1,0:T(8,128)(2,1)S(1)}, u32[]{:S(2)}, u32[]{:S(2)}) collective-permute-start(bf16[208,256]{1,0:T(8,128)(2,1)S(1)} %mix.2.own_ref), channel_id=1, source_target_pairs={{0,4},{1,9},{2,6},{3,11},{4,0},{5,13},{6,2},{7,15},{8,12},{9,1},{1... | collective-permute-start | bytes 319496 | tf_op jit(solution)/shard_map/ppermute | solution.py:627
  37.9 5.9 %collective-permute-start.5 = (bf16[256,256]{1,0:T(8,128)(2,1)S(1)}, bf16[256,256]{1,0:T(8,128)(2,1)S(1)}, u32[]{:S(2)}, u32[]{:S(2)}) collective-permute-start(bf16[256,256]{1,0:T(8,128)(2,1)S(1)} %mix.3.refs_1_.own_ref), channel_id=1, source_target_pairs={{0,8},{1,3},{2,10},{3,1},{4,12},{5,7},{6,14},{7,5},{8,0},{9,11},{1... | collective-permute-start | bytes 393224 | tf_op jit(solution)/shard_map/ppermute | solution.py:627
  43.9 1.6 %collective-permute-start.6 = (f32[152,256]{1,0:T(8,128)S(1)}, f32[152,256]{1,0:T(8,128)S(1)}, u32[]{:S(2)}, u32[]{:S(2)}) collective-permute-start(f32[152,256]{1,0:T(8,128)S(1)} %last_mix.1.refs_1_), channel_id=1, source_target_pairs={{0,1},{1,0},{2,3},{3,2},{4,5},{5,4},{6,7},{7,6},{8,9},{9,8},{10,11... | collective-permute-start | bytes 466952 | tf_op jit(solution)/shard_map/ppermute | solution.py:597

commit v5 on v4

--- a/solution.py
+++ b/solution.py
@@ -74,7 +74,7 @@
 def pair_steps(
     own_ref, other_ref, ew_ref, eb_ref, pw_ref, pb_ref,
     pooled_ref, h_ref, g_ref, ready, weigh,
-    embed_mat, block_mat, a_rows, feat_a, feat_b, bias_row, columns, misc_all,
+    embed_mat, block_mat, a_rows, feat_a, feat_b, bias_row,
     pre_a, pre_b, act_a, act_b, in_a, in_b, in_c, in_d, slope_a, slope_b, sum_a, sum_b, sum_c, sum_d,
 ):
     count = own_ref.shape[1]
@@ -82,27 +82,37 @@
     pre, acts, slopes = (pre_a, pre_b), (act_a, act_b), (slope_a, slope_b)
     ins, sums = (in_a, in_b, in_c, in_d), (sum_a, sum_b, sum_c, sum_d)
 
-    def features(feat, at, first, size):
+    def features(feat, at):
+        size = 256
+        points = [
+            jnp.concatenate([ref[c, pl.ds(at, 1), :] for ref in (own_ref, other_ref)], axis=1)
+            for c in range(3)
+        ]
+        columns = jnp.concatenate(points + [jnp.zeros((5, 256), f32)], axis=0).T
+        misc = jnp.zeros((24, 256), f32)
+        row = iota((24, 256), 0)
+        for c in range(3):
+            s1, s2, s3 = split3(points[c])
+            for p, piece in enumerate((s1, s1, s1, s2, s2, s3)):
+                misc = jnp.where(row == 6 * c + p, piece, misc)
+        zeros = jnp.zeros((64, 256), f32)
+        misc = jnp.concatenate([zeros, misc, zeros[0:40]], axis=0).T
         lane = iota((size, 128), 1)
         square = jnp.ones((size, 128), f32)
         for c in range(3):
-            spread = jnp.broadcast_to(
-                columns[at, first : first + size, c : c + 1], (size, 128)
-            )
+            spread = jnp.broadcast_to(columns[:, c : c + 1], (size, 128))
             offset = spread - own_ref[c, pl.ds(at, 1), :]
             square = square + offset * offset
         radial = square * lax.rsqrt(square)
-        misc = misc_all[at, first : first + size, :]
         high = radial.astype(bf16).astype(f32)
         low = radial - high
         high_turned = pltpu.roll(high, 64, 1)
         low_turned = pltpu.roll(low, 64, 1)
         left = lane < 64
-        rows = slice(first, first + size)
-        feat[0, rows, :128] = jnp.where(left, high, low_turned).astype(bf16)
-        feat[0, rows, 128:] = jnp.where(left, high, misc).astype(bf16)
-        feat[1, rows, :128] = jnp.where(left, high_turned, low).astype(bf16)
-        feat[1, rows, 128:] = jnp.where(left, high_turned, misc).astype(bf16)
+        feat[0, :, :128] = jnp.where(left, high, low_turned).astype(bf16)
+        feat[0, :, 128:] = jnp.where(left, high, misc).astype(bf16)
+        feat[1, :, :128] = jnp.where(left, high_turned, low).astype(bf16)
+        feat[1, :, 128:] = jnp.where(left, high_turned, misc).astype(bf16)
 
     wide = jnp.concatenate([ew_ref[...]] * 8, axis=1)
     w1, w2, w3 = split3(wide)
@@ -146,28 +156,7 @@
             )
             total = total + point * wide[c : c + 1, :]
         a_rows[:, g * 256 : (g + 1) * 256] = total
-    blank = jnp.zeros((5, 256), f32)
-    for at in range(count):
-        stacked = jnp.concatenate(
-            [
-                jnp.concatenate(
-                    [own_ref[c, at : at + 1, :], other_ref[c, at : at + 1, :]], axis=1
-                )
-                for c in range(3)
-            ]
-            + [blank],
-            axis=0,
-        )
-        columns[at] = stacked.T
-        spread = jnp.zeros((24, 256), f32)
-        row = iota((24, 256), 0)
-        for c in range(3):
-            s1, s2, s3 = split3(stacked[c : c + 1, :])
-            for p, piece in enumerate((s1, s1, s1, s2, s2, s3)):
-                spread = jnp.where(row == 6 * c + p, piece, spread)
-        zeros = jnp.zeros((64, 256), f32)
-        misc_all[at] = jnp.concatenate([zeros, spread, zeros[0:40]], axis=0).T
-    features(feat_a, 0, 0, 256)
+    features(feat_a, 0)
     diagonal = iota((8, 256), 0) == iota((8, 256), 1) // 32
     block = iota((32, 256), 1) // 32
 
@@ -213,17 +202,20 @@
                     stage(place - lag)
             if started and place % 16 == 0:
                 upcoming = jnp.minimum(2 * step + place // 16 + 1, count - 1)
-                features(feats[1 - place // 16], upcoming, 0, 256)
+                features(feats[1 - place // 16], upcoming)
 
     turns = count // 2
 
     def body(step, carry):
-        weigh(step)
+        pl.when(step == 1)(ready)
+        pl.when(step >= 1)(lambda: weigh(step - 1))
         turn(step, range(32), 32)
         return carry
 
-    ready()
     lax.fori_loop(0, turns, body, 0)
+    if turns == 1:
+        ready()
+    weigh(turns - 1)
     turn(turns, range(4), 0)
 
 
@@ -250,8 +242,6 @@
             pltpu.VMEM((2, 256, 256), bf16),
             pltpu.VMEM((2, 256, 256), bf16),
             pltpu.VMEM((8, 256), f32),
-            pltpu.VMEM((count, 256, 8), f32),
-            pltpu.VMEM((count, 256, 128), f32),
         ]
         + [pltpu.VMEM((256, 256), f32)] * 4
         + [pltpu.VMEM((256, 256), bf16)] * 6
@@ -358,7 +348,7 @@
         in_specs=[SMEM] + [VMEM] * 11,
         out_specs=[VMEM] * 5,
         out_shape=[
-            jax.ShapeDtypeStruct((count * rows, width), bf16),
+            pltpu.VMEM((count * rows, width), bf16),
             pltpu.VMEM((count * rows, width), bf16),
             pltpu.VMEM((HALF + count, width), f32),
             pltpu.VMEM((HALF + count, width), f32),
@@ -452,7 +442,7 @@
 
 def back_kernel(
     cot_ref, pre_ref, upd_ref, col_ref, pos_ref, ow_ref, mw_ref, dw_ref,
-    grad_ref, link_ref, last_ref,
+    grad_ref, out_ref, link_ref, last_ref,
 ):
     count = col_ref.shape[0]
     back = dot(col_ref[...], mw_ref[...].astype(f32), 1, 1, HIGH) * (1.0 / 256)
@@ -462,6 +452,7 @@
         grad = cot_ref[at, :].astype(f32) + dot(pre_ref[at, :], ow_ref[...], 1, 1)
         grad_ref[at, :] = (grad + back[s : s + 1, :]).astype(bf16)
         drifts.append(dot(dw_ref[...], upd_ref[at, :], 1, 1))
+        out_ref[at, :] = upd_ref[at, :]
     for s in range(count):
         here = [-pos_ref[c, s : s + 1, :] - step_tau * drifts[s][c : c + 1, :] for c in range(3)]
         if s < count - 1:
@@ -474,12 +465,13 @@
 
 
 def back_call(cot, pre, updated, col, pos, ow, mw, dw):
-    args = (near(cot), near(pre), far(updated), near(col), far(pos), near(ow), near(mw), far(dw))
+    args = (near(cot), near(pre), near(updated), near(col), far(pos), near(ow), near(mw), far(dw))
     return pl.pallas_call(
         back_kernel,
         in_specs=[VMEM] * len(args),
-        out_specs=[VMEM] * 3,
+        out_specs=[VMEM] * 4,
         out_shape=[
+            jax.ShapeDtypeStruct(cot.shape, bf16),
             jax.ShapeDtypeStruct(cot.shape, bf16),
             pltpu.VMEM((col.shape[0], 128), f32),
             pltpu.VMEM((8, 128), f32),
@@ -616,7 +608,7 @@
         pool_near, mean_near, one_bias,
     )
     state, col_total = first_call(keep, swap(send), mean_rows, positions)
-    hidden_grad, link, last = back_call(
+    hidden_grad, updated, link, last = back_call(
         cot_near.reshape(pre.shape), pre, updated, col_total, positions, one_near,
         mean_near, drift_weight,
     )

time: 47 us -> 45.9 us (0.977)
  Pallas kernels: 28 us -> 26.5 us
    pallas_call x1, Pallas kernels: 3.33 us -> 2.53 us  [one_call(): pl.pallas_call(one_kernel, in_specs=[SMEM] + [VMEM] * 11, out_specs=[VMEM...]
  transfers between devices with their start and end apart: 7 -> 7, of which waited for: 4 -> 4; matrix products, arithmetic and copies ran while one was open for 3% -> 3% of each run, Pallas kernels for 51% -> 50%
where the time goes in v5:
time: 45.9 us; the launch traced here: 45.3 us
  Pallas kernels  26.5 us (58%)
  starting transfers between devices  8.75 us (19%)
  waiting for transfers between devices  8.21 us (18%)
  other arithmetic  1.2 us (3%)
  between operations  0.69 us (2%)
    pallas_call x1, Pallas kernels, pair_call(): pl.pallas_call(pair_kernel, in_specs=[VMEM] * 6 + [pl.BlockSpec(memory_sp...  19.1 us
    ppermute x3, starting transfers between devices, local(): came = lax.ppermute(state, ('slices', 'ering'), pairs)  7.52 us
    ppermute x3, waiting for transfers between devices, local(): came = lax.ppermute(state, ('slices', 'ering'), pairs)  7.17 us
    pallas_call x1, Pallas kernels, one_call(): pl.pallas_call(one_kernel, in_specs=[SMEM] + [VMEM] * 11, out_specs=[VMEM...  2.53 us
    pallas_call x1, Pallas kernels, back_call(): pl.pallas_call(back_kernel, in_specs=[VMEM] * len(args), out_specs=[VMEM]...  2.32 us
    pallas_call x1, Pallas kernels, mean_call(): pl.pallas_call(body, in_specs=[SMEM] + [VMEM] * 4, out_specs=[VMEM] * 2,...  1.48 us
    ppermute x4, starting transfers between devices, swap(): return lax.ppermute(array, 'ering', [(0, 1), (1, 0)])  1.23 us
    reduce_sum x1, other arithmetic, local(): part_sum = jnp.sum(hidden.astype(f32), axis=1)  1.12 us
  transfers between devices with their start and end apart: 7, of which 4 were waited for; matrix products, arithmetic and copies ran while one was open for 3% of the time, Pallas kernels for 50%

profile of v5, /device:TPU:0, one launch (start us, length us, event | category | flops | bytes accessed | tf_op | source)
XLA Modules:
  0.0 45.3 jit_solution(11482138254712173204)
XLA Ops:
  0.6 0.5 %collective-permute-start = (f32[3,8,128]{2,1,0:T(8,128)}, f32[3,8,128]{2,1,0:T(8,128)S(1)}, u32[]{:S(2)}, u32[]{:S(2)}) collective-permute-start(f32[3,8,128]{2,1,0:T(8,128)} %pos_ref.3), channel_id=1, source_target_pairs={{0,1},{1,0},{2,3},{3,2},{4,5},{5,4},{6,7},{7,6},{8,9},{9,8},{10,11... | collective-permute-start | bytes 36872 | tf_op jit(solution)/shard_map/ppermute | solution.py:589
  1.1 1.1 %convert_reduce_fusion.sum_a_ref = f32[8,256]{1,0:T(8,128)S(1)} fusion(bf16[8,128,256]{2,1,0:T(8,128)(2,1)} %refs_0_.1), kind=kLoop, calls=%fused_computation | loop fusion | flops 522240 | bytes 532480 | tf_op jit(solution)/shard_map/reduce_sum | solution.py:600
  2.3 0.1 collective-permute-start.1
  2.4 0.0 collective-permute-done.other_ref
  2.4 0.0 copy-start
  2.4 19.1 %pair_stage.1 = (f32[8,128,256]{2,1,0:T(8,128)S(1)}, f32[8,16,256]{2,1,0:T(8,128)S(1)}, f32[8,512,256]{2,1,0:T(8,128)S(1)}, f32[8,128,256]{2,1,0:T(8,128)S(1)}, ...) custom-call(f32[3,8,128]{2,1,0:T(8,128)} %pos_ref.3, ...), custom_call_target="tpu_custom_call" | custom-call | tf_op jit(solution)/shard_map/pair_stage/pallas_call | solution.py:227
  21.5 0.0 collective-permute-done.1.sum_b_ref
  21.5 2.5 %one_stage.1 = (bf16[1024,256]{1,0:T(8,128)(2,1)S(1)}, bf16[1024,256]{1,0:T(8,128)(2,1)S(1)}, f32[160,256]{1,0:T(8,128)S(1)}, f32[160,256]{1,0:T(8,128)S(1)}, bf16[8,256]{1,0:T(8,128)(2,1)S(1)}) custom-call(s32[1]{0:T(128)} %bitcast.4.core_ref.refs_0_, bf16[8,128,256]{2,1,0:T(8,128)(2,1)S(1)} %get-tuple-element.39.hid_ref, ...), custom_call_target="tpu_custom_call" | custom-call | tf_op jit(solution)/shard_map/one_stage/pallas_call | solution.py:346
  24.0 0.5 %collective-permute-start.2 = (f32[160,256]{1,0:T(8,128)S(1)}, f32[160,256]{1,0:T(8,128)S(1)}, u32[]{:S(2)}, u32[]{:S(2)}) collective-permute-start(f32[160,256]{1,0:T(8,128)S(1)} %get-tuple-element.49), channel_id=1, source_target_pairs={{0,1},{1,0},{2,3},{3,2},{4,5},{5,4},{6,7},{7,6},{8,9},{9,8},{10,11... | collective-permute-start | bytes 491528 | tf_op jit(solution)/shard_map/ppermute | solution.py:589
  24.6 1.0 %collective-permute-done.2.came_ref = f32[160,256]{1,0:T(8,128)S(1)} collective-permute-done((f32[160,256]{1,0:T(8,128)S(1)}, f32[160,256]{1,0:T(8,128)S(1)}, u32[]{:S(2)}, u32[]{:S(2)}) %collective-permute-start.2) | collective-permute-done | bytes 163872 | tf_op jit(solution)/shard_map/ppermute | solution.py:589
  25.6 0.0 copy-done
  25.6 2.9 %collective-permute-start.3 = (bf16[184,256]{1,0:T(8,128)(2,1)S(1)}, bf16[184,256]{1,0:T(8,128)(2,1)S(1)}, u32[]{:S(2)}, u32[]{:S(2)}) collective-permute-start(bf16[184,256]{1,0:T(8,128)(2,1)S(1)} %get-tuple-element.54.own_ref), channel_id=1, source_target_pairs={{0,2},{1,5},{2,0},{3,7},{4,6},{5,1},{6,4},{7,3},{8,10},{9,13},{10,... | collective-permute-start | bytes 282632 | tf_op jit(solution)/shard_map/ppermute | solution.py:619
  28.5 2.6 %collective-permute-done.3.came_ref = bf16[184,256]{1,0:T(8,128)(2,1)S(1)} collective-permute-done((bf16[184,256]{1,0:T(8,128)(2,1)S(1)}, bf16[184,256]{1,0:T(8,128)(2,1)S(1)}, u32[]{:S(2)}, u32[]{:S(2)}) %collective-permute-start.3) | collective-permute-done | bytes 94240 | tf_op jit(solution)/shard_map/ppermute | solution.py:619
  31.1 2.2 %collective-permute-start.4 = (bf16[208,256]{1,0:T(8,128)(2,1)S(1)}, bf16[208,256]{1,0:T(8,128)(2,1)S(1)}, u32[]{:S(2)}, u32[]{:S(2)}) collective-permute-start(bf16[208,256]{1,0:T(8,128)(2,1)S(1)} %mix.2.own_ref), channel_id=1, source_target_pairs={{0,4},{1,9},{2,6},{3,11},{4,0},{5,13},{6,2},{7,15},{8,12},{9,1},{1... | collective-permute-start | bytes 319496 | tf_op jit(solution)/shard_map/ppermute | solution.py:619
  33.3 3.4 %collective-permute-done.4.came_ref = bf16[208,256]{1,0:T(8,128)(2,1)S(1)} collective-permute-done((bf16[208,256]{1,0:T(8,128)(2,1)S(1)}, bf16[208,256]{1,0:T(8,128)(2,1)S(1)}, u32[]{:S(2)}, u32[]{:S(2)}) %collective-permute-start.4) | collective-permute-done | bytes 106528 | tf_op jit(solution)/shard_map/ppermute | solution.py:619
  36.8 2.4 %collective-permute-start.5 = (bf16[256,256]{1,0:T(8,128)(2,1)S(1)}, bf16[256,256]{1,0:T(8,128)(2,1)S(1)}, u32[]{:S(2)}, u32[]{:S(2)}) collective-permute-start(bf16[256,256]{1,0:T(8,128)(2,1)S(1)} %mix.3.refs_1_.own_ref), channel_id=1, source_target_pairs={{0,8},{1,3},{2,10},{3,1},{4,12},{5,7},{6,14},{7,5},{8,0},{9,11},{1... | collective-permute-start | bytes 393224 | tf_op jit(solution)/shard_map/ppermute | solution.py:619
  39.2 2.3 %hidden_back.1 = (bf16[1024,256]{1,0:T(8,128)(2,1)}, bf16[1024,256]{1,0:T(8,128)(2,1)}, f32[8,128]{1,0:T(8,128)S(1)}, f32[8,128]{1,0:T(8,128)S(1)}) custom-call(bf16[1024,256]{1,0:T(8,128)(2,1)S(1)} %bitcast.10, bf16[1024,256]{1,0:T(8,128)(2,1)S(1)} %get-tuple-element.46.pre_ref, bf16[1024,256]{1,0:T(8,128)(2,1)S(1)} %get-tuple-element.47.upd_ref, ...), custom_call_target="tpu_custom_call" | custom-call | tf_op jit(solution)/shard_map/hidden_back/pallas_call | solution.py:469
  41.5 1.2 %collective-permute-done.5.refs_2_.came_ref = bf16[256,256]{1,0:T(8,128)(2,1)S(1)} collective-permute-done((bf16[256,256]{1,0:T(8,128)(2,1)S(1)}, bf16[256,256]{1,0:T(8,128)(2,1)S(1)}, u32[]{:S(2)}, u32[]{:S(2)}) %collective-permute-start.5) | collective-permute-done | bytes 131104 | tf_op jit(solution)/shard_map/ppermute | solution.py:619
  42.7 0.1 collective-permute-start.6
  42.8 0.1 pad_add_fusion.refs_0_
  42.9 1.5 %mean_and_link.1 = (f32[256,256]{1,0:T(8,128)}, f32[8,128]{1,0:T(8,128)}) custom-call(s32[2]{0:T(128)S(1)} %pad_add_fusion.refs_0_, bf16[256,256]{1,0:T(8,128)(2,1)S(1)} %mix.3.refs_1_.own_ref, bf16[256,256]{1,0:T(8,128)(2,1)S(1)} %collective-permute-done.5.refs_2_.came_ref, f32[8,128]{1,0:T(8,128)S(1)} %get-tuple-element.60.refs_3_, ...), custom_call_target="tpu_custom_call" | custom-call | tf_op jit(solution)/shard_map/mean_and_link/pallas_call | solution.py:517
  44.4 0.0 collective-permute-done.6.refs_2_
  44.4 0.9 %unpack.1 = (f32[256,256]{1,0:T(8,128)}, f32[32,256]{1,0:T(8,128)}, f32[32,32]{1,0:T(8,128)}, f32[1,32]{1,0:T(1,128)}) custom-call(s32[1]{0:T(128)} %bitcast.4.core_ref.refs_0_, f32[152,256]{1,0:T(8,128)S(1)} %last_mix.1.refs_1_, f32[152,256]{1,0:T(8,128)S(1)} %collective-permute-done.6.refs_2_), custom_call_target="tpu_custom_call" | custom-call | tf_op jit(solution)/shard_map/unpack/pallas_call | solution.py:562
  (4 shorter events, 0.1 us)
Async XLA Ops:
  0.6 1.8 %collective-permute-start = (f32[3,8,128]{2,1,0:T(8,128)}, f32[3,8,128]{2,1,0:T(8,128)S(1)}, u32[]{:S(2)}, u32[]{:S(2)}) collective-permute-start(f32[3,8,128]{2,1,0:T(8,128)} %pos_ref.3), channel_id=1, source_target_pairs={{0,1},{1,0},{2,3},{3,2},{4,5},{5,4},{6,7},{7,6},{8,9},{9,8},{10,11... | collective-permute-start | bytes 36872 | tf_op jit(solution)/shard_map/ppermute | solution.py:589
  2.3 19.2 %collective-permute-start.1 = (f32[8,256]{1,0:T(8,128)S(1)}, f32[8,256]{1,0:T(8,128)S(1)}, u32[]{:S(2)}, u32[]{:S(2)}) collective-permute-start(f32[8,256]{1,0:T(8,128)S(1)} %convert_reduce_fusion.sum_a_ref), channel_id=1, source_target_pairs={{0,1},{1,0},{2,3},{3,2},{4,5},{5,4},{6,7},{7,6},{8,9},{9,8},{10,11... | collective-permute-start | bytes 24584 | tf_op jit(solution)/shard_map/ppermute | solution.py:589
  2.4 23.2 %copy-start = (f32[3,8,128]{2,1,0:T(8,128)S(1)}, f32[3,8,128]{2,1,0:T(8,128)}, u32[]{:S(2)}) copy-start(f32[3,8,128]{2,1,0:T(8,128)} %pos_ref.3) | copy-start | bytes 36868
  24.0 1.6 %collective-permute-start.2 = (f32[160,256]{1,0:T(8,128)S(1)}, f32[160,256]{1,0:T(8,128)S(1)}, u32[]{:S(2)}, u32[]{:S(2)}) collective-permute-start(f32[160,256]{1,0:T(8,128)S(1)} %get-tuple-element.49), channel_id=1, source_target_pairs={{0,1},{1,0},{2,3},{3,2},{4,5},{5,4},{6,7},{7,6},{8,9},{9,8},{10,11... | collective-permute-start | bytes 491528 | tf_op jit(solution)/shard_map/ppermute | solution.py:589
  25.6 5.5 %collective-permute-start.3 = (bf16[184,256]{1,0:T(8,128)(2,1)S(1)}, bf16[184,256]{1,0:T(8,128)(2,1)S(1)}, u32[]{:S(2)}, u32[]{:S(2)}) collective-permute-start(bf16[184,256]{1,0:T(8,128)(2,1)S(1)} %get-tuple-element.54.own_ref), channel_id=1, source_target_pairs={{0,2},{1,5},{2,0},{3,7},{4,6},{5,1},{6,4},{7,3},{8,10},{9,13},{10,... | collective-permute-start | bytes 282632 | tf_op jit(solution)/shard_map/ppermute | solution.py:619
  31.1 5.6 %collective-permute-start.4 = (bf16[208,256]{1,0:T(8,128)(2,1)S(1)}, bf16[208,256]{1,0:T(8,128)(2,1)S(1)}, u32[]{:S(2)}, u32[]{:S(2)}) collective-permute-start(bf16[208,256]{1,0:T(8,128)(2,1)S(1)} %mix.2.own_ref), channel_id=1, source_target_pairs={{0,4},{1,9},{2,6},{3,11},{4,0},{5,13},{6,2},{7,15},{8,12},{9,1},{1... | collective-permute-start | bytes 319496 | tf_op jit(solution)/shard_map/ppermute | solution.py:619
  36.8 5.9 %collective-permute-start.5 = (bf16[256,256]{1,0:T(8,128)(2,1)S(1)}, bf16[256,256]{1,0:T(8,128)(2,1)S(1)}, u32[]{:S(2)}, u32[]{:S(2)}) collective-permute-start(bf16[256,256]{1,0:T(8,128)(2,1)S(1)} %mix.3.refs_1_.own_ref), channel_id=1, source_target_pairs={{0,8},{1,3},{2,10},{3,1},{4,12},{5,7},{6,14},{7,5},{8,0},{9,11},{1... | collective-permute-start | bytes 393224 | tf_op jit(solution)/shard_map/ppermute | solution.py:619
  42.7 1.6 %collective-permute-start.6 = (f32[152,256]{1,0:T(8,128)S(1)}, f32[152,256]{1,0:T(8,128)S(1)}, u32[]{:S(2)}, u32[]{:S(2)}) collective-permute-start(f32[152,256]{1,0:T(8,128)S(1)} %last_mix.1.refs_1_), channel_id=1, source_target_pairs={{0,1},{1,0},{2,3},{3,2},{4,5},{5,4},{6,7},{7,6},{8,9},{9,8},{10,11... | collective-permute-start | bytes 466952 | tf_op jit(solution)/shard_map/ppermute | solution.py:589

commit v6 on v5

--- a/solution.py
+++ b/solution.py
@@ -305,12 +305,15 @@
             for g in range(32):
                 part = g_ref[2 * n + g // 16, g % 16 * 32 : (g % 16 + 1) * 32, :]
                 pair_total = pair_total + part * back_all[n, g : g + 1, :]
-    fold = jnp.where(iota((256, 256), 0) % 32 == iota((256, 256), 1) % 32, 1.0, 0.0)
     pool = pool_total[0:32]
     for q in range(1, 8):
         pool = pool + pool_total[q * 32 : (q + 1) * 32]
     bias_one = jnp.broadcast_to(jnp.sum(bias_total, axis=0, keepdims=True), (8, 256))
-    folded = dot(jnp.concatenate([pair_total, bias_one], axis=0), fold, 1, 0, HIGH)
+    folded = jnp.concatenate([pair_total, bias_one], axis=0)
+    folded = folded[:, 0:128] + folded[:, 128:]
+    folded = folded + pltpu.roll(folded, 64, 1)
+    folded = folded + pltpu.roll(folded, 32, 1)
+    folded = jnp.concatenate([folded, folded], axis=1)
     picked = jnp.where(iota((32, 256), 0) % 8 == iota((32, 256), 1) // 32, folded[0:32], 0.0)
     packed = jnp.sum(picked.reshape(4, 8, 256), axis=1)
     small = jnp.concatenate([packed, folded[32:36]], axis=0)
@@ -482,13 +485,13 @@
 
 
 def mean_kernel(
-    info_ref, own_ref, came_ref, link_ref, last_ref,
+    place_ref, core_ref, own_ref, came_ref, link_ref, last_ref,
     mean_ref, out_link_ref,
     mean_all, col_all, border, *, scale, count, masks,
 ):
     stride = 2 * count + 8
     half = (own_ref.shape[0] - SENT) // stride
-    place, core = info_ref[0], info_ref[1]
+    place, core = place_ref[0], core_ref[0]
     for d in range(2 * half):
         owner = place ^ jnp.where(core == 0, masks[0][d], masks[1][d])
         ref = own_ref if d < half else came_ref
@@ -507,8 +510,8 @@
     out_link_ref[count - 1 : count, :] = jnp.where(place == 2 * half - 1, 0.0, total)
 
 
-def mean_call(info, own, came, link, last, scale, count, masks):
-    args = (info, near(own), near(came), near(link), near(last))
+def mean_call(place, core, own, came, link, last, scale, count, masks):
+    args = (place, core, near(own), near(came), near(link), near(last))
     devices = len(masks[0])
 
     def body(*refs):
@@ -516,7 +519,7 @@
 
     return pl.pallas_call(
         body,
-        in_specs=[SMEM] + [VMEM] * 4,
+        in_specs=[SMEM] * 2 + [VMEM] * 4,
         out_specs=[VMEM] * 2,
         out_shape=[
             jax.ShapeDtypeStruct((256, 256), f32),
@@ -593,7 +596,7 @@
         [sum(((d >> t) & 1) << orders[e][t] for t in range(bits)) for d in range(slices)]
         for e in range(2)
     ]
-    info = jnp.stack([place, core])
+    place = place.reshape(1)
     core = core.reshape(1)
 
     other_pos = swap(positions)
@@ -623,7 +626,7 @@
             state = mix_call(state, came)
     total = last_call(state, came)
     other_total = swap(total)
-    mean_grad, link_terms = mean_call(info, state, came, link, last, scale, count, masks)
+    mean_grad, link_terms = mean_call(place, core, state, came, link, last, scale, count, masks)
     one_grad, pool_grad, pair_grad, bias_grad = end_call(core, total, other_total, scale)
     return (
         updated.reshape(hidden.shape),

time: 45.9 us -> 45.2 us (0.985)
  Pallas kernels: 26.5 us -> 25.7 us
    pallas_call x1, Pallas kernels: 1.48 us -> 0.94 us  [mean_call(): pl.pallas_call(body, in_specs=[SMEM] * 2 + [VMEM] * 4, out_specs=[VMEM] *...]
  transfers between devices with their start and end apart: 7 -> 7, of which waited for: 4 -> 5; matrix products, arithmetic and copies ran while one was open for 3% -> 3% of each run, Pallas kernels for 50% -> 50%
where the time goes in v6:
time: 45.2 us; the launch traced here: 44.9 us
  Pallas kernels  25.7 us (57%)
  starting transfers between devices  8.76 us (19%)
  waiting for transfers between devices  8.63 us (19%)
  other arithmetic  1.12 us (2%)
  between operations  0.69 us (2%)
    pallas_call x1, Pallas kernels, pair_call(): pl.pallas_call(pair_kernel, in_specs=[VMEM] * 6 + [pl.BlockSpec(memory_sp...  19.1 us
    ppermute x3, starting transfers between devices, local(): came = lax.ppermute(state, ('slices', 'ering'), pairs)  7.52 us
    ppermute x3, waiting for transfers between devices, local(): came = lax.ppermute(state, ('slices', 'ering'), pairs)  7.17 us
    pallas_call x1, Pallas kernels, one_call(): pl.pallas_call(one_kernel, in_specs=[SMEM] + [VMEM] * 11, out_specs=[VMEM...  2.33 us
    pallas_call x1, Pallas kernels, back_call(): pl.pallas_call(back_kernel, in_specs=[VMEM] * len(args), out_specs=[VMEM]...  2.32 us
    ppermute x4, waiting for transfers between devices, swap(): return lax.ppermute(array, 'ering', [(0, 1), (1, 0)])  1.46 us
    ppermute x4, starting transfers between devices, swap(): return lax.ppermute(array, 'ering', [(0, 1), (1, 0)])  1.24 us
    reduce_sum x1, other arithmetic, local(): part_sum = jnp.sum(hidden.astype(f32), axis=1)  1.12 us
  transfers between devices with their start and end apart: 7, of which 5 were waited for; matrix products, arithmetic and copies ran while one was open for 3% of the time, Pallas kernels for 50%

profile of v6, /device:TPU:0, one launch (start us, length us, event | category | flops | bytes accessed | tf_op | source)
XLA Modules:
  0.0 44.9 jit_solution(8866714033210676871)
XLA Ops:
  0.6 0.5 %collective-permute-start = (f32[3,8,128]{2,1,0:T(8,128)}, f32[3,8,128]{2,1,0:T(8,128)S(1)}, u32[]{:S(2)}, u32[]{:S(2)}) collective-permute-start(f32[3,8,128]{2,1,0:T(8,128)} %pos_ref.3), channel_id=1, source_target_pairs={{0,1},{1,0},{2,3},{3,2},{4,5},{5,4},{6,7},{7,6},{8,9},{9,8},{10,11... | collective-permute-start | bytes 36872 | tf_op jit(solution)/shard_map/ppermute | solution.py:592
  1.1 1.1 %convert_reduce_fusion.sum_a_ref = f32[8,256]{1,0:T(8,128)S(1)} fusion(bf16[8,128,256]{2,1,0:T(8,128)(2,1)} %refs_0_.1), kind=kLoop, calls=%fused_computation | loop fusion | flops 522240 | bytes 532480 | tf_op jit(solution)/shard_map/reduce_sum | solution.py:603
  2.3 0.1 collective-permute-start.1
  2.4 0.0 collective-permute-done.other_ref
  2.4 0.0 copy-start
  2.4 19.1 %pair_stage.1 = (f32[8,128,256]{2,1,0:T(8,128)S(1)}, f32[8,16,256]{2,1,0:T(8,128)S(1)}, f32[8,512,256]{2,1,0:T(8,128)S(1)}, f32[8,128,256]{2,1,0:T(8,128)S(1)}, ...) custom-call(f32[3,8,128]{2,1,0:T(8,128)} %pos_ref.3, ...), custom_call_target="tpu_custom_call" | custom-call | tf_op jit(solution)/shard_map/pair_stage/pallas_call | solution.py:227
  21.5 0.0 collective-permute-done.1.sum_b_ref
  21.5 2.3 %one_stage.1 = (bf16[1024,256]{1,0:T(8,128)(2,1)S(1)}, bf16[1024,256]{1,0:T(8,128)(2,1)S(1)}, f32[160,256]{1,0:T(8,128)S(1)}, f32[160,256]{1,0:T(8,128)S(1)}, bf16[8,256]{1,0:T(8,128)(2,1)S(1)}) custom-call(s32[1]{0:T(128)} %bitcast.4.core_ref.refs_1_.refs_0_, bf16[8,128,256]{2,1,0:T(8,128)(2,1)S(1)} %get-tuple-element.39.hid_ref, ...), custom_call_target="tpu_custom_call" | custom-call | tf_op jit(solution)/shard_map/one_stage/pallas_call | solution.py:349
  23.8 0.5 %collective-permute-start.2 = (f32[160,256]{1,0:T(8,128)S(1)}, f32[160,256]{1,0:T(8,128)S(1)}, u32[]{:S(2)}, u32[]{:S(2)}) collective-permute-start(f32[160,256]{1,0:T(8,128)S(1)} %get-tuple-element.49), channel_id=1, source_target_pairs={{0,1},{1,0},{2,3},{3,2},{4,5},{5,4},{6,7},{7,6},{8,9},{9,8},{10,11... | collective-permute-start | bytes 491528 | tf_op jit(solution)/shard_map/ppermute | solution.py:592
  24.4 1.0 %collective-permute-done.2.came_ref = f32[160,256]{1,0:T(8,128)S(1)} collective-permute-done((f32[160,256]{1,0:T(8,128)S(1)}, f32[160,256]{1,0:T(8,128)S(1)}, u32[]{:S(2)}, u32[]{:S(2)}) %collective-permute-start.2) | collective-permute-done | bytes 163872 | tf_op jit(solution)/shard_map/ppermute | solution.py:592
  25.4 0.0 copy-done
  25.4 2.9 %collective-permute-start.3 = (bf16[184,256]{1,0:T(8,128)(2,1)S(1)}, bf16[184,256]{1,0:T(8,128)(2,1)S(1)}, u32[]{:S(2)}, u32[]{:S(2)}) collective-permute-start(bf16[184,256]{1,0:T(8,128)(2,1)S(1)} %get-tuple-element.54.own_ref), channel_id=1, source_target_pairs={{0,2},{1,5},{2,0},{3,7},{4,6},{5,1},{6,4},{7,3},{8,10},{9,13},{10,... | collective-permute-start | bytes 282632 | tf_op jit(solution)/shard_map/ppermute | solution.py:622
  28.3 2.6 %collective-permute-done.3.came_ref = bf16[184,256]{1,0:T(8,128)(2,1)S(1)} collective-permute-done((bf16[184,256]{1,0:T(8,128)(2,1)S(1)}, bf16[184,256]{1,0:T(8,128)(2,1)S(1)}, u32[]{:S(2)}, u32[]{:S(2)}) %collective-permute-start.3) | collective-permute-done | bytes 94240 | tf_op jit(solution)/shard_map/ppermute | solution.py:622
  30.9 2.2 %collective-permute-start.4 = (bf16[208,256]{1,0:T(8,128)(2,1)S(1)}, bf16[208,256]{1,0:T(8,128)(2,1)S(1)}, u32[]{:S(2)}, u32[]{:S(2)}) collective-permute-start(bf16[208,256]{1,0:T(8,128)(2,1)S(1)} %mix.2.own_ref), channel_id=1, source_target_pairs={{0,4},{1,9},{2,6},{3,11},{4,0},{5,13},{6,2},{7,15},{8,12},{9,1},{1... | collective-permute-start | bytes 319496 | tf_op jit(solution)/shard_map/ppermute | solution.py:622
  33.1 3.4 %collective-permute-done.4.came_ref = bf16[208,256]{1,0:T(8,128)(2,1)S(1)} collective-permute-done((bf16[208,256]{1,0:T(8,128)(2,1)S(1)}, bf16[208,256]{1,0:T(8,128)(2,1)S(1)}, u32[]{:S(2)}, u32[]{:S(2)}) %collective-permute-start.4) | collective-permute-done | bytes 106528 | tf_op jit(solution)/shard_map/ppermute | solution.py:622
  36.6 2.4 %collective-permute-start.5 = (bf16[256,256]{1,0:T(8,128)(2,1)S(1)}, bf16[256,256]{1,0:T(8,128)(2,1)S(1)}, u32[]{:S(2)}, u32[]{:S(2)}) collective-permute-start(bf16[256,256]{1,0:T(8,128)(2,1)S(1)} %mix.3.refs_2_.own_ref), channel_id=1, source_target_pairs={{0,8},{1,3},{2,10},{3,1},{4,12},{5,7},{6,14},{7,5},{8,0},{9,11},{1... | collective-permute-start | bytes 393224 | tf_op jit(solution)/shard_map/ppermute | solution.py:622
  39.0 2.3 %hidden_back.1 = (bf16[1024,256]{1,0:T(8,128)(2,1)}, bf16[1024,256]{1,0:T(8,128)(2,1)}, f32[8,128]{1,0:T(8,128)S(1)}, f32[8,128]{1,0:T(8,128)S(1)}) custom-call(bf16[1024,256]{1,0:T(8,128)(2,1)S(1)} %bitcast.10, bf16[1024,256]{1,0:T(8,128)(2,1)S(1)} %get-tuple-element.46.pre_ref, bf16[1024,256]{1,0:T(8,128)(2,1)S(1)} %get-tuple-element.47.upd_ref, ...), custom_call_target="tpu_custom_call" | custom-call | tf_op jit(solution)/shard_map/hidden_back/pallas_call | solution.py:472
  41.3 1.2 %collective-permute-done.5.refs_3_.came_ref = bf16[256,256]{1,0:T(8,128)(2,1)S(1)} collective-permute-done((bf16[256,256]{1,0:T(8,128)(2,1)S(1)}, bf16[256,256]{1,0:T(8,128)(2,1)S(1)}, u32[]{:S(2)}, u32[]{:S(2)}) %collective-permute-start.5) | collective-permute-done | bytes 131104 | tf_op jit(solution)/shard_map/ppermute | solution.py:622
  42.5 0.1 collective-permute-start.6
  42.6 0.9 %mean_and_link.1 = (f32[256,256]{1,0:T(8,128)}, f32[8,128]{1,0:T(8,128)}) custom-call(s32[1]{0:T(128)} %bitcast.8.refs_0_, s32[1]{0:T(128)} %bitcast.4.core_ref.refs_1_.refs_0_, bf16[256,256]{1,0:T(8,128)(2,1)S(1)} %mix.3.refs_2_.own_ref, bf16[256,256]{1,0:T(8,128)(2,1)S(1)} %collective-permute-done.5.refs_3_.came_ref, ...), custom_call_target="tpu_custom_call" | custom-call | tf_op jit(solution)/shard_map/mean_and_link/pallas_call | solution.py:520
  43.6 0.4 collective-permute-done.6.refs_2_
  44.0 0.9 %unpack.1 = (f32[256,256]{1,0:T(8,128)}, f32[32,256]{1,0:T(8,128)}, f32[32,32]{1,0:T(8,128)}, f32[1,32]{1,0:T(1,128)}) custom-call(s32[1]{0:T(128)} %bitcast.4.core_ref.refs_1_.refs_0_, f32[152,256]{1,0:T(8,128)S(1)} %last_mix.1.refs_1_, f32[152,256]{1,0:T(8,128)S(1)} %collective-permute-done.6.refs_2_), custom_call_target="tpu_custom_call" | custom-call | tf_op jit(solution)/shard_map/unpack/pallas_call | solution.py:565
  (4 shorter events, 0.1 us)
Async XLA Ops:
  0.6 1.8 %collective-permute-start = (f32[3,8,128]{2,1,0:T(8,128)}, f32[3,8,128]{2,1,0:T(8,128)S(1)}, u32[]{:S(2)}, u32[]{:S(2)}) collective-permute-start(f32[3,8,128]{2,1,0:T(8,128)} %pos_ref.3), channel_id=1, source_target_pairs={{0,1},{1,0},{2,3},{3,2},{4,5},{5,4},{6,7},{7,6},{8,9},{9,8},{10,11... | collective-permute-start | bytes 36872 | tf_op jit(solution)/shard_map/ppermute | solution.py:592
  2.3 19.2 %collective-permute-start.1 = (f32[8,256]{1,0:T(8,128)S(1)}, f32[8,256]{1,0:T(8,128)S(1)}, u32[]{:S(2)}, u32[]{:S(2)}) collective-permute-start(f32[8,256]{1,0:T(8,128)S(1)} %convert_reduce_fusion.sum_a_ref), channel_id=1, source_target_pairs={{0,1},{1,0},{2,3},{3,2},{4,5},{5,4},{6,7},{7,6},{8,9},{9,8},{10,11... | collective-permute-start | bytes 24584 | tf_op jit(solution)/shard_map/ppermute | solution.py:592
  2.4 23.0 %copy-start = (f32[3,8,128]{2,1,0:T(8,128)S(1)}, f32[3,8,128]{2,1,0:T(8,128)}, u32[]{:S(2)}) copy-start(f32[3,8,128]{2,1,0:T(8,128)} %pos_ref.3) | copy-start | bytes 36868
  23.8 1.6 %collective-permute-start.2 = (f32[160,256]{1,0:T(8,128)S(1)}, f32[160,256]{1,0:T(8,128)S(1)}, u32[]{:S(2)}, u32[]{:S(2)}) collective-permute-start(f32[160,256]{1,0:T(8,128)S(1)} %get-tuple-element.49), channel_id=1, source_target_pairs={{0,1},{1,0},{2,3},{3,2},{4,5},{5,4},{6,7},{7,6},{8,9},{9,8},{10,11... | collective-permute-start | bytes 491528 | tf_op jit(solution)/shard_map/ppermute | solution.py:592
  25.4 5.5 %collective-permute-start.3 = (bf16[184,256]{1,0:T(8,128)(2,1)S(1)}, bf16[184,256]{1,0:T(8,128)(2,1)S(1)}, u32[]{:S(2)}, u32[]{:S(2)}) collective-permute-start(bf16[184,256]{1,0:T(8,128)(2,1)S(1)} %get-tuple-element.54.own_ref), channel_id=1, source_target_pairs={{0,2},{1,5},{2,0},{3,7},{4,6},{5,1},{6,4},{7,3},{8,10},{9,13},{10,... | collective-permute-start | bytes 282632 | tf_op jit(solution)/shard_map/ppermute | solution.py:622
  30.9 5.6 %collective-permute-start.4 = (bf16[208,256]{1,0:T(8,128)(2,1)S(1)}, bf16[208,256]{1,0:T(8,128)(2,1)S(1)}, u32[]{:S(2)}, u32[]{:S(2)}) collective-permute-start(bf16[208,256]{1,0:T(8,128)(2,1)S(1)} %mix.2.own_ref), channel_id=1, source_target_pairs={{0,4},{1,9},{2,6},{3,11},{4,0},{5,13},{6,2},{7,15},{8,12},{9,1},{1... | collective-permute-start | bytes 319496 | tf_op jit(solution)/shard_map/ppermute | solution.py:622
  36.6 5.9 %collective-permute-start.5 = (bf16[256,256]{1,0:T(8,128)(2,1)S(1)}, bf16[256,256]{1,0:T(8,128)(2,1)S(1)}, u32[]{:S(2)}, u32[]{:S(2)}) collective-permute-start(bf16[256,256]{1,0:T(8,128)(2,1)S(1)} %mix.3.refs_2_.own_ref), channel_id=1, source_target_pairs={{0,8},{1,3},{2,10},{3,1},{4,12},{5,7},{6,14},{7,5},{8,0},{9,11},{1... | collective-permute-start | bytes 393224 | tf_op jit(solution)/shard_map/ppermute | solution.py:622
  42.5 1.4 %collective-permute-start.6 = (f32[152,256]{1,0:T(8,128)S(1)}, f32[152,256]{1,0:T(8,128)S(1)}, u32[]{:S(2)}, u32[]{:S(2)}) collective-permute-start(f32[152,256]{1,0:T(8,128)S(1)} %last_mix.1.refs_1_), channel_id=1, source_target_pairs={{0,1},{1,0},{2,3},{3,2},{4,5},{5,4},{6,7},{7,6},{8,9},{9,8},{10,11... | collective-permute-start | bytes 466952 | tf_op jit(solution)/shard_map/ppermute | solution.py:592
